TPU v7x, 32 devices: a whole 2x2x4 slice. The times are simulated.
32 devices in a mesh: dp: 4 (over z), row: 2 (over x), col: 4 (over y, core).
Axes of the slice: x: 2, y: 2, z: 4, core: 2. Of those that a mesh axis runs over, the one named last changes fastest.
Arguments:
- hidden: bfloat16 [4096, 2560], P(('dp', 'col'), 'row'), may hold values from -6 to 6
- cotangent: bfloat16 [4096, 2560], P(('dp', 'col'), 'row'), may hold values from -6 to 6
- sequence_index: int32 [4096], P('dp'), may hold values from 0 to 7, as said below
- block_index: int32 [4096], P('dp'), may hold values from 0 to 31, never falling along the last dimension, each value on 1 to 256 neighbouring positions
- attention_gain: bfloat16 [2560], P('row'), may hold values from 0.5 to 1.5
- query_down: bfloat16 [2560, 768], P('row', 'col'), may hold values from -0.125 to 0.125
- query_gain: bfloat16 [768], replicated, may hold values from 0.5 to 1.5
- query_up: bfloat16 [768, 3840], P('row', 'col'), may hold values from -0.3125 to 0.3125
- latent_down: bfloat16 [2560, 288], P('row', 'col'), may hold values from -0.125 to 0.125
- latent_gain: bfloat16 [256], replicated, may hold values from 0.5 to 1.5
- latent_up: bfloat16 [256, 5120], P(None, 'col'), may hold values from -0.5 to 0.5
- attention_out: bfloat16 [2560, 2560], P('col', 'row'), may hold values from -3 to 3
- feedforward_gain: bfloat16 [2560], P('row'), may hold values from 0.5 to 1.5
- gate_weight: bfloat16 [2560, 6400], P('row', 'col'), may hold values from -0.125 to 0.125
- up_weight: bfloat16 [2560, 6400], P('row', 'col'), may hold values from -0.125 to 0.125
- down_weight: bfloat16 [6400, 2560], P('col', 'row'), may hold values from -0.625 to 0.625
Outputs:
- output: bfloat16 [4096, 2560], P(('dp', 'col'), 'row')
- input_gradient: bfloat16 [4096, 2560], P(('dp', 'col'), 'row')
- attention_gain_gradient: float32 [2560], P('row')
- query_down_gradient: float32 [2560, 768], P('row', 'col')
- query_gain_gradient: float32 [768], replicated
- query_up_gradient: float32 [768, 3840], P('row', 'col')
- latent_down_gradient: float32 [2560, 288], P('row', 'col')
- latent_gain_gradient: float32 [256], replicated
- latent_up_gradient: float32 [256, 5120], P(None, 'col')
- attention_out_gradient: float32 [2560, 2560], P('col', 'row')
- feedforward_gain_gradient: float32 [2560], P('row')
- gate_weight_gradient: float32 [2560, 6400], P('row', 'col')
- up_weight_gradient: float32 [2560, 6400], P('row', 'col')
- down_weight_gradient: float32 [6400, 2560], P('col', 'row')
Inputs may be any that keep to these rules, and one draw needn't show every extreme that they name: `sequence_index`: ids never fall along the tokens. The g-th aligned block of 1024 tokens holds exactly the sequences 2 g and 2 g + 1, each of 256 tokens or more. `block_index`: ids never fall along the tokens; each block holds 1 to 256 tokens, and some block holds exactly 256.
All inputs are finite; a program needn't handle non-finite values.
Results may differ from a plain program's by a relative error of at most 0.018.
Values may be sent and summed in bfloat16 or wider, within the bound.
No kernel may reach another device: no remote copies, remote signals or barrier semaphores. Data moves between devices by JAX's collectives and lax.ppermute only.
A program may use at most 256 MiB of HBM per device.

v0:
```python
import math

import jax
import jax.numpy as jnp
from jax import lax
from jax.sharding import PartitionSpec as P

D = 2560
KVR = 256
NOPE = 64
RD = 32
VD = 64


EPSILON = 1e-05
RESIDUAL_SCALE = 1.4 / math.sqrt(62.0)
MASKED = -1000000000.0


def matmul(operand, other):
    return jnp.dot(operand, other, preferred_element_type=jnp.float32)


def times_transposed(operand, other):
    return lax.dot_general(
        operand, other, (((1,), (1,)), ((), ())), preferred_element_type=jnp.float32
    )


def transposed_times(operand, other):
    return lax.dot_general(
        operand, other, (((0,), (0,)), ((), ())), preferred_element_type=jnp.float32
    )


def take_rows(values, offset, length):
    return lax.dynamic_slice_in_dim(values, offset, length, 0)


def rms_norm(values, scaling):
    return values * lax.rsqrt(jnp.mean(values * values, axis=-1, keepdims=True) + EPSILON) * scaling


def rotate(values, cosine, sine_part):
    half_width = values.shape[-1] // 2
    first_half = values[..., :half_width]
    second_half = values[..., half_width:]
    return jnp.concatenate(
        [
            first_half * cosine - second_half * sine_part,
            second_half * cosine + first_half * sine_part,
        ],
        axis=-1,
    )


def frequencies(rotary_width):
    return jnp.exp(
        jnp.arange(rotary_width // 2, dtype=jnp.float32) * (-2.0 * math.log(10000.0) / rotary_width)
    )


def gather_tokens(values):
    return lax.all_gather(values, "col", axis=0, tiled=True)


def reduce_tokens(term_of, row_count):
    return lax.psum_scatter(
        term_of(jnp.int32(0), lax.axis_size("col") * row_count),
        "col",
        scatter_dimension=0,
        tiled=True,
    )


def gather_queries(values):
    return lax.all_gather(values, "row", axis=0, tiled=True)


def reduce_queries(term_of, row_count):
    return lax.psum_scatter(
        term_of(jnp.int32(0), lax.axis_size("row") * row_count),
        "row",
        scatter_dimension=0,
        tiled=True,
    )


def feature_total(values):
    return lax.psum(values, "row")


def norm_forward(values, scaling):
    inverse = lax.rsqrt(feature_total(jnp.sum(values * values, axis=1)) / D + EPSILON)
    return (values * inverse[:, None] * scaling, inverse)


def norm_backward(upstream, values, inverse, scaling):
    scaled = values * inverse[:, None]
    weighted = upstream * scaling
    mean_inner = feature_total(jnp.sum(weighted * scaled, axis=1)) / D
    return (
        inverse[:, None] * (weighted - scaled * mean_inner[:, None]),
        jnp.sum(upstream * scaled, axis=0),
    )


def share_feedforward(gate_grad, up_grad, down_grad):
    return (
        lax.psum_scatter(gate_grad, "dp", scatter_dimension=0, tiled=True),
        lax.psum_scatter(up_grad, "dp", scatter_dimension=0, tiled=True),
        lax.psum_scatter(down_grad, "dp", scatter_dimension=0, tiled=True),
    )


def per_device(
    hidden,
    cotangent,
    sequence_index,
    block_index,
    attention_gain,
    query_down,
    query_gain,
    query_up,
    latent_down,
    latent_gain,
    latent_up,
    attention_out,
    feedforward_gain,
    gate_weight,
    up_weight,
    down_weight,
):
    row_place = lax.axis_index("row")
    col_place = lax.axis_index("col")
    residual_in = hidden.astype(jnp.float32)
    rows_col = residual_in.shape[0]
    group_rows = sequence_index.shape[0]
    rows_row = group_rows // lax.axis_size("row")
    head_count = query_up.shape[1] // (NOPE + RD)
    score_scale = (NOPE + RD) ** (-0.5)
    places = jnp.arange(group_rows, dtype=jnp.int32)
    earlier = jnp.sum((sequence_index[None, :] < sequence_index[:, None]).astype(jnp.int32), axis=1)
    angles = (places - earlier).astype(jnp.float32)[:, None] * frequencies(RD)[None, :]
    cosine = jnp.cos(angles)
    sine_part = jnp.sin(angles)
    query_start = row_place * rows_row
    query_cosine = take_rows(cosine, query_start, rows_row)[:, None]
    query_sine = take_rows(sine_part, query_start, rows_row)[:, None]
    query_sequence = take_rows(sequence_index, query_start, rows_row)
    query_blocks = take_rows(block_index, query_start, rows_row)
    gain_in = attention_gain.astype(jnp.float32)
    normed_in, inverse_in = norm_forward(residual_in, gain_in)
    tokens_in = gather_tokens(normed_in.astype(jnp.bfloat16))
    query_part, key_part = lax.psum(
        (matmul(tokens_in, query_down), matmul(tokens_in, latent_down)), "row"
    )
    query_latent, kv_latent = (
        lax.all_gather(query_part, "col", axis=1, tiled=True),
        lax.all_gather(key_part, "col", axis=1, tiled=True),
    )

    def latent_norms(query_values, key_values, query_scaling, key_scaling):
        return (
            rms_norm(query_values, query_scaling),
            rms_norm(key_values[:, :KVR], key_scaling),
            rotate(key_values[:, KVR:], cosine, sine_part),
        )

    (compressed, latent, key_rope), latent_back = jax.vjp(
        latent_norms,
        query_latent,
        kv_latent,
        query_gain.astype(jnp.float32),
        latent_gain.astype(jnp.float32),
    )
    compressed = compressed.astype(jnp.bfloat16)
    latent = latent.astype(jnp.bfloat16)
    key_rope = key_rope.astype(jnp.bfloat16)
    half_rank = query_up.shape[0]
    own_rank = lax.dynamic_slice_in_dim(compressed, row_place * half_rank, half_rank, 1)

    def query_term(offset, length):
        return matmul(take_rows(own_rank, offset, length), query_up)

    query_raw = reduce_queries(query_term, rows_row).reshape(rows_row, head_count, NOPE + RD)
    queries = jnp.concatenate(
        [query_raw[..., :NOPE], rotate(query_raw[..., NOPE:], query_cosine, query_sine)], axis=-1
    ).astype(jnp.bfloat16)
    keyval = matmul(latent, latent_up).reshape(group_rows, head_count, NOPE + VD)
    key_nope = keyval[..., :NOPE].astype(jnp.bfloat16)
    values_low = keyval[..., NOPE:].astype(jnp.bfloat16)
    block_rows = min(512, rows_row)
    blocks_count = rows_row // block_rows
    head_parts = 2
    per_part = head_count // head_parts
    item_starts = jnp.repeat(jnp.arange(blocks_count, dtype=jnp.int32) * block_rows, head_parts)
    item_heads = jnp.tile(jnp.arange(head_parts, dtype=jnp.int32) * per_part, blocks_count)

    def arrange_heads(stacked, width):
        shaped = stacked.reshape(blocks_count, head_parts, block_rows, per_part, width)
        return shaped.transpose(0, 2, 1, 3, 4).reshape(rows_row, head_count, width)

    def block_scores(offset, head_offset):
        block_queries = lax.dynamic_slice(
            queries, (offset, head_offset, 0), (block_rows, per_part, NOPE + RD)
        )
        block_keys = lax.dynamic_slice_in_dim(key_nope, head_offset, per_part, 1)
        block_values = lax.dynamic_slice_in_dim(values_low, head_offset, per_part, 1)
        block_sequence = take_rows(query_sequence, offset, block_rows)
        block_ids = take_rows(query_blocks, offset, block_rows)
        raw_dots = jnp.einsum(
            "qhd,khd->hqk",
            block_queries[..., :NOPE],
            block_keys,
            preferred_element_type=jnp.float32,
        )
        raw_dots = raw_dots + jnp.einsum(
            "qhd,kd->hqk", block_queries[..., NOPE:], key_rope, preferred_element_type=jnp.float32
        )
        allowed = (block_sequence[:, None] == sequence_index[None, :]) & (
            block_index[None, :] <= block_ids[:, None]
        )
        return (
            jnp.where(allowed[None], raw_dots * score_scale, MASKED),
            block_queries,
            block_keys,
            block_values,
        )

    def forward_block(entries):
        offset, head_offset = entries
        scores, block_queries, block_keys, block_values = block_scores(offset, head_offset)
        highest = jnp.max(scores, axis=2, keepdims=True)
        log_total = highest + jnp.log(jnp.sum(jnp.exp(scores - highest), axis=2, keepdims=True))
        probabilities = jnp.exp(scores - log_total).astype(jnp.bfloat16)
        return (
            jnp.einsum(
                "hqk,khd->qhd", probabilities, block_values, preferred_element_type=jnp.float32
            ),
            log_total[..., 0],
        )

    attended_parts, log_totals = lax.map(forward_block, (item_starts, item_heads))
    attended = (
        arrange_heads(attended_parts, VD).reshape(rows_row, head_count * VD).astype(jnp.bfloat16)
    )
    outputs_all = gather_queries(attended)

    def branch_term(offset, length):
        return matmul(take_rows(outputs_all, offset, length), attention_out)

    middle = residual_in + RESIDUAL_SCALE * reduce_tokens(branch_term, rows_col)
    gain_mid = feedforward_gain.astype(jnp.float32)
    normed_mid, inverse_mid = norm_forward(middle, gain_mid)
    tokens_mid = gather_tokens(normed_mid.astype(jnp.bfloat16))
    hidden_width = gate_weight.shape[1]

    def gate_term(offset, length):
        piece_rows = take_rows(tokens_mid, offset, length)
        return jnp.concatenate(
            [matmul(piece_rows, gate_weight), matmul(piece_rows, up_weight)], axis=1
        )

    both_parts = reduce_queries(gate_term, rows_row)
    gate_value = both_parts[:, :hidden_width]
    up_value = both_parts[:, hidden_width:]
    sigmoid_gate = jax.nn.sigmoid(gate_value)
    swish_gate = gate_value * sigmoid_gate
    activation = (swish_gate * up_value).astype(jnp.bfloat16)
    activations_all = gather_queries(activation)

    def down_term(offset, length):
        return matmul(take_rows(activations_all, offset, length), down_weight)

    output = (middle + RESIDUAL_SCALE * reduce_tokens(down_term, rows_col)).astype(jnp.bfloat16)
    incoming = cotangent.astype(jnp.float32)
    grad_down = gather_tokens((RESIDUAL_SCALE * incoming).astype(jnp.bfloat16))
    down_grad = transposed_times(activations_all, grad_down)

    def act_term(offset, length):
        return times_transposed(take_rows(grad_down, offset, length), down_weight)

    grad_act = reduce_queries(act_term, rows_row)
    grad_gate = grad_act * up_value * sigmoid_gate * (1.0 + gate_value * (1.0 - sigmoid_gate))
    grad_up = grad_act * swish_gate
    grad_both = gather_queries(jnp.concatenate([grad_gate, grad_up], axis=1).astype(jnp.bfloat16))
    gate_grad = transposed_times(tokens_mid, grad_both[:, :hidden_width])
    up_grad = transposed_times(tokens_mid, grad_both[:, hidden_width:])

    def mid_term(offset, length):
        piece_rows = take_rows(grad_both, offset, length)
        return times_transposed(piece_rows[:, :hidden_width], gate_weight) + times_transposed(
            piece_rows[:, hidden_width:], up_weight
        )

    grad_mid, gain_mid_grad = norm_backward(
        reduce_tokens(mid_term, rows_col), middle, inverse_mid, gain_mid
    )
    grad_middle = incoming + grad_mid
    grad_branch = gather_tokens((RESIDUAL_SCALE * grad_middle).astype(jnp.bfloat16))
    out_grad = transposed_times(outputs_all, grad_branch)

    def attended_term(offset, length):
        return times_transposed(take_rows(grad_branch, offset, length), attention_out)

    grad_attended = (
        reduce_queries(attended_term, rows_row)
        .astype(jnp.bfloat16)
        .reshape(rows_row, head_count, VD)
    )

    def backward_block(running, entries):
        offset, head_offset, log_total = entries
        scores, block_queries, block_keys, block_values = block_scores(offset, head_offset)
        grad_block = lax.dynamic_slice(
            grad_attended, (offset, head_offset, 0), (block_rows, per_part, VD)
        )
        probabilities = jnp.exp(scores - log_total[..., None])
        grad_probs = jnp.einsum(
            "qhd,khd->hqk", grad_block, block_values, preferred_element_type=jnp.float32
        )
        row_inner = jnp.sum(probabilities * grad_probs, axis=2, keepdims=True)
        grad_dots = (probabilities * (grad_probs - row_inner) * score_scale).astype(jnp.bfloat16)
        query_grad = jnp.concatenate(
            [
                jnp.einsum(
                    "hqk,khd->qhd", grad_dots, block_keys, preferred_element_type=jnp.float32
                ),
                jnp.einsum("hqk,kd->qhd", grad_dots, key_rope, preferred_element_type=jnp.float32),
            ],
            axis=-1,
        )
        key_grad = jnp.concatenate(
            [
                jnp.einsum(
                    "hqk,qhd->khd",
                    grad_dots,
                    block_queries[..., :NOPE],
                    preferred_element_type=jnp.float32,
                ),
                jnp.einsum(
                    "hqk,qhd->khd",
                    probabilities.astype(jnp.bfloat16),
                    grad_block,
                    preferred_element_type=jnp.float32,
                ),
            ],
            axis=-1,
        )
        rope_grad = jnp.einsum(
            "hqk,qhd->kd", grad_dots, block_queries[..., NOPE:], preferred_element_type=jnp.float32
        )
        keys_total, rope_total = running
        current = lax.dynamic_slice_in_dim(keys_total, head_offset, per_part, 1)
        keys_total = lax.dynamic_update_slice_in_dim(keys_total, current + key_grad, head_offset, 1)
        return ((keys_total, rope_total + rope_grad), query_grad)

    initial = (
        jnp.zeros((group_rows, head_count, NOPE + VD), jnp.float32),
        jnp.zeros((group_rows, RD), jnp.float32),
    )
    (keys_total, rope_total), query_grads = lax.scan(
        backward_block, initial, (item_starts, item_heads, log_totals)
    )
    query_grads = arrange_heads(query_grads, NOPE + RD)
    query_raw_grad = (
        jnp.concatenate(
            [query_grads[..., :NOPE], rotate(query_grads[..., NOPE:], query_cosine, -query_sine)],
            axis=-1,
        )
        .astype(jnp.bfloat16)
        .reshape(rows_row, head_count * (NOPE + RD))
    )
    keyval_grad, rope_rows = lax.psum(
        (keys_total.reshape(group_rows, head_count * (NOPE + VD)), rope_total), "row"
    )
    keyval_grad = keyval_grad.astype(jnp.bfloat16)
    latent_up_grad = transposed_times(latent, keyval_grad)
    query_all_grad = gather_queries(query_raw_grad)
    query_up_grad = transposed_times(own_rank, query_all_grad)
    compressed_half, latent_grad, rope_grad_total = lax.psum(
        (
            times_transposed(query_all_grad, query_up),
            times_transposed(keyval_grad, latent_up),
            rope_rows,
        ),
        "col",
    )
    compressed_grad = lax.all_gather(compressed_half, "row", axis=1, tiled=True)
    query_latent_grad, kv_latent_grad, query_gain_grad, latent_gain_grad = latent_back(
        (compressed_grad, latent_grad, rope_grad_total)
    )
    query_tile = query_down.shape[1]
    key_tile = latent_down.shape[1]
    query_latent_low = lax.dynamic_slice_in_dim(
        query_latent_grad, col_place * query_tile, query_tile, 1
    ).astype(jnp.bfloat16)
    key_latent_low = lax.dynamic_slice_in_dim(
        kv_latent_grad, col_place * key_tile, key_tile, 1
    ).astype(jnp.bfloat16)
    query_down_grad = transposed_times(tokens_in, query_latent_low)
    latent_down_grad = transposed_times(tokens_in, key_latent_low)

    def normed_term(offset, length):
        return times_transposed(
            take_rows(query_latent_low, offset, length), query_down
        ) + times_transposed(take_rows(key_latent_low, offset, length), latent_down)

    grad_in, gain_in_grad = norm_backward(
        reduce_tokens(normed_term, rows_col), residual_in, inverse_in, gain_in
    )
    input_gradient = (grad_middle + grad_in).astype(jnp.bfloat16)
    gain_totals = lax.psum((gain_in_grad, gain_mid_grad), ("dp", "col"))
    attention_parts = (
        lax.psum_scatter(query_down_grad, "dp", scatter_dimension=0, tiled=True),
        lax.psum_scatter(query_gain_grad, "dp", scatter_dimension=0, tiled=True),
        lax.psum_scatter(query_up_grad, "dp", scatter_dimension=0, tiled=True),
        lax.psum_scatter(latent_down_grad, "dp", scatter_dimension=0, tiled=True),
        lax.psum_scatter(latent_gain_grad, "dp", scatter_dimension=0, tiled=True),
        lax.psum_scatter(latent_up_grad, "dp", scatter_dimension=0, tiled=True),
        lax.psum_scatter(out_grad, "dp", scatter_dimension=0, tiled=True),
    )
    feedforward_parts = share_feedforward(gate_grad, up_grad, down_grad)
    copies = (
        lax.all_gather(attention_parts[0], "dp", axis=0, tiled=True),
        lax.all_gather(attention_parts[1], "dp", axis=0, tiled=True),
        lax.all_gather(attention_parts[2], "dp", axis=0, tiled=True),
        lax.all_gather(attention_parts[3], "dp", axis=0, tiled=True),
        lax.all_gather(attention_parts[4], "dp", axis=0, tiled=True),
        lax.all_gather(attention_parts[5], "dp", axis=0, tiled=True),
        lax.all_gather(attention_parts[6], "dp", axis=0, tiled=True),
        lax.all_gather(feedforward_parts[0], "dp", axis=0, tiled=True),
        lax.all_gather(feedforward_parts[1], "dp", axis=0, tiled=True),
        lax.all_gather(feedforward_parts[2], "dp", axis=0, tiled=True),
    )
    return (
        output,
        input_gradient,
        gain_totals[0],
        copies[0],
        copies[1],
        copies[2],
        copies[3],
        copies[4],
        copies[5],
        copies[6],
        gain_totals[1],
        copies[7],
        copies[8],
        copies[9],
    )


def solution(mesh):
    return jax.shard_map(
        per_device,
        mesh=mesh,
        in_specs=(
            P(("dp", "col"), "row"),
            P(("dp", "col"), "row"),
            P("dp"),
            P("dp"),
            P("row"),
            P("row", "col"),
            P(),
            P("row", "col"),
            P("row", "col"),
            P(),
            P(None, "col"),
            P("col", "row"),
            P("row"),
            P("row", "col"),
            P("row", "col"),
            P("col", "row"),
        ),
        out_specs=(
            P(("dp", "col"), "row"),
            P(("dp", "col"), "row"),
            P("row"),
            P("row", "col"),
            P(),
            P("row", "col"),
            P("row", "col"),
            P(),
            P(None, "col"),
            P("col", "row"),
            P("row"),
            P("row", "col"),
            P("row", "col"),
            P("col", "row"),
        ),
        check_vma=False,
    )
```

profile of v0, /device:TPU:0, one launch (start us, length us, event | category | flops | bytes accessed | tf_op | source)
XLA Modules:
  0.0 2728.7 jit_solution(4413344150325788755)
XLA Ops:
  18.1 27.5 %all-gather.20.cloned.1.call-done = bf16[1024,1280]{1,0:T(8,128)(2,1)} async-done(((bf16[256,1280]{1,0:T(8,128)(2,1)}), bf16[1024,1280]{1,0:T(8,128)(2,1)}) %all-gather.20.cloned.1.call-update) | async-done | bytes 2621456 | tf_op jit(solution)/shard_map/all_gather | solution.py:64
  51.0 41.0 %all-reduce.22.cloned.1.call-done = (f32[1024,72]{0,1:T(8,128)}, f32[1024,192]{0,1:T(8,128)}) async-done(((f32[1024,72]{0,1:T(8,128)}, f32[1024,192]{0,1:T(8,128)}), (f32[1024,72]{0,1:T(8,128)}, f32[1024,192]{0,1:T(8,128)})) %all-reduce.22.cloned.1.call-update) | async-done | bytes 1081360 | tf_op jit(solution)/shard_map/psum | solution.py:155
  92.8 29.4 %all-gather.24.cloned.1.call-done = f32[1024,768]{0,1:T(8,128)} async-done(((f32[1024,192]{0,1:T(8,128)}), f32[1024,768]{0,1:T(8,128)}) %all-gather.24.cloned.1.call-update) | async-done | bytes 3145744 | tf_op jit(solution)/shard_map/all_gather | solution.py:159
  132.1 9.0 all-gather.22.cloned.1.call-done
  156.0 39.8 %reduce-scatter.21.cloned.1.call-done = f32[512,960]{0,1:T(8,128)} async-done(((f32[1024,960]{0,1:T(8,128)}), f32[512,960]{0,1:T(8,128)}) %reduce-scatter.21.cloned.1.call-update) | async-done | bytes 1966096 | tf_op jit(solution)/shard_map/reduce_scatter | solution.py:81
  199.4 44.2 %while.27 = (s32[]{:T(128)}, bf16[2,512,5,64]{1,3,2,0:T(8,128)(2,1)S(1)}, f32[2,5,512]{2,1,0:T(8,128)S(1)}, s32[2]{0:T(128)S(1)}, bf16[1024,10,64]{0,2,1:T(8,128...) while((s32[]{:T(128)}, ...), condition=%wide.region_11.12_spmd, body=%wide.region_8.11_spmd.sunk | while | flops 861402624 | bytes 56126700 | solution.py:244
  208.9 7.0 fusion.229
  231.0 7.0 fusion.229
  244.9 24.0 all-gather.26.cloned.1.call-done
  277.0 49.4 %reduce-scatter.23.cloned.1.call-done = f32[256,1280]{1,0:T(8,128)} async-done(((f32[1024,1280]{1,0:T(8,128)}), f32[256,1280]{1,0:T(8,128)}) %reduce-scatter.23.cloned.1.call-update) | async-done | bytes 1310736 | tf_op jit(solution)/shard_map/reduce_scatter | solution.py:68
  334.2 19.9 all-gather.32.cloned.1.call-done
  354.1 10.3 fusion.144
  365.1 16.7 all-gather.28.cloned.1.call-done
  381.9 7.2 fusion.142
  393.5 7.9 pad_maximum_fusion
  401.5 63.1 %reduce-scatter.29.cloned.1.call-done = f32[512,1600]{0,1:T(8,128)} async-done(((f32[1024,1600]{0,1:T(8,128)}), f32[512,1600]{0,1:T(8,128)}) %reduce-scatter.29.cloned.1.call-update) | async-done | bytes 3276816 | tf_op jit(solution)/shard_map/reduce_scatter | solution.py:81
  464.5 152.6 %reduce-scatter.25.cloned.1.call-done = f32[512,3200]{0,1:T(8,128)} async-done(((f32[1024,3200]{0,1:T(8,128)}), f32[512,3200]{0,1:T(8,128)}) %reduce-scatter.25.cloned.1.call-update) | async-done | bytes 6553616 | tf_op jit(solution)/shard_map/reduce_scatter | solution.py:81
  625.1 83.3 %all-gather.34.cloned.1.call-done = bf16[1024,3200]{0,1:T(8,128)(2,1)} async-done(((bf16[512,3200]{0,1:T(8,128)(2,1)}), bf16[1024,3200]{0,1:T(8,128)(2,1)}) %all-gather.34.cloned.1.call-update) | async-done | bytes 6553616 | tf_op jit(solution)/shard_map/all_gather | solution.py:77
  708.4 8.5 fusion.91
  716.9 7.1 convolution_add_fusion.1
  724.1 51.5 %reduce-scatter.31.cloned.1.call-done = f32[256,1280]{1,0:T(8,128)} async-done(((f32[1024,1280]{1,0:T(8,128)}), f32[256,1280]{1,0:T(8,128)}) %reduce-scatter.31.cloned.1.call-update) | async-done | bytes 1310736 | tf_op jit(solution)/shard_map/reduce_scatter | solution.py:68
  785.7 25.7 all-gather.36.cloned.1.call-done
  816.9 37.7 %reduce-scatter.33.cloned.1.call-done = f32[512,640]{1,0:T(8,128)} async-done(((f32[1024,640]{1,0:T(8,128)}), f32[512,640]{1,0:T(8,128)}) %reduce-scatter.33.cloned.1.call-update) | async-done | bytes 1310736 | tf_op jit(solution)/shard_map/reduce_scatter | solution.py:81
  859.2 190.1 %while.28 = (s32[]{:T(128)}, f32[1024,10,128]{0,2,1:T(8,128)}, f32[1024,32]{0,1:T(8,128)}, f32[2,512,5,96]{1,3,2,0:T(8,128)}, s32[2]{0:T(128)S(1)}, /*index=5*/b...) while((s32[]{:T(128)}, f32[1024,10,128]{0,2,1:T(8,128)}, ...), condition=%wide.region_24.25_spmd.clone, body=%wide.region_22.24_spmd.clone.sunk | while | flops 2249783296 | bytes 278049248 | solution.py:363
  871.6 8.7 fusion.248
  880.3 16.1 fusion.253
  896.4 14.4 fusion.254
  910.8 16.8 fusion.255
  927.6 16.6 fusion.251
  957.4 6.5 fusion.250
  966.4 8.7 fusion.248
  975.0 16.2 fusion.253
  991.2 14.4 fusion.254
  1005.6 16.8 fusion.255
  1022.4 16.6 fusion.251
  1054.2 182.6 %all-reduce.23 = bf16[1024,1280]{0,1:T(8,128)(2,1)} all-reduce(f32[1024,1280]{0,1:T(8,128)} %bitcast.150), channel_id=1, replica_groups=mesh['dp'=4,'row'=2,'col'=4] {'row'}, use_global_device_ids=true, to_apply=%region_29.30 | all-reduce | flops 1310720 | bytes 7864320 | tf_op jit(solution)/shard_map/psum | solution.py:375
  1249.2 11.0 fusion.150
  1271.8 35.8 %all-reduce.20.cloned.1.call-done = (f32[1024,384]{0,1:T(8,128)}, f32[1024,32]{0,1:T(8,128)}, f32[1024,256]{0,1:T(8,128)}) async-done(((f32[1024,384]{0,1:T(8,128)}, f32[1024,32]{0,1:T(8,128)}, f32[1024,256]{0,1:T(8,128)}), (f32[1024,384]{0,1:T(8,128)}, f32[1024,32]{0,1:T(8,128)}, f32[1024,256]{0,1:T(8,128)})) %all-reduce.20.cloned.1.call-update) | async-done | bytes 2752528 | tf_op jit(solution)/shard_map/psum | solution.py:382
  1307.9 11.1 fusion.86
  1319.0 11.1 fusion.89
  1335.2 6.5 reduce-scatter.39.cloned.1.call-done
  1341.8 143.2 %reduce-scatter.47.cloned.1.call-done = f32[400,1280]{1,0:T(8,128)} async-done(((f32[1600,1280]{1,0:T(8,128)}), f32[400,1280]{1,0:T(8,128)}) %reduce-scatter.47.cloned.1.call-update) | async-done | bytes 2048016 | tf_op jit(solution)/shard_map/reduce_scatter | solution.py:112
  1485.1 65.8 %reduce-scatter.41.cloned.1.call-done = f32[160,1280]{1,0:T(8,128)} async-done(((f32[640,1280]{1,0:T(8,128)}), f32[160,1280]{1,0:T(8,128)}) %reduce-scatter.41.cloned.1.call-update) | async-done | bytes 819216 | tf_op jit(solution)/shard_map/reduce_scatter | solution.py:422
  1550.9 37.7 %reduce-scatter.37.cloned.1.call-done = f32[96,960]{1,0:T(8,128)} async-done(((f32[384,960]{1,0:T(8,128)}), f32[96,960]{1,0:T(8,128)}) %reduce-scatter.37.cloned.1.call-update) | async-done | bytes 368656 | tf_op jit(solution)/shard_map/reduce_scatter | solution.py:418
  1589.1 44.8 %all-gather.40.cloned.1.call-done = f32[1024,768]{0,1:T(8,128)} async-done(((f32[1024,384]{0,1:T(8,128)}), f32[1024,768]{0,1:T(8,128)}) %all-gather.40.cloned.1.call-update) | async-done | bytes 3145744 | tf_op jit(solution)/shard_map/all_gather | solution.py:390
  1641.4 141.5 %reduce-scatter.45.cloned.1.call-done = f32[320,1600]{1,0:T(8,128)} async-done(((f32[1280,1600]{1,0:T(8,128)}), f32[320,1600]{1,0:T(8,128)}) %reduce-scatter.45.cloned.1.call-update) | async-done | bytes 2048016 | tf_op jit(solution)/shard_map/reduce_scatter | solution.py:111
  1782.9 149.6 %reduce-scatter.43.cloned.1.call-done = f32[320,1600]{1,0:T(8,128)} async-done(((f32[1280,1600]{1,0:T(8,128)}), f32[320,1600]{1,0:T(8,128)}) %reduce-scatter.43.cloned.1.call-update) | async-done | bytes 2048016 | tf_op jit(solution)/shard_map/reduce_scatter | solution.py:110
  1936.9 10.5 fusion.143
  1951.3 6.9 reduce-scatter.51.cloned.1.call-done
  1959.2 17.6 all-gather.1
  1978.0 14.9 all-gather.44.cloned.1.call-done
  1992.9 147.5 %all-gather.52.cloned.1.call-done = f32[1600,1280]{1,0:T(8,128)} async-done(((f32[400,1280]{1,0:T(8,128)}), f32[1600,1280]{1,0:T(8,128)}) %all-gather.52.cloned.1.call-update) | async-done | bytes 8192016 | tf_op jit(solution)/shard_map/all_gather | solution.py:435
  2140.4 65.3 %all-gather.46.cloned.1.call-done = f32[640,1280]{1,0:T(8,128)} async-done(((f32[160,1280]{1,0:T(8,128)}), f32[640,1280]{1,0:T(8,128)}) %all-gather.46.cloned.1.call-update) | async-done | bytes 3276816 | tf_op jit(solution)/shard_map/all_gather | solution.py:432
  2205.8 9.2 all-reduce.11
  2215.3 11.0 all-reduce.10
  2226.3 17.4 all-gather.42.cloned.1.call-done
  2246.6 30.0 %reduce-scatter.49.cloned.1.call-done = f32[320,192]{1,0:T(8,128)} async-done(((f32[1280,192]{1,0:T(8,128)}), f32[320,192]{1,0:T(8,128)}) %reduce-scatter.49.cloned.1.call-update) | async-done | bytes 245776
  2277.7 34.6 %all-gather = f32[4,320,192]{1,2,0:T(8,128)S(1)} all-gather(f32[1,320,192]{1,2,0:T(8,128)S(1)} %bitcast.156), channel_id=1, replica_groups=mesh['dp'=4,'row'=2,'col'=4] {'dp'}, dimensions={0}, use_global_device_ids=true | all-gather | bytes 1228800 | tf_op jit(solution)/shard_map/all_gather | solution.py:426
  2314.8 122.9 %all-gather.50.cloned.1.call-done = f32[1280,1600]{1,0:T(8,128)} async-done(((f32[320,1600]{1,0:T(8,128)}), f32[1280,1600]{1,0:T(8,128)}) %all-gather.50.cloned.1.call-update) | async-done | bytes 8192016 | tf_op jit(solution)/shard_map/all_gather | solution.py:434
  2437.7 9.9 copy.64
  2447.6 143.3 %all-gather.48.cloned.1.call-done = f32[1280,1600]{1,0:T(8,128)} async-done(((f32[320,1600]{1,0:T(8,128)}), f32[1280,1600]{1,0:T(8,128)}) %all-gather.48.cloned.1.call-update) | async-done | bytes 8192016 | tf_op jit(solution)/shard_map/all_gather | solution.py:433
  2590.9 9.9 copy.63
  2600.8 42.9 %reduce-scatter.35.cloned.1.call-done = f32[256,1280]{1,0:T(8,128)} async-done(((f32[1024,1280]{1,0:T(8,128)}), f32[256,1280]{1,0:T(8,128)}) %reduce-scatter.35.cloned.1.call-update) | async-done | bytes 1310736 | tf_op jit(solution)/shard_map/reduce_scatter | solution.py:68
  2650.4 59.9 %all-reduce.8 = (f32[1280]{0:T(1024)}, f32[1280]{0:T(1024)}) all-reduce(f32[1280]{0:T(1024)S(1)} %get-tuple-element.284, f32[1280]{0:T(1024)S(1)} %copy-done.49), channel_id=1, replica_groups=mesh['dp'=4,'row'=2,'col'=4] {'dp','col'}, use_global_device_ids=true, to_apply=%region_36.37 | all-reduce | flops 2560 | bytes 20480 | tf_op jit(solution)/shard_map/psum | solution.py:414
  (365 shorter events, 230.6 us)
Async XLA Ops:
  7.2 261.7 %copy-start = (bf16[640,1280]{1,0:T(8,128)(2,1)S(1)}, bf16[640,1280]{1,0:T(8,128)(2,1)}, u32[]{:S(2)}) copy-start(bf16[640,1280]{1,0:T(8,128)(2,1)} %param.31) | copy-start | bytes 4915204
  7.2 38.3 %copy-start.24 = (bf16[1280,72]{0,1:T(8,128)(2,1)S(1)}, bf16[1280,72]{0,1:T(8,128)(2,1)}, u32[]{:S(2)}) copy-start(bf16[1280,72]{0,1:T(8,128)(2,1)} %param.28) | copy-start | bytes 552964
  7.2 38.3 %all-gather.20.cloned.1.call-start = ((), (), s32[]{:S(2)}) async-start(), calls=%async_computation.16 | async-start | bytes 3276800 | tf_op jit(solution)/shard_map/all_gather | solution.py:64
  18.0 31.0 %copy-start.18 = (bf16[1280,192]{0,1:T(8,128)(2,1)S(1)}, bf16[1280,192]{0,1:T(8,128)(2,1)}, u32[]{:S(2)}) copy-start(bf16[1280,192]{0,1:T(8,128)(2,1)} %param.25) | copy-start | bytes 1474564
  18.0 74.0 %all-reduce.22.cloned.1.call-start = ((), (), s32[]{:S(2)}) async-start(), calls=%async_computation.51 | async-start | bytes 2162688 | tf_op jit(solution)/shard_map/psum | solution.py:155
  49.1 43.6 %copy-start.60 = (bf16[768]{0:T(1024)(128)(2,1)S(1)}, bf16[768]{0:T(1024)(128)(2,1)}, u32[]{:S(2)}) copy-start(bf16[768]{0:T(1024)(128)(2,1)} %param.26) | copy-start | bytes 4612
  51.0 71.2 %all-gather.24.cloned.1.call-start = ((), (), s32[]{:S(2)}) async-start(), calls=%async_computation.18 | async-start | bytes 3932160 | tf_op jit(solution)/shard_map/all_gather | solution.py:159
  92.1 49.1 %all-gather.22.cloned.1.call-start = ((), (), s32[]{:S(2)}) async-start(), calls=%async_computation.17 | async-start | bytes 1474560 | tf_op jit(solution)/shard_map/all_gather | solution.py:160
  92.6 103.2 %reduce-scatter.21.cloned.1.call-start = ((), (), s32[]{:S(2)}) async-start(), calls=%async_computation.19 | async-start | bytes 5898240 | tf_op jit(solution)/shard_map/reduce_scatter | solution.py:81
  92.8 33.0 %copy-start.58 = (f32[384]{0:T(512)}, f32[384]{0:T(512)S(1)}, u32[]{:S(2)}) copy-start(f32[384]{0:T(512)S(1)} %dynamic-slice.10) | copy-start | bytes 4612
  130.6 138.3 %all-gather.26.cloned.1.call-start = ((), (), s32[]{:S(2)}) async-start(), calls=%async_computation.20 | async-start | bytes 1966080 | tf_op jit(solution)/shard_map/all_gather | solution.py:77
  152.5 44.7 %copy-start.31 = (f32[512,16]{0,1:T(8,128)}, f32[512,16]{0,1:T(8,128)S(1)}, u32[]{:S(2)}) copy-start(f32[512,16]{0,1:T(8,128)S(1)} %get-tuple-element.381) | copy-start | bytes 98308
  244.5 81.9 %reduce-scatter.23.cloned.1.call-start = ((), (), s32[]{:S(2)}) async-start(), calls=%async_computation.21 | async-start | bytes 6553600 | tf_op jit(solution)/shard_map/reduce_scatter | solution.py:68
  274.9 79.3 %all-gather.32.cloned.1.call-start = ((), (), s32[]{:S(2)}) async-start(), calls=%async_computation.26 | async-start | bytes 3276800 | tf_op jit(solution)/shard_map/all_gather | solution.py:64
  276.9 105.0 %all-gather.28.cloned.1.call-start = ((), (), s32[]{:S(2)}) async-start(), calls=%async_computation.22 | async-start | bytes 3276800 | tf_op jit(solution)/shard_map/all_gather | solution.py:64
  276.9 505.9 %copy-start.33 = (f32[1280]{0:T(1024)}, f32[1280]{0:T(1024)S(1)}, u32[]{:S(2)}) copy-start(f32[1280]{0:T(1024)S(1)} %convert_element_type.111) | copy-start | bytes 15364
  328.2 454.7 %copy-start.7 = (f32[256,1280]{1,0:T(8,128)}, f32[256,1280]{1,0:T(8,128)S(1)}, u32[]{:S(2)}) copy-start(f32[256,1280]{1,0:T(8,128)S(1)} %get-tuple-element.358) | copy-start | bytes 3932164
  333.1 449.7 %copy-start.50 = (f32[256]{0:T(256)}, f32[256]{0:T(256)S(1)}, u32[]{:S(2)}) copy-start(f32[256]{0:T(256)S(1)} %add_rsqrt_fusion) | copy-start | bytes 3076
  334.2 130.4 %reduce-scatter.29.cloned.1.call-start = ((), (), s32[]{:S(2)}) async-start(), calls=%async_computation.27 | async-start | bytes 9830400 | tf_op jit(solution)/shard_map/reduce_scatter | solution.py:81
  364.5 252.6 %reduce-scatter.25.cloned.1.call-start = ((), (), s32[]{:S(2)}) async-start(), calls=%async_computation.23 | async-start | bytes 19660800 | tf_op jit(solution)/shard_map/reduce_scatter | solution.py:81
  401.4 307.0 %all-gather.34.cloned.1.call-start = ((), (), s32[]{:S(2)}) async-start(), calls=%async_computation.28 | async-start | bytes 9830400 | tf_op jit(solution)/shard_map/all_gather | solution.py:77
  624.9 150.7 %reduce-scatter.31.cloned.1.call-start = ((), (), s32[]{:S(2)}) async-start(), calls=%async_computation.29 | async-start | bytes 6553600 | tf_op jit(solution)/shard_map/reduce_scatter | solution.py:68
  724.0 87.3 %all-gather.36.cloned.1.call-start = ((), (), s32[]{:S(2)}) async-start(), calls=%async_computation.30 | async-start | bytes 3276800 | tf_op jit(solution)/shard_map/all_gather | solution.py:64
  782.8 33.9 %copy-start.56 = (f32[256]{0:T(256)}, f32[256]{0:T(256)S(1)}, u32[]{:S(2)}) copy-start(f32[256]{0:T(256)S(1)} %broadcast_multiply_fusion.3) | copy-start | bytes 3076
  785.6 68.9 %reduce-scatter.33.cloned.1.call-start = ((), (), s32[]{:S(2)}) async-start(), calls=%async_computation.31 | async-start | bytes 3932160 | tf_op jit(solution)/shard_map/reduce_scatter | solution.py:81
  816.8 423.6 %all-gather.38.cloned.1.call-start = ((), (), s32[]{:S(2)}) async-start(), calls=%async_computation.32 | async-start | bytes 2949120 | tf_op jit(solution)/shard_map/all_gather | solution.py:77
  859.2 191.5 %copy-start.32 = (f32[512,16]{0,1:T(8,128)S(1)}, f32[512,16]{0,1:T(8,128)}, u32[]{:S(2)}) copy-start(f32[512,16]{0,1:T(8,128)} %copy-done.31) | copy-start | bytes 98308
  859.2 191.5 %copy-start.37 = (f32[512,16]{0,1:T(8,128)S(1)}, f32[512,16]{0,1:T(8,128)}, u32[]{:S(2)}) copy-start(f32[512,16]{0,1:T(8,128)} %get-tuple-element.355) | copy-start | bytes 98308
  927.6 21.9 slice-start
  1022.4 21.9 slice-start
  1053.0 191.2 %all-reduce.18.cloned.1.call-start = ((), (), s32[]{:S(2)}) async-start(), calls=%async_computation.34 | async-start | bytes 262144 | tf_op jit(solution)/shard_map/psum | solution.py:375
  1053.5 195.7 %all-gather.30.cloned.1.call-start = ((), (), s32[]{:S(2)}) async-start(), calls=%async_computation.24 | async-start | bytes 4915200 | tf_op jit(solution)/shard_map/all_gather | solution.py:77
  1054.1 253.5 %all-reduce.20.cloned.1.call-start = ((), (), s32[]{:S(2)}) async-start(), calls=%async_computation.50 | async-start | bytes 5505024 | tf_op jit(solution)/shard_map/psum | solution.py:382
  1054.2 182.7 %copy-start.28 = (bf16[256,1280]{1,0:T(8,128)(2,1)S(1)}, bf16[256,1280]{1,0:T(8,128)(2,1)}, u32[]{:S(2)}) copy-start(bf16[256,1280]{1,0:T(8,128)(2,1)} %param.30) | copy-start | bytes 1966084
  1244.2 97.5 %reduce-scatter.39.cloned.1.call-start = ((), (), s32[]{:S(2)}) async-start(), calls=%async_computation.38 | async-start | bytes 1638400 | tf_op jit(solution)/shard_map/reduce_scatter | solution.py:421
  1249.2 235.8 %reduce-scatter.47.cloned.1.call-start = ((), (), s32[]{:S(2)}) async-start(), calls=%async_computation.46 | async-start | bytes 10240000 | tf_op jit(solution)/shard_map/reduce_scatter | solution.py:112
  1260.3 290.6 %reduce-scatter.41.cloned.1.call-start = ((), (), s32[]{:S(2)}) async-start(), calls=%async_computation.40 | async-start | bytes 4096000 | tf_op jit(solution)/shard_map/reduce_scatter | solution.py:422
  1266.9 321.7 %reduce-scatter.37.cloned.1.call-start = ((), (), s32[]{:S(2)}) async-start(), calls=%async_computation.36 | async-start | bytes 1966080 | tf_op jit(solution)/shard_map/reduce_scatter | solution.py:418
  1271.7 362.2 %all-gather.40.cloned.1.call-start = ((), (), s32[]{:S(2)}) async-start(), calls=%async_computation.33 | async-start | bytes 4718592 | tf_op jit(solution)/shard_map/all_gather | solution.py:390
  1307.6 475.3 %reduce-scatter.45.cloned.1.call-start = ((), (), s32[]{:S(2)}) async-start(), calls=%async_computation.44 | async-start | bytes 10649600 | tf_op jit(solution)/shard_map/reduce_scatter | solution.py:111
  1319.0 613.6 %reduce-scatter.43.cloned.1.call-start = ((), (), s32[]{:S(2)}) async-start(), calls=%async_computation.42 | async-start | bytes 10649600 | tf_op jit(solution)/shard_map/reduce_scatter | solution.py:110
  1330.1 628.1 %reduce-scatter.51.cloned.1.call-start = ((), (), s32[]{:S(2)}) async-start(), calls=%async_computation.49 | async-start | bytes 819200
  1335.1 254.0 %copy-start.61 = (bf16[768]{0:T(1024)(128)(2,1)S(1)}, bf16[768]{0:T(1024)(128)(2,1)}, u32[]{:S(2)}) copy-start(bf16[768]{0:T(1024)(128)(2,1)} %param.26) | copy-start | bytes 4612
  1335.1 298.8 %copy-start.42 = (f32[1024]{0:T(1024)S(1)}, f32[1024]{0:T(1024)}, u32[]{:S(2)}) copy-start(f32[1024]{0:T(1024)} %copy-done.41) | copy-start | bytes 12292
  1335.1 657.8 %all-gather.44.cloned.1.call-start = ((), (), s32[]{:S(2)}) async-start(), calls=%async_computation.39 | async-start | bytes 1638400 | tf_op jit(solution)/shard_map/all_gather | solution.py:431
  1341.7 798.7 %all-gather.52.cloned.1.call-start = ((), (), s32[]{:S(2)}) async-start(), calls=%async_computation.47 | async-start | bytes 10240000 | tf_op jit(solution)/shard_map/all_gather | solution.py:435
  1485.0 720.8 %all-gather.46.cloned.1.call-start = ((), (), s32[]{:S(2)}) async-start(), calls=%async_computation.41 | async-start | bytes 4096000 | tf_op jit(solution)/shard_map/all_gather | solution.py:432
  1550.9 692.8 %all-gather.42.cloned.1.call-start = ((), (), s32[]{:S(2)}) async-start(), calls=%async_computation.37 | async-start | bytes 1966080 | tf_op jit(solution)/shard_map/all_gather | solution.py:428
  1588.6 688.0 %reduce-scatter.49.cloned.1.call-start = ((), (), s32[]{:S(2)}) async-start(), calls=%async_computation.48 | async-start | bytes 1638400
  1589.1 48.6 %copy-start.44 = (f32[1024]{0:T(1024)S(1)}, f32[1024]{0:T(1024)}, u32[]{:S(2)}) copy-start(f32[1024]{0:T(1024)} %copy-done.43) | copy-start | bytes 12292
  1641.3 291.3 %copy-start.19 = (bf16[1280,192]{0,1:T(8,128)(2,1)S(1)}, bf16[1280,192]{0,1:T(8,128)(2,1)}, u32[]{:S(2)}) copy-start(bf16[1280,192]{0,1:T(8,128)(2,1)} %param.25) | copy-start | bytes 1474564
  1641.3 796.4 %all-gather.50.cloned.1.call-start = ((), (), s32[]{:S(2)}) async-start(), calls=%async_computation.45 | async-start | bytes 10649600 | tf_op jit(solution)/shard_map/all_gather | solution.py:434
  1782.9 808.0 %all-gather.48.cloned.1.call-start = ((), (), s32[]{:S(2)}) async-start(), calls=%async_computation.43 | async-start | bytes 10649600 | tf_op jit(solution)/shard_map/all_gather | solution.py:433
  1932.6 711.0 %reduce-scatter.35.cloned.1.call-start = ((), (), s32[]{:S(2)}) async-start(), calls=%async_computation.35 | async-start | bytes 6553600 | tf_op jit(solution)/shard_map/reduce_scatter | solution.py:68
  1936.8 773.4 %reduce-scatter.27.cloned.1.call-start = ((), (), s32[]{:S(2)}) async-start(), calls=%async_computation.25 | async-start | bytes 6553600 | tf_op jit(solution)/shard_map/reduce_scatter | solution.py:68
  2447.6 196.1 %copy-start.11 = (bf16[256,1280]{1,0:T(8,128)(2,1)S(1)}, bf16[256,1280]{1,0:T(8,128)(2,1)}, u32[]{:S(2)}) copy-start(bf16[256,1280]{1,0:T(8,128)(2,1)} %param.20) | copy-start | bytes 1966084
  2447.6 196.1 %copy-start.36 = (f32[1280]{0:T(1024)S(1)}, f32[1280]{0:T(1024)}, u32[]{:S(2)}) copy-start(f32[1280]{0:T(1024)} %copy-done.35) | copy-start | bytes 15364
  2447.6 196.1 %copy-start.53 = (f32[256]{0:T(256)S(1)}, f32[256]{0:T(256)}, u32[]{:S(2)}) copy-start(f32[256]{0:T(256)} %copy-done.52) | copy-start | bytes 3076
  2447.6 202.8 %copy-start.49 = (f32[1280]{0:T(1024)S(1)}, f32[1280]{0:T(1024)}, u32[]{:S(2)}) copy-start(f32[1280]{0:T(1024)} %get-tuple-element.280) | copy-start | bytes 15364
  2447.6 262.7 %copy-start.15 = (bf16[256,1280]{1,0:T(8,128)(2,1)S(1)}, bf16[256,1280]{1,0:T(8,128)(2,1)}, u32[]{:S(2)}) copy-start(bf16[256,1280]{1,0:T(8,128)(2,1)} %param.21) | copy-start | bytes 1966084
  2447.6 262.7 %copy-start.34 = (f32[1280]{0:T(1024)S(1)}, f32[1280]{0:T(1024)}, u32[]{:S(2)}) copy-start(f32[1280]{0:T(1024)} %copy-done.33) | copy-start | bytes 15364
  2447.6 262.7 %copy-start.51 = (f32[256]{0:T(256)S(1)}, f32[256]{0:T(256)}, u32[]{:S(2)}) copy-start(f32[256]{0:T(256)} %copy-done.50) | copy-start | bytes 3076
  2447.6 262.7 %copy-start.57 = (f32[256]{0:T(256)S(1)}, f32[256]{0:T(256)}, u32[]{:S(2)}) copy-start(f32[256]{0:T(256)} %copy-done.56) | copy-start | bytes 3076
  2600.8 109.5 %copy-start.8 = (f32[256,1280]{1,0:T(8,128)S(1)}, f32[256,1280]{1,0:T(8,128)}, u32[]{:S(2)}) copy-start(f32[256,1280]{1,0:T(8,128)} %copy-done.7) | copy-start | bytes 3932164
  (55 other events, 211.0 us)
Sparse Core Ops, SparseCore 0:
  18.1 27.3 all-gather.19
  51.1 40.8 all-reduce.21
  93.6 28.5 all-gather.23
  123.6 17.4 all-gather.21
  143.8 51.9 reduce-scatter.20
  244.6 24.2 all-gather.25
  275.0 51.3 reduce-scatter.22
  328.5 25.5 all-gather.31
  356.3 25.5 all-gather.27
  384.6 79.8 reduce-scatter.28
  466.9 150.1 reduce-scatter.24
  625.0 83.3 all-gather.33
  724.1 51.3 reduce-scatter.30
  785.7 25.5 all-gather.35
  816.9 37.5 reduce-scatter.32
  1053.1 52.8 all-gather.37
  1108.7 23.2 all-reduce.17
  1133.5 81.6 all-gather.29
  1244.3 63.1 all-reduce.19
  1310.4 31.2 reduce-scatter.38
  1344.8 140.1 reduce-scatter.46
  1487.9 62.9 reduce-scatter.40
  1553.1 35.3 reduce-scatter.36
  1590.0 43.8 all-gather.39
  1636.3 146.5 reduce-scatter.44
  1785.2 147.3 reduce-scatter.42
  1935.3 22.9 reduce-scatter.50
  1959.8 33.0 all-gather.43
  1994.5 145.8 all-gather.51
  2141.9 63.8 all-gather.45
  2207.4 36.2 all-gather.41
  2246.5 30.0 reduce-scatter.48
  2278.0 159.6 all-gather.49
  2439.3 151.5 all-gather.47
  2594.0 49.6 reduce-scatter.34
  2646.2 52.0 reduce-scatter.26
where the time goes:
time: 2730 us
  waiting for transfers between devices  1890 us (69%)
  matrix products  340 us (12%)
  blocking collectives  335 us (12%)
  local copies, waits for them, and re-layouts  73 us (3%)
  other arithmetic  61.1 us (2%)
    reduce_scatter x4, waiting for transfers between devices, reduce_queries(): lax.psum_scatter(term_of(jnp.int32(0), lax.axis_size('row') * row_count),...  293 us
    psum x1, blocking collectives, per_device(): lax.psum((keys_total.reshape(group_rows, head_count * (NOPE + VD)), rope_...  183 us
    reduce_scatter x1, waiting for transfers between devices, share_feedforward(): lax.psum_scatter(gate_grad, 'dp', scatter_dimension=0, tiled=True)  150 us
    all_gather x1, waiting for transfers between devices, per_device(): lax.all_gather(feedforward_parts[2], 'dp', axis=0, tiled=True)  148 us
    reduce_scatter x4, waiting for transfers between devices, reduce_tokens(): lax.psum_scatter(term_of(jnp.int32(0), lax.axis_size('col') * row_count),...  144 us
    all_gather x1, waiting for transfers between devices, per_device(): lax.all_gather(feedforward_parts[0], 'dp', axis=0, tiled=True)  143 us
    reduce_scatter x1, waiting for transfers between devices, share_feedforward(): lax.psum_scatter(down_grad, 'dp', scatter_dimension=0, tiled=True)  143 us
    reduce_scatter x1, waiting for transfers between devices, share_feedforward(): lax.psum_scatter(up_grad, 'dp', scatter_dimension=0, tiled=True)  141 us
  transfers between devices with their start and end apart: 36, of which 32 were waited for; matrix products, arithmetic and copies ran while one was open for 6% of the time, Pallas kernels for 0%

commit v1 on v0

v1 whole, which is shorter than its diff:
```python
import math

import jax
import jax.numpy as jnp
from jax import lax
from jax.experimental import pallas as pl
from jax.experimental.pallas import tpu as pltpu
from jax.sharding import PartitionSpec as P

D = 2560
QR = 768
KVR = 256
NOPE = 64
RD = 32
VD = 64
SLOT = 128

EPSILON = 1e-05
RESIDUAL_SCALE = 1.4 / math.sqrt(62.0)
SCORE_SCALE = (NOPE + RD) ** (-0.5)
MASKED = -1000000000.0
F32 = jnp.float32
BF16 = jnp.bfloat16

OVER_X = ((0, 1), (1, 0))
OVER_CORE = ((0, 1), (1, 0), (2, 3), (3, 2))
OVER_Y = ((0, 2), (1, 3), (2, 0), (3, 1))
OVER_YCORE = ((0, 3), (1, 2), (2, 1), (3, 0))


def px(values):
    return lax.ppermute(values, "row", OVER_X)


def pc(values):
    return lax.ppermute(values, "col", OVER_CORE)


def py(values):
    return lax.ppermute(values, "col", OVER_Y)


def pyc(values):
    return lax.ppermute(values, "col", OVER_YCORE)


def dot(a, b, contract, out=F32):
    return lax.dot_general(a, b, ((contract[:1], contract[1:]), ((), ())), preferred_element_type=out)


def rows_at(values, start, length):
    return lax.dynamic_slice_in_dim(values, start, length, 0)


def put(target, piece, row, column):
    return lax.dynamic_update_slice(target, piece, (row, column))


def pair(first_is_own, own, other, axis):
    return jnp.where(
        first_is_own,
        jnp.concatenate([own, other], axis),
        jnp.concatenate([other, own], axis),
    )


def gather_plane(own):
    half = own.shape[0] // 2
    from_x, from_y = px(own), py(own)
    far = [py(from_x[:half]), px(from_y[half:])]
    same_core = jnp.concatenate([own, from_x, from_y] + far, 0)
    return jnp.concatenate([same_core, pc(same_core)], 0)


def scatter_plane(partial):
    rows = partial.shape[0] // 8
    half = rows // 2
    other = pc(partial[4 * rows :])
    total = (partial[: 4 * rows].astype(F32) + other.astype(F32)).astype(BF16)
    own, to_x, to_y, far = (total[i * rows : (i + 1) * rows] for i in range(4))
    for_y, for_x = px(far[:half]), py(far[half:])
    y_top = (to_y[:half].astype(F32) + for_y.astype(F32)).astype(BF16)
    x_low = (to_x[half:].astype(F32) + for_x.astype(F32)).astype(BF16)
    from_x = px(jnp.concatenate([to_x[:half], x_low], 0))
    from_y = py(jnp.concatenate([y_top, to_y[half:]], 0))
    return own.astype(F32) + from_x.astype(F32) + from_y.astype(F32)


def swap_over_x(values, dp_place, dp_size):
    if dp_size % 2:
        return px(values)
    half = values.shape[0] // 2
    odd = dp_place % 2
    mine = px(rows_at(values, odd * half, half))
    pairs = [(i, i ^ 1) for i in range(dp_size)]
    other = lax.ppermute(mine, "dp", pairs)
    return pair(odd == 0, mine, other, 0)


def total_over(values, axes, dp_size):
    if "core" in axes:
        values = values + pc(values)
    if "y" in axes:
        values = values + py(values)
    if "x" in axes:
        values = values + px(values)
    if dp_size & (dp_size - 1):
        return lax.psum(values, "dp")
    step = 1
    while step < dp_size:
        values = values + lax.ppermute(values, "dp", [(i, i ^ step) for i in range(dp_size)])
        step *= 2
    return values


def rms_norm(values, scaling):
    return values * lax.rsqrt(jnp.mean(values * values, axis=-1, keepdims=True) + EPSILON) * scaling


def rotate(values, cosine, sine_part):
    half_width = values.shape[-1] // 2
    first_half = values[..., :half_width]
    second_half = values[..., half_width:]
    return jnp.concatenate(
        [
            first_half * cosine - second_half * sine_part,
            second_half * cosine + first_half * sine_part,
        ],
        axis=-1,
    )


def turned(values, cosine, low_sine, high_sine):
    return (
        values * cosine
        + pltpu.roll(values, SLOT - RD // 2, 1) * low_sine
        + pltpu.roll(values, RD // 2, 1) * high_sine
    )


def allowed_bias(q_seq, q_block, k_seq, k_block):
    allowed = (q_seq == k_seq) & (k_block <= q_block)
    return jnp.where(allowed, 0.0, MASKED)


def attend_kernel(
    heads, comp, lat, rope, cosine, low_sine, high_sine, w_query, w_keyval, q_seq, q_block, k_seq, k_block,
    query_out, key_out, value_out, attended_out, lse_out,
):
    @pl.when(pl.program_id(0) == 0)
    def _():
        keyval = jnp.dot(lat[...], w_keyval[...], preferred_element_type=F32)
        lanes = lax.broadcasted_iota(jnp.int32, (lat.shape[0], SLOT), 1)
        for h in range(heads):
            part = keyval[:, h * SLOT : (h + 1) * SLOT]
            key_out[:, h * SLOT : (h + 1) * SLOT] = jnp.where(
                lanes < NOPE, part, rope[...].astype(F32)
            ).astype(BF16)
            value_out[:, h * VD : (h + 1) * VD] = part[:, NOPE:].astype(BF16)

    bias = allowed_bias(q_seq[...], q_block[...], k_seq[...], k_block[...])
    raw = jnp.dot(comp[...], w_query[...], preferred_element_type=F32)
    for h in range(heads):
        slot = slice(h * SLOT, (h + 1) * SLOT)
        query = turned(raw[:, slot], cosine[...], low_sine[...], high_sine[...]).astype(BF16)
        query_out[:, slot] = query
        scores = dot(query, key_out[:, slot], (1, 1)) * SCORE_SCALE + bias
        highest = jnp.max(scores, axis=1, keepdims=True)
        powers = jnp.exp(scores - highest)
        total = jnp.sum(powers, axis=1, keepdims=True)
        probs = (powers * (1.0 / total)).astype(BF16)
        result = jnp.dot(probs, value_out[:, h * VD : (h + 1) * VD], preferred_element_type=F32)
        attended_out[:, h * VD : (h + 1) * VD] = result.astype(BF16)
        lse_out[:, h : h + 1] = highest + jnp.log(total)


def attend_back_kernel(
    heads, query, key, value, lse, grad_out, cosine, low_sine, high_sine, q_seq, q_block, k_seq, k_block,
    query_grad, keyval_grad, rope_grad, key_total, value_total,
):
    step = pl.program_id(0)

    @pl.when(step == 0)
    def _():
        key_total[...] = jnp.zeros_like(key_total)
        value_total[...] = jnp.zeros_like(value_total)

    bias = allowed_bias(q_seq[...], q_block[...], k_seq[...], k_block[...])
    for h in range(heads):
        slot = slice(h * SLOT, (h + 1) * SLOT)
        narrow = slice(h * VD, (h + 1) * VD)
        scores = dot(query[:, slot], key[:, slot], (1, 1)) * SCORE_SCALE + bias
        probs = jnp.exp(scores - lse[:, h : h + 1])
        grad_probs = dot(grad_out[:, narrow], value[:, narrow], (1, 1))
        inner = jnp.sum(probs * grad_probs, axis=1, keepdims=True)
        grad_dots = (probs * (grad_probs - inner) * SCORE_SCALE).astype(BF16)
        back = jnp.dot(grad_dots, key[:, slot], preferred_element_type=F32)
        query_grad[:, slot] = turned(back, cosine[...], -low_sine[...], -high_sine[...]).astype(BF16)
        key_total[:, slot] += dot(grad_dots, query[:, slot], (0, 0))
        value_total[:, narrow] += dot(probs.astype(BF16), grad_out[:, narrow], (0, 0))

    @pl.when(step == pl.num_programs(0) - 1)
    def _():
        rope_total = jnp.zeros((key.shape[0], SLOT), F32)
        for h in range(heads):
            part = key_total[:, h * SLOT : (h + 1) * SLOT]
            rope_total = rope_total + part
            keyval_grad[:, h * SLOT : h * SLOT + NOPE] = part[:, :NOPE].astype(BF16)
            keyval_grad[:, h * SLOT + NOPE : (h + 1) * SLOT] = value_total[:, h * VD : (h + 1) * VD].astype(BF16)
        rope_grad[...] = rope_total[:, NOPE : NOPE + RD]


def row_tile(rows, width):
    return pl.BlockSpec((rows, width), lambda i: (i, 0))


def whole(shape):
    return pl.BlockSpec(shape, lambda i: (0, 0))


def attend(comp, lat, rope, turns, w_query, w_keyval, marks, heads, tile):
    rows = comp.shape[0]
    column = row_tile(tile, 1)
    line = whole((1, rows))
    return pl.pallas_call(
        lambda *refs: attend_kernel(heads, *refs),
        grid=(rows // tile,),
        in_specs=[
            row_tile(tile, QR), whole((rows, KVR)), whole((rows, SLOT)),
            row_tile(tile, SLOT), row_tile(tile, SLOT), row_tile(tile, SLOT),
            whole(w_query.shape), whole(w_keyval.shape), column, column, line, line,
        ],
        out_specs=[
            row_tile(tile, heads * SLOT), whole((rows, heads * SLOT)), whole((rows, heads * VD)),
            row_tile(tile, heads * VD), row_tile(tile, 8),
        ],
        out_shape=[
            jax.ShapeDtypeStruct((rows, heads * SLOT), BF16),
            jax.ShapeDtypeStruct((rows, heads * SLOT), BF16),
            jax.ShapeDtypeStruct((rows, heads * VD), BF16),
            jax.ShapeDtypeStruct((rows, heads * VD), BF16),
            jax.ShapeDtypeStruct((rows, 8), F32),
        ],
        compiler_params=pltpu.CompilerParams(vmem_limit_bytes=48 << 20),
        cost_estimate=pl.CostEstimate(
            flops=2 * rows * heads * (rows * 2 * SLOT + QR * SLOT), bytes_accessed=8 << 20,
            transcendentals=heads * rows * rows,
        ),
        name="attend",
    )(comp, lat, rope, *turns, w_query, w_keyval, *marks)


def attend_back(query, key, value, lse, grad_out, turns, marks, heads, tile):
    rows = query.shape[0]
    column = row_tile(tile, 1)
    line = whole((1, rows))
    return pl.pallas_call(
        lambda *refs: attend_back_kernel(heads, *refs),
        grid=(rows // tile,),
        in_specs=[
            row_tile(tile, heads * SLOT), whole((rows, heads * SLOT)), whole((rows, heads * VD)),
            row_tile(tile, 8), row_tile(tile, heads * VD),
            row_tile(tile, SLOT), row_tile(tile, SLOT), row_tile(tile, SLOT), column, column, line, line,
        ],
        out_specs=[
            row_tile(tile, heads * SLOT), whole((rows, heads * SLOT)), whole((rows, RD)),
        ],
        out_shape=[
            jax.ShapeDtypeStruct((rows, heads * SLOT), BF16),
            jax.ShapeDtypeStruct((rows, heads * SLOT), BF16),
            jax.ShapeDtypeStruct((rows, RD), F32),
        ],
        scratch_shapes=[pltpu.VMEM((rows, heads * SLOT), F32), pltpu.VMEM((rows, heads * VD), F32)],
        compiler_params=pltpu.CompilerParams(vmem_limit_bytes=48 << 20),
        cost_estimate=pl.CostEstimate(
            flops=2 * rows * heads * rows * 5 * SLOT, bytes_accessed=8 << 20, transcendentals=heads * rows * rows,
        ),
        name="attend_back",
    )(query, key, value, lse, grad_out, *turns, *marks)


def feedforward(rows, grad_rows, gate_up, down):
    units = down.shape[0]
    both = dot(gate_up, rows, (1, 1))
    return activate(both[:units], both[units:], dot(down, grad_rows, (1, 1)))


def activate(gate, up, grad_act):
    sigmoid_gate = jax.nn.sigmoid(gate)
    swish = gate * sigmoid_gate
    grad_gate = grad_act * up * sigmoid_gate * (1.0 + gate * (1.0 - sigmoid_gate))
    return (
        (swish * up).astype(BF16),
        jnp.concatenate([grad_gate.astype(BF16), (grad_act * swish).astype(BF16)], 0),
    )


def together(*values):
    return lax.optimization_barrier(values)


def per_device(
    dp_size, hidden, cotangent, sequence_index, block_index, attention_gain, query_down, query_gain, query_up,
    latent_down, latent_gain, latent_up, attention_out, feedforward_gain, gate_weight, up_weight, down_weight,
):
    dp_place, row, col = lax.axis_index("dp"), lax.axis_index("row"), lax.axis_index("col")
    first_x = row == 0
    token_rows = hidden.shape[0]
    own_rows = token_rows // 2
    group_rows = sequence_index.shape[0]
    half_width = hidden.shape[1]
    heads = query_up.shape[1] // (NOPE + RD) // 2
    units = gate_weight.shape[1] // 2
    tile = group_rows // 4
    shard_order = [(a, b) for b in (0, 2) for a in (0, 1)] + [(a, b) for b in (1, 3) for a in (0, 1)]
    places = [((col ^ b) * 2 + (row ^ a)) for a, b in shard_order]

    def half_of(values, axis, which):
        length = values.shape[axis] // 2
        return lax.dynamic_slice_in_dim(values, which * length, length, axis)

    stream = pair(first_x, half_of(hidden, 0, row), px(half_of(hidden, 0, 1 - row)), 1).astype(F32)
    latent_tile = jnp.concatenate([query_down.T, latent_down.T], 0)
    tile_width = latent_tile.shape[0]
    near_tiles = jnp.concatenate([latent_tile, py(latent_tile)], 0)
    latent_weights = jnp.concatenate([near_tiles, pc(near_tiles)], 0)

    query_columns = query_up.shape[1] // 2
    other_query = px(half_of(query_up, 1, 1 - row))
    w_query = pair(first_x, half_of(query_up, 1, row), other_query, 0)
    w_query = jnp.pad(w_query.reshape(QR, heads, NOPE + RD), ((0, 0), (0, 0), (0, SLOT - NOPE - RD)))
    w_query = w_query.reshape(QR, heads * SLOT)
    w_keyval = half_of(latent_up, 1, row)
    w_out = pair(first_x, half_of(attention_out, 0, row), px(half_of(attention_out, 0, 1 - row)), 1)

    def whole_units(tile_t):
        other = swap_over_x(rows_at(tile_t, (1 - row) * units, units), dp_place, dp_size)
        return pair(first_x, rows_at(tile_t, row * units, units), other, 1)

    gate_up = jnp.concatenate([whole_units(gate_weight.T), whole_units(up_weight.T)], 0)
    down = whole_units(down_weight)

    incoming = pair(first_x, half_of(cotangent, 0, row), px(half_of(cotangent, 0, 1 - row)), 1).astype(F32)
    grad_down_own = (RESIDUAL_SCALE * incoming).astype(BF16)
    grad_down = gather_plane(grad_down_own)
    by_factors = dp_size == 4
    every = ("dp", "row", "col")

    second = jnp.sum((sequence_index == sequence_index[0]).astype(jnp.int32))
    inverse_rate = -2.0 * math.log(10000.0) / RD

    def in_order(values):
        return jnp.concatenate([rows_at(values, place * own_rows, own_rows) for place in places], 0)

    seq_all, block_all = in_order(sequence_index), in_order(block_index)
    index_all = in_order(jnp.arange(group_rows, dtype=jnp.int32))
    position = (index_all - jnp.where(seq_all == sequence_index[0], 0, second)).astype(F32)
    lane = jnp.arange(SLOT, dtype=jnp.int32)
    turning = (lane >= NOPE) & (lane < NOPE + RD)
    rate = jnp.exp(((lane - NOPE) % (RD // 2)).astype(F32) * inverse_rate)
    angle = jnp.where(turning, rate, 0.0)[None, :] * position[:, None]
    cosine, sine = jnp.cos(angle), jnp.sin(angle)
    low_sine = jnp.where(lane < NOPE + RD // 2, -sine, 0.0)
    high_sine = jnp.where(lane >= NOPE + RD // 2, sine, 0.0)
    turns = (cosine, low_sine, high_sine)
    marks = (seq_all[:, None], block_all[:, None], seq_all[None, :], block_all[None, :])
    own_cosine = cosine[:own_rows, NOPE : NOPE + RD // 2]
    own_sine = sine[:own_rows, NOPE : NOPE + RD // 2]

    gain_in = attention_gain.astype(F32)
    inverse_in = lax.rsqrt(jnp.mean(stream * stream, axis=1) + EPSILON)
    inverse_half = pair(first_x, inverse_in, px(inverse_in[None, :])[0], 0)
    scaled_in = hidden.astype(F32) * inverse_half[:, None]
    normed_half = (scaled_in * gain_in[None, :]).astype(BF16)
    latent_part = dot(normed_half, latent_weights, (1, 1))
    latent_raw = half_of(latent_part, 0, row) + px(half_of(latent_part, 0, 1 - row))

    def in_place(values):
        blocks = [values[:, i * tile_width : (i + 1) * tile_width] for i in range(4)]
        core, high = (col % 2) == 1, (col // 2) == 1
        b0, b2, b1, b3 = blocks
        c0, c1 = jnp.where(core, b1, b0), jnp.where(core, b0, b1)
        c2, c3 = jnp.where(core, b3, b2), jnp.where(core, b2, b3)
        return (
            jnp.where(high, c2, c0), jnp.where(high, c3, c1), jnp.where(high, c0, c2), jnp.where(high, c1, c3),
        )

    blocks = in_place(latent_raw)
    query_tile = query_down.shape[1]
    query_latent = jnp.concatenate([b[:, :query_tile] for b in blocks], 1)
    kv_latent = jnp.concatenate([b[:, query_tile:] for b in blocks], 1)

    def latent_norms(query_values, key_values, query_scaling, key_scaling):
        return (
            rms_norm(query_values, query_scaling),
            rms_norm(key_values[:, :KVR], key_scaling),
            rotate(key_values[:, KVR:], own_cosine, own_sine),
        )

    own_latents, latent_back = jax.vjp(
        latent_norms, query_latent, kv_latent, query_gain.astype(F32), latent_gain.astype(F32)
    )
    latents = gather_plane(jnp.concatenate(own_latents, 1).astype(BF16))
    if by_factors:
        grad_down_late, latents = together(grad_down_own, latents)
        grads_all = lax.all_gather(grad_down_late, every, axis=0, tiled=True)
    compressed, latent = latents[:, :QR], latents[:, QR : QR + KVR]
    rope = jnp.pad(latents[:, QR + KVR :], ((0, 0), (NOPE, SLOT - NOPE - RD)))

    query, key, value, attended, lse = attend(
        compressed, latent, rope, turns, w_query, w_keyval, marks, heads, tile
    )

    middle = stream + RESIDUAL_SCALE * scatter_plane(dot(attended, w_out, (1, 0), BF16))
    gain_mid = pair(first_x, feedforward_gain, px(feedforward_gain), 0).astype(F32)
    inverse_mid = lax.rsqrt(jnp.mean(middle * middle, axis=1, keepdims=True) + EPSILON)
    scaled_mid = middle * inverse_mid
    normed_mid_own = (scaled_mid * gain_mid[None, :]).astype(BF16)
    normed_mid = gather_plane(normed_mid_own)

    if by_factors:
        rows_all = lax.all_gather(normed_mid_own, every, axis=0, tiled=True)

    activation, grad_both = feedforward(normed_mid, grad_down, gate_up, down)
    mid_part = dot(grad_both, gate_up, (0, 0), BF16)
    output_part = dot(activation, down, (0, 0), BF16)
    if by_factors:
        mid_part, grads_all = together(mid_part, grads_all)
        odd = dp_place % 2
        own_units = units // 2

        def own_half(weights):
            return rows_at(weights, odd * own_units, own_units)

        down_half = own_half(down)
        gate_up_half = jnp.concatenate([own_half(gate_up[:units]), own_half(gate_up[units:])], 0)
        grad_act_all = dot(down_half, grads_all, (1, 1))
    upstream_mid = scatter_plane(mid_part)
    if by_factors:
        upstream_mid, grad_act_all, output_part = together(upstream_mid, grad_act_all, output_part)
    weighted = upstream_mid * gain_mid[None, :]
    mean_inner = jnp.mean(weighted * scaled_mid, axis=1, keepdims=True)
    gain_mid_part = jnp.sum(upstream_mid * scaled_mid, axis=0)
    grad_middle = incoming + inverse_mid * (weighted - scaled_mid * mean_inner)
    grad_branch = gather_plane((RESIDUAL_SCALE * grad_middle).astype(BF16))

    grad_attended = dot(grad_branch, w_out, (1, 1), BF16)
    query_grad, keyval_grad, rope_grad = attend_back(
        query, key, value, lse, grad_attended, turns, marks, heads, tile
    )
    latent_grad_part = jnp.concatenate(
        [
            dot(query_grad, w_query, (1, 1), BF16),
            dot(keyval_grad, w_keyval, (1, 1), BF16),
            rope_grad.astype(BF16),
        ],
        1,
    )
    if by_factors:
        latent_grad_part, rows_all = together(latent_grad_part, rows_all)
        both_all = dot(gate_up_half, rows_all, (1, 1))
    latent_grad = scatter_plane(latent_grad_part)
    if by_factors:
        latent_grad, both_all = together(latent_grad, both_all)
    query_latent_grad, kv_latent_grad, query_gain_part, latent_gain_part = latent_back(
        (latent_grad[:, :QR], latent_grad[:, QR : QR + KVR], latent_grad[:, QR + KVR :])
    )
    kv_tile = latent_down.shape[1]
    query_low, kv_low = query_latent_grad.astype(BF16), kv_latent_grad.astype(BF16)
    inner_in = (
        jnp.sum(query_low.astype(F32) * query_latent, axis=1) + jnp.sum(kv_low.astype(F32) * kv_latent, axis=1)
    ) / D
    in_blocks = jnp.concatenate(
        [
            part
            for i in (0, 2, 1, 3)
            for part in (
                query_low[:, i * query_tile : (i + 1) * query_tile],
                kv_low[:, i * kv_tile : (i + 1) * kv_tile],
            )
        ],
        1,
    )
    g0, g1, g2, g3 = in_place(in_blocks)
    latent_low = jnp.concatenate([g0, g2, g1, g3], 1)
    latent_low = pair(first_x, latent_low, px(latent_low), 0)
    inner_half = pair(first_x, inner_in, px(inner_in[None, :])[0], 0)
    grad_normed = dot(latent_low, latent_weights, (1, 0))
    grad_middle_half = pair(
        first_x,
        half_of(grad_middle, 1, row),
        px(half_of(grad_middle, 1, 1 - row).astype(BF16)).astype(F32),
        0,
    )
    grad_in = inverse_half[:, None] * (grad_normed * gain_in[None, :] - scaled_in * inner_half[:, None])
    input_gradient = (grad_middle_half + grad_in).astype(BF16)
    gain_in_total = total_over(
        jnp.sum(grad_normed * scaled_in, axis=0).reshape(-1, SLOT), ("core", "y"), dp_size
    ).reshape(-1)

    output_own = (middle + RESIDUAL_SCALE * scatter_plane(output_part)).astype(BF16)
    output = pair(first_x, half_of(output_own, 1, row), px(half_of(output_own, 1, 1 - row)), 0)

    if by_factors:
        act_all, grad_both_all = together(*activate(both_all[:own_units], both_all[own_units:], grad_act_all))
        up_total = dot(grad_both_all[own_units:], rows_all, (1, 0), BF16)
        gate_total = dot(grad_both_all[:own_units], rows_all, (1, 0), BF16)
        down_total_ff = dot(act_all, grads_all, (1, 0), BF16)
        pairs = [(i, i ^ 1) for i in range(dp_size)]

        def pz(values):
            return lax.ppermute(values, "dp", pairs)

        def to_tile(total):
            kept = half_of(total, 1, row)
            fetched = px(half_of(total, 1, 1 - row))
            kept, fetched = pair(odd == 0, kept, pz(kept), 0), pair(odd == 0, fetched, pz(fetched), 0)
            return pair(first_x, kept, fetched, 0).astype(F32)

        up_grad_t, gate_grad_t, down_grad = (to_tile(g) for g in (up_total, gate_total, down_total_ff))
    else:

        def to_tile(part):
            total = lax.psum(part, "dp")
            return pair(first_x, half_of(total, 1, row), px(half_of(total, 1, 1 - row)), 0).astype(F32)

        up_grad_t, gate_grad_t, down_grad = (
            to_tile(dot(a, b, (1, 0), BF16))
            for a, b in (
                (grad_both[units:], normed_mid), (grad_both[:units], normed_mid), (activation, grad_down),
            )
        )

    out_part = dot(attended, grad_branch, (0, 0), BF16)
    out_grad = lax.psum(pair(first_x, half_of(out_part, 1, row), px(half_of(out_part, 1, 1 - row)), 0), "dp")
    up_part = dot(compressed, query_grad, (0, 0), BF16).reshape(QR, heads, SLOT)[:, :, : NOPE + RD]
    up_part = up_part.reshape(QR, query_columns)
    query_up_grad = lax.psum(pair(first_x, half_of(up_part, 0, row), px(half_of(up_part, 0, 1 - row)), 1), "dp")
    latent_part_grad = dot(latent, keyval_grad, (0, 0), BF16)
    latent_up_grad = lax.psum(pair(first_x, latent_part_grad, px(latent_part_grad), 1), "dp")
    normed_rows = jnp.concatenate([normed_half, py(normed_half)], 0)
    normed_rows = jnp.concatenate([normed_rows, pc(normed_rows)], 0)
    low_blocks = [latent_low[:, i * tile_width : (i + 1) * tile_width] for i in range(4)]
    low_rows = jnp.concatenate([low_blocks[0], py(low_blocks[1]), pc(low_blocks[2]), pyc(low_blocks[3])], 0)
    down_part = dot(low_rows, normed_rows, (0, 0), BF16)
    down_total = lax.psum(down_part, "dp").astype(F32)

    own_gains = jnp.concatenate([gain_mid_part, query_gain_part, latent_gain_part]).reshape(-1, SLOT)
    gain_totals = total_over(own_gains, ("core", "y", "x"), dp_size).reshape(-1)
    width = 2 * half_width
    return (
        output,
        input_gradient,
        gain_in_total,
        down_total[:query_tile].T,
        gain_totals[width : width + QR],
        query_up_grad.astype(F32),
        down_total[query_tile:].T,
        gain_totals[width + QR :],
        latent_up_grad.astype(F32),
        out_grad.astype(F32),
        lax.dynamic_slice_in_dim(gain_totals, row * half_width, half_width, 0),
        gate_grad_t.T,
        up_grad_t.T,
        down_grad,
    )


def solution(mesh):
    dp_size = mesh.shape["dp"]

    def program(*arguments):
        return per_device(dp_size, *arguments)

    return jax.shard_map(
        program,
        mesh=mesh,
        in_specs=(
            P(("dp", "col"), "row"),
            P(("dp", "col"), "row"),
            P("dp"),
            P("dp"),
            P("row"),
            P("row", "col"),
            P(),
            P("row", "col"),
            P("row", "col"),
            P(),
            P(None, "col"),
            P("col", "row"),
            P("row"),
            P("row", "col"),
            P("row", "col"),
            P("col", "row"),
        ),
        out_specs=(
            P(("dp", "col"), "row"),
            P(("dp", "col"), "row"),
            P("row"),
            P("row", "col"),
            P(),
            P("row", "col"),
            P("row", "col"),
            P(),
            P(None, "col"),
            P("col", "row"),
            P("row"),
            P("row", "col"),
            P("row", "col"),
            P("col", "row"),
        ),
        check_vma=False,
    )
```

time: 2730 us -> 1100 us (0.40)
  waiting for transfers between devices: 1890 us -> 607 us
  blocking collectives: 335 us -> 0 us
  matrix products: 340 us -> 155 us
  starting transfers between devices: 3.46 us -> 78.3 us
  Pallas kernels: 0 us -> 44.5 us
  other arithmetic: 61.1 us -> 97.6 us
    reduce_scatter x14 -> x0, waiting for transfers between devices: 981 us -> none  [the longest x4 293 us: reduce_queries(): lax.psum_scatter(term_of(jnp.int32(0), lax.axis_size('row') * row_count),...]
    all_gather x17 -> x2, waiting for transfers between devices: 792 us -> 0.01 us  [the longest x1 0.01 us: per_device(): grads_all = lax.all_gather(grad_down_late, every, axis=0, tiled=True)]
    ppermute x0 -> x85, waiting for transfers between devices: none -> 607 us  [the longest x37 230 us: px(): return lax.ppermute(values, 'row', OVER_X)]
    psum x6 -> x0, blocking collectives: 263 us -> none  [the longest x1 183 us: per_device(): lax.psum((keys_total.reshape(group_rows, head_count * (NOPE + VD)), rope_...]
    dot_general x44 -> x19, matrix products: 336 us -> 155 us  [dot(): lax.dot_general(a, b, ((contract[:1], contract[1:]), ((), ())), preferred...]
    ppermute x0 -> x85, starting transfers between devices: none -> 77.4 us  [the longest x37 41.7 us: px(): return lax.ppermute(values, 'row', OVER_X)]
    psum x3 -> x1, waiting for transfers between devices: 76.8 us -> 0.01 us  [per_device(): down_total = lax.psum(down_part, 'dp').astype(F32)]
    all_gather x2 -> x0, blocking collectives: 52.2 us -> none  [the longest x1 34.6 us: per_device(): lax.all_gather(attention_parts[0], 'dp', axis=0, tiled=True)]
  transfers between devices with their start and end apart: 36 -> 88, of which waited for: 32 -> 52; matrix products, arithmetic and copies ran while one was open for 6% -> 29% of each run, Pallas kernels for 0% -> 4%
where the time goes in v1:
time: 1100 us; the launch traced here: 1090 us
  waiting for transfers between devices  607 us (55%)
  matrix products  155 us (14%)
  other arithmetic  97.6 us (9%)
  local copies, waits for them, and re-layouts  93.1 us (8%)
  starting transfers between devices  78.3 us (7%)
  Pallas kernels  44.5 us (4%)
  between operations  15.9 us (1%)
    ppermute x37, waiting for transfers between devices, px(): return lax.ppermute(values, 'row', OVER_X)  230 us
    ppermute x6, waiting for transfers between devices, pz(): return lax.ppermute(values, 'dp', pairs)  183 us
    dot_general x19, matrix products, dot(): lax.dot_general(a, b, ((contract[:1], contract[1:]), ((), ())), preferred...  155 us
    ppermute x21, waiting for transfers between devices, py(): return lax.ppermute(values, 'col', OVER_Y)  87.7 us
    ppermute x3, waiting for transfers between devices, swap_over_x(): other = lax.ppermute(mine, 'dp', pairs)  83.6 us
    ppermute x37, starting transfers between devices, px(): return lax.ppermute(values, 'row', OVER_X)  41.7 us
    select_n x20, other arithmetic, pair(): jnp.where(first_is_own, jnp.concatenate([own, other], axis), jnp.concaten...  36.2 us
    pallas_call x1, Pallas kernels, attend_back(): pl.pallas_call(lambda *refs: attend_back_kernel(heads, *refs), grid=(rows...  26.1 us
  transfers between devices with their start and end apart: 88, of which 52 were waited for; matrix products, arithmetic and copies ran while one was open for 29% of the time, Pallas kernels for 4%

profile of v1, /device:TPU:0, one launch (start us, length us, event | category | flops | bytes accessed | tf_op | source)
XLA Modules:
  0.0 1091.1 jit_solution(12171155168218509691)
XLA Ops:
  9.2 2.9 collective-permute-start
  17.2 13.8 %collective-permute-done.3 = bf16[264,1280]{1,0:T(8,128)(2,1)S(1)} collective-permute-done((bf16[264,1280]{1,0:T(8,128)(2,1)}, bf16[264,1280]{1,0:T(8,128)(2,1)S(1)}, u32[]{:S(2)}, u32[]{:S(2)}) %collective-permute-start.3) | collective-permute-done | bytes 675872 | tf_op jit(solution)/shard_map/ppermute | solution.py:40
  33.5 3.0 collective-permute-done.2
  42.9 3.0 fusion.38
  46.1 8.7 collective-permute-done.5
  64.8 3.7 collective-permute-done.6
  79.8 8.9 collective-permute-done.1
  101.7 6.8 collective-permute-done.11
  113.3 2.7 slice.348.refs_0_
  118.2 18.4 %attend.1 = (bf16[1024,640]{1,0:T(8,128)(2,1)}, bf16[1024,640]{1,0:T(8,128)(2,1)}, bf16[1024,320]{1,0:T(8,128)(2,1)S(1)}, bf16[1024,320]{1,0:T(8,128)(2,1)S(1)}, f32[1024,8]{1,0:T(8,128)S(1)}) custom-call(bf16[1024,768]{1,0:T(8,128)(2,1)} %slice.348.refs_0_, bf16[1024,256]{1,0:T(8,128)(2,1)S(1)} %slice.349.refs_1_, bf16[1024,128]{1,0:T(8,128)(2,1)S(1)} %pad.20.refs_2_, ...), custom_call_target="tpu_custom_call" | custom-call | flops 3690987520 | bytes 8388608 | tf_op jit(solution)/shard_map/attend/pallas_call | solution.py:225
  136.6 5.2 fusion.42
  142.1 4.9 collective-permute-done.13
  151.0 6.6 collective-permute-done.14
  162.3 23.8 %collective-permute-done.29 = bf16[1280]{0:T(1024)(128)(2,1)S(1)} collective-permute-done((bf16[1280]{0:T(1024)(128)(2,1)S(1)}, bf16[1280]{0:T(1024)(128)(2,1)S(1)}, u32[]{:S(2)}, u32[]{:S(2)}) %collective-permute-start.29) | collective-permute-done | bytes 2592 | tf_op jit(solution)/shard_map/ppermute | solution.py:32
  207.5 90.6 %collective-permute-done.20 = bf16[128,2560]{1,0:T(8,128)(2,1)S(1)} collective-permute-done((bf16[128,2560]{1,0:T(8,128)(2,1)S(1)}, bf16[128,2560]{1,0:T(8,128)(2,1)S(1)}, u32[]{:S(2)}, u32[]{:S(2)}) %collective-permute-start.20) | collective-permute-done | bytes 655392 | tf_op jit(solution)/shard_map/ppermute | solution.py:32
  304.6 8.9 collective-permute-done.22
  317.0 22.1 %collective-permute-done.30 = bf16[128,2560]{1,0:T(8,128)(2,1)S(1)} collective-permute-done((bf16[128,2560]{1,0:T(8,128)(2,1)S(1)}, bf16[128,2560]{1,0:T(8,128)(2,1)S(1)}, u32[]{:S(2)}, u32[]{:S(2)}) %collective-permute-start.30) | collective-permute-done | bytes 655392 | tf_op jit(solution)/shard_map/ppermute | solution.py:32
  342.1 7.2 collective-permute-done.32
  351.2 7.6 collective-permute-done.33
  361.9 2.7 maximum_select_fusion.8
  364.6 30.3 %collective-permute-done.26 = bf16[400,1280]{1,0:T(8,128)(2,1)S(1)} collective-permute-done((bf16[400,1280]{1,0:T(8,128)(2,1)}, bf16[400,1280]{1,0:T(8,128)(2,1)S(1)}, u32[]{:S(2)}, u32[]{:S(2)}) %collective-permute-start.26) | collective-permute-done | bytes 1024032 | tf_op jit(solution)/shard_map/ppermute | solution.py:96
  397.0 53.4 %collective-permute-done.19 = bf16[400,1280]{1,0:T(8,128)(2,1)S(1)} collective-permute-done((bf16[400,1280]{1,0:T(8,128)(2,1)}, bf16[400,1280]{1,0:T(8,128)(2,1)S(1)}, u32[]{:S(2)}, u32[]{:S(2)}) %collective-permute-start.19) | collective-permute-done | bytes 1024032 | tf_op jit(solution)/shard_map/ppermute | solution.py:96
  454.8 3.0 maximum_select_fusion
  461.1 13.1 %fusion.2 = f32[1600,1024]{1,0:T(8,128)} fusion(bf16[1024,2560]{1,0:T(8,128)(2,1)} %constant_dynamic-update-slice_fusion.30, bf16[800,2560]{1,0:T(8,128)(2,1)S(1)} %maximum_select_fusion.2, bf16[800,2560]{1,0:T(8,128)(2,1)S(1)} %maximum_select_fusion.1), kind=kOutput, calls=%fused_computation.10 | convolution fusion | flops 8404992000 | bytes 19988480 | tf_op jit(solution)/shard_map/dot_general | solution.py:48
  474.2 8.9 multiply_convert_fusion.5
  483.1 12.2 %fusion.1 = bf16[1024,2560]{1,0:T(8,128)(2,1)} fusion(bf16[800,2560]{1,0:T(8,128)(2,1)S(1)} %maximum_select_fusion.2, bf16[800,2560]{1,0:T(8,128)(2,1)S(1)} %maximum_select_fusion.1, bf16[800,1024]{1,0:T(8,128)(2,1)S(1)} %get-tuple-element.83, bf16[800,1024]{1,0:T(8,128)(2,1)S(1)} %get-tuple-element.82), kind=kOutput, calls=%fused_computation.9 | convolution fusion | flops 8411545600 | bytes 16711680 | tf_op jit(solution)/shard_map/dot_general | solution.py:48
  497.5 4.9 collective-permute-done.35
  505.7 10.5 fusion.24
  520.4 15.5 %fusion.22 = f32[400,4096]{1,0:T(8,128)} fusion(bf16[4096,2560]{1,0:T(8,128)(2,1)} %all-gather.3.cloned.1.call-done, bf16[800,2560]{1,0:T(8,128)(2,1)} %maximum_select_fusion, s32[]{:T(128)S(6)} %select_n.462), kind=kOutput, calls=%fused_computation.55 | convolution fusion | flops 8388608000 | bytes 29573124 | tf_op jit(solution)/shard_map/dot_general | solution.py:48
  540.0 4.9 collective-permute-done.40
  549.3 7.8 collective-permute-done.41
  560.3 13.1 %collective-permute-done.44 = bf16[128,2560]{1,0:T(8,128)(2,1)S(1)} collective-permute-done((bf16[128,2560]{1,0:T(8,128)(2,1)S(1)}, bf16[128,2560]{1,0:T(8,128)(2,1)S(1)}, u32[]{:S(2)}, u32[]{:S(2)}) %collective-permute-start.44) | collective-permute-done | bytes 655392 | tf_op jit(solution)/shard_map/ppermute | solution.py:40
  580.1 12.5 %collective-permute-done.47 = bf16[128,2560]{1,0:T(8,128)(2,1)S(1)} collective-permute-done((bf16[128,2560]{1,0:T(8,128)(2,1)S(1)}, bf16[128,2560]{1,0:T(8,128)(2,1)S(1)}, u32[]{:S(2)}, u32[]{:S(2)}) %collective-permute-start.47) | collective-permute-done | bytes 655392 | tf_op jit(solution)/shard_map/ppermute | solution.py:32
  597.5 2.8 collective-permute-done.49
  605.9 16.1 %collective-permute-done.66 = bf16[256,1280]{1,0:T(8,128)(2,1)} collective-permute-done((bf16[256,1280]{1,0:T(8,128)(2,1)}, bf16[256,1280]{1,0:T(8,128)(2,1)}, u32[]{:S(2)}, u32[]{:S(2)}) %collective-permute-start.66) | collective-permute-done | bytes 655392 | tf_op jit(solution)/shard_map/ppermute | solution.py:40
  628.9 4.0 constant_dynamic-slice_fusion.10
  633.7 9.1 collective-permute-done.46
  646.7 4.4 fusion.41.refs_4_
  651.1 26.1 %attend_back.1 = (bf16[1024,640]{1,0:T(8,128)(2,1)}, bf16[1024,640]{1,0:T(8,128)(2,1)}, f32[1024,32]{1,0:T(8,128)S(1)}) custom-call(bf16[1024,640]{1,0:T(8,128)(2,1)} %get-tuple-element.42.refs_0_, bf16[1024,640]{1,0:T(8,128)(2,1)} %get-tuple-element.43.refs_1_, bf16[1024,320]{1,0:T(8,128)(2,1)S(1)} %copy-done.7, f32[1024,8]{1,0:T(8,128)S(1)} %get-tuple-element.45.refs_3_, ...), custom_call_target="tpu_custom_call" | custom-call | flops 6710886400 | bytes 8388608 | tf_op jit(solution)/shard_map/attend_back/pallas_call | solution.py:257
  683.4 3.7 fusion.63
  687.0 3.1 fusion.76
  700.3 22.3 %fusion.3 = f32[800,4096]{1,0:T(8,128)} fusion(bf16[4096,2560]{1,0:T(8,128)(2,1)} %all-gather.5.cloned.1.call-done, bf16[400,2560]{1,0:T(8,128)(2,1)S(1)} %copy-done.43, bf16[400,2560]{1,0:T(8,128)(2,1)S(1)} %copy-done.44), kind=kOutput, calls=%fused_computation.17 | convolution fusion | flops 16785408000 | bytes 38174720 | tf_op jit(solution)/shard_map/dot_general | solution.py:48
  736.4 3.1 maximum_select_fusion.16
  739.5 3.7 collective-permute-done.56
  747.3 7.1 multiply_convert_fusion.1
  754.3 3.6 pad_maximum_fusion.1
  757.9 16.6 %fusion.13 = bf16[400,2560]{1,0:T(8,128)(2,1)S(1)} fusion(bf16[4096,2560]{1,0:T(8,128)(2,1)} %all-gather.5.cloned.1.call-done, bf16[800,4096]{1,0:T(8,128)(2,1)} %pad_maximum_fusion.1), kind=kOutput, calls=%fused_computation.30 | convolution fusion | flops 8388608000 | bytes 26296320 | tf_op jit(solution)/shard_map/dot_general | solution.py:48
  774.6 13.6 %fusion.11 = bf16[400,2560]{1,0:T(8,128)(2,1)} fusion(bf16[4096,2560]{1,0:T(8,128)(2,1)} %all-gather.5.cloned.1.call-done, bf16[800,4096]{1,0:T(8,128)(2,1)S(1)} %copy-done.15), kind=kOutput, calls=%fused_computation.28 | convolution fusion | flops 8388608000 | bytes 26296320 | tf_op jit(solution)/shard_map/dot_general | solution.py:48
  792.9 2.7 collective-permute-done.69
  800.3 12.3 %fusion.77 = bf16[400,2560]{1,0:T(8,128)(2,1)S(1)} fusion(bf16[400,4096]{1,0:T(8,128)(2,1)S(1)} %copy-done.23, bf16[4096,2560]{1,0:T(8,128)(2,1)} %all-gather.3.cloned.1.call-done), kind=kOutput, calls=%fused_computation.322 | convolution fusion | flops 8388608000 | bytes 26296320 | tf_op jit(solution)/shard_map/dot_general | solution.py:48
  812.5 5.6 collective-permute-done.70
  838.8 3.2 collective-permute-done.63
  846.9 3.4 fusion.16
  850.3 2.9 collective-permute-done.80
  855.4 15.2 %collective-permute-done.83 = bf16[400,1280]{1,0:T(8,128)(2,1)} collective-permute-done((bf16[400,1280]{1,0:T(8,128)(2,1)}, bf16[400,1280]{1,0:T(8,128)(2,1)}, u32[]{:S(2)}, u32[]{:S(2)}) %collective-permute-start.83) | collective-permute-done | bytes 1024032 | tf_op jit(solution)/shard_map/ppermute | solution.py:32
  871.2 10.9 %collective-permute-done.79 = bf16[400,1280]{1,0:T(8,128)(2,1)} collective-permute-done((bf16[400,1280]{1,0:T(8,128)(2,1)S(1)}, bf16[400,1280]{1,0:T(8,128)(2,1)}, u32[]{:S(2)}, u32[]{:S(2)}) %collective-permute-start.79) | collective-permute-done | bytes 1024032 | tf_op jit(solution)/shard_map/ppermute | solution.py:512
  884.4 56.2 %collective-permute-done.82 = bf16[400,1280]{1,0:T(8,128)(2,1)} collective-permute-done((bf16[400,1280]{1,0:T(8,128)(2,1)S(1)}, bf16[400,1280]{1,0:T(8,128)(2,1)}, u32[]{:S(2)}, u32[]{:S(2)}) %collective-permute-start.82) | collective-permute-done | bytes 1024032 | tf_op jit(solution)/shard_map/ppermute | solution.py:512
  942.7 24.6 %collective-permute-done.78 = bf16[400,1280]{1,0:T(8,128)(2,1)} collective-permute-done((bf16[400,1280]{1,0:T(8,128)(2,1)}, bf16[400,1280]{1,0:T(8,128)(2,1)}, u32[]{:S(2)}, u32[]{:S(2)}) %collective-permute-start.78) | collective-permute-done | bytes 1024032 | tf_op jit(solution)/shard_map/ppermute | solution.py:512
  967.3 2.8 maximum_select_fusion.10
  970.1 29.3 %collective-permute-done.81 = bf16[400,1280]{1,0:T(8,128)(2,1)S(1)} collective-permute-done((bf16[400,1280]{1,0:T(8,128)(2,1)}, bf16[400,1280]{1,0:T(8,128)(2,1)S(1)}, u32[]{:S(2)}, u32[]{:S(2)}) %collective-permute-start.81) | collective-permute-done | bytes 1024032 | tf_op jit(solution)/shard_map/ppermute | solution.py:512
  1001.5 62.1 %collective-permute-done.84 = bf16[400,1280]{1,0:T(8,128)(2,1)S(1)} collective-permute-done((bf16[400,1280]{1,0:T(8,128)(2,1)}, bf16[400,1280]{1,0:T(8,128)(2,1)S(1)}, u32[]{:S(2)}, u32[]{:S(2)}) %collective-permute-start.84) | collective-permute-done | bytes 1024032 | tf_op jit(solution)/shard_map/ppermute | solution.py:512
  1065.8 3.7 convert_bitcast_fusion.1
  1069.6 3.7 convert_bitcast_fusion
  1073.3 3.7 fusion.7
  (575 shorter events, 252.1 us)
Async XLA Ops:
  7.2 488.1 %all-gather.3.cloned.1.call-start = ((), (), s32[]{:S(2)}) async-start(), calls=%async_computation | async-start | bytes 21626880 | tf_op jit(solution)/shard_map/all_gather | solution.py:406
  9.2 23.4 %collective-permute-start = (bf16[128,1280]{1,0:T(8,128)(2,1)}, bf16[128,1280]{1,0:T(8,128)(2,1)S(1)}, u32[]{:S(2)}, u32[]{:S(2)}) collective-permute-start(bf16[128,1280]{1,0:T(8,128)(2,1)} %get-tuple-element.145), channel_id=1, source_target_pairs={{0,4},{4,0},{1,5},{5,1},{2,6},{6,2},{3,7},{7,3},{8,12},{12,8},{9,1... | collective-permute-start | bytes 983048 | tf_op jit(solution)/shard_map/ppermute | solution.py:32
  14.2 16.8 %collective-permute-start.3 = (bf16[264,1280]{1,0:T(8,128)(2,1)}, bf16[264,1280]{1,0:T(8,128)(2,1)S(1)}, u32[]{:S(2)}, u32[]{:S(2)}) collective-permute-start(bf16[264,1280]{1,0:T(8,128)(2,1)} %pad_maximum_fusion.8), channel_id=1, source_target_pairs={{0,2},{1,3},{2,0},{3,1},{4,6},{5,7},{6,4},{7,5},{8,10},{9,11},{10,... | collective-permute-start | bytes 2027528 | tf_op jit(solution)/shard_map/ppermute | solution.py:40
  41.0 13.8 %collective-permute-start.5 = (f32[128,1056]{0,1:T(8,128)}, f32[128,1056]{0,1:T(8,128)}, u32[]{:S(2)}, u32[]{:S(2)}) collective-permute-start(f32[128,1056]{0,1:T(8,128)} %get-tuple-element.125), channel_id=1, source_target_pairs={{0,4},{4,0},{1,5},{5,1},{2,6},{6,2},{3,7},{7,3},{8,12},{12,8},{9,1... | collective-permute-start | bytes 1622024 | tf_op jit(solution)/shard_map/ppermute | solution.py:32
  61.3 8.7 collective-permute-start.7
  77.3 12.6 %collective-permute-start.10 = (bf16[512,1056]{0,1:T(8,128)(2,1)}, bf16[512,1056]{0,1:T(8,128)(2,1)}, u32[]{:S(2)}, u32[]{:S(2)}) collective-permute-start(bf16[512,1056]{0,1:T(8,128)(2,1)} %copy.49), channel_id=1, source_target_pairs={{0,1},{1,0},{2,3},{3,2},{4,5},{5,4},{6,7},{7,6},{8,9},{9,8},{10,11... | collective-permute-start | bytes 3244040 | tf_op jit(solution)/shard_map/ppermute | solution.py:36
  78.5 10.2 collective-permute-start.1
  92.7 597.4 %all-gather.5.cloned.1.call-start = ((), (), s32[]{:S(2)}) async-start(), calls=%async_computation.1 | async-start | bytes 21626880 | tf_op jit(solution)/shard_map/all_gather | solution.py:422
  95.1 13.4 %collective-permute-start.11 = (bf16[384,480]{0,1:T(8,128)(2,1)}, bf16[384,480]{0,1:T(8,128)(2,1)}, u32[]{:S(2)}, u32[]{:S(2)}) collective-permute-start(bf16[384,480]{0,1:T(8,128)(2,1)} %get-tuple-element.130), channel_id=1, source_target_pairs={{0,4},{4,0},{1,5},{5,1},{2,6},{6,2},{3,7},{7,3},{8,12},{12,8},{9,1... | collective-permute-start | bytes 1105928 | tf_op jit(solution)/shard_map/ppermute | solution.py:32
  99.0 37.6 %collective-permute-start.12 = (bf16[320,1280]{1,0:T(8,128)(2,1)}, bf16[320,1280]{1,0:T(8,128)(2,1)}, u32[]{:S(2)}, u32[]{:S(2)}) collective-permute-start(bf16[320,1280]{1,0:T(8,128)(2,1)} %get-tuple-element.115), channel_id=1, source_target_pairs={{0,4},{4,0},{1,5},{5,1},{2,6},{6,2},{3,7},{7,3},{8,12},{12,8},{9,1... | collective-permute-start | bytes 2457608 | tf_op jit(solution)/shard_map/ppermute | solution.py:32
  147.8 9.8 collective-permute-start.14
  148.6 10.2 collective-permute-start.16
  159.0 27.2 %collective-permute-start.17 = (bf16[128,2560]{1,0:T(8,128)(2,1)S(1)}, bf16[128,2560]{1,0:T(8,128)(2,1)S(1)}, u32[]{:S(2)}, u32[]{:S(2)}) collective-permute-start(bf16[128,2560]{1,0:T(8,128)(2,1)S(1)} %pad_maximum_fusion.10), channel_id=1, source_target_pairs={{0,2},{1,3},{2,0},{3,1},{4,6},{5,7},{6,4},{7,5},{8,10},{9,11},{10,... | collective-permute-start | bytes 1966088 | tf_op jit(solution)/shard_map/ppermute | solution.py:40
  160.2 26.0 %collective-permute-start.15 = (bf16[128,2560]{1,0:T(8,128)(2,1)S(1)}, bf16[128,2560]{1,0:T(8,128)(2,1)S(1)}, u32[]{:S(2)}, u32[]{:S(2)}) collective-permute-start(bf16[128,2560]{1,0:T(8,128)(2,1)S(1)} %pad_maximum_fusion.9), channel_id=1, source_target_pairs={{0,4},{4,0},{1,5},{5,1},{2,6},{6,2},{3,7},{7,3},{8,12},{12,8},{9,1... | collective-permute-start | bytes 1966088 | tf_op jit(solution)/shard_map/ppermute | solution.py:32
  162.0 24.1 %collective-permute-start.29 = (bf16[1280]{0:T(1024)(128)(2,1)S(1)}, bf16[1280]{0:T(1024)(128)(2,1)S(1)}, u32[]{:S(2)}, u32[]{:S(2)}) collective-permute-start(bf16[1280]{0:T(1024)(128)(2,1)S(1)} %copy-done.89), channel_id=1, source_target_pairs={{0,4},{4,0},{1,5},{5,1},{2,6},{6,2},{3,7},{7,3},{8,12},{12,8},{9,1... | collective-permute-start | bytes 7688 | tf_op jit(solution)/shard_map/ppermute | solution.py:32
  189.1 887.9 %all-reduce.9.cloned.1.call-start = ((), (), s32[]{:S(2)}) async-start(), calls=%async_computation.2 | async-start | bytes 7413760 | tf_op jit(solution)/shard_map/psum | solution.py:546
  192.2 108.7 %collective-permute-start.27 = (bf16[400,1280]{1,0:T(8,128)(2,1)}, bf16[400,1280]{1,0:T(8,128)(2,1)}, u32[]{:S(2)}, u32[]{:S(2)}) collective-permute-start(bf16[400,1280]{1,0:T(8,128)(2,1)} %dynamic-slice_bitcast_fusion.2), channel_id=1, source_target_pairs={{0,4},{4,0},{1,5},{5,1},{2,6},{6,2},{3,7},{7,3},{8,12},{12,8},{9,1... | collective-permute-start | bytes 3072008 | tf_op jit(solution)/shard_map/ppermute | solution.py:32
  197.1 105.5 %collective-permute-start.25 = (bf16[400,1280]{1,0:T(8,128)(2,1)}, bf16[400,1280]{1,0:T(8,128)(2,1)}, u32[]{:S(2)}, u32[]{:S(2)}) collective-permute-start(bf16[400,1280]{1,0:T(8,128)(2,1)} %dynamic-slice_bitcast_fusion.3), channel_id=1, source_target_pairs={{0,4},{4,0},{1,5},{5,1},{2,6},{6,2},{3,7},{7,3},{8,12},{12,8},{9,1... | collective-permute-start | bytes 3072008 | tf_op jit(solution)/shard_map/ppermute | solution.py:32
  199.5 103.4 %collective-permute-start.18 = (bf16[400,1280]{1,0:T(8,128)(2,1)}, bf16[400,1280]{1,0:T(8,128)(2,1)}, u32[]{:S(2)}, u32[]{:S(2)}) collective-permute-start(bf16[400,1280]{1,0:T(8,128)(2,1)} %constant_dynamic-slice_fusion.15), channel_id=1, source_target_pairs={{0,4},{4,0},{1,5},{5,1},{2,6},{6,2},{3,7},{7,3},{8,12},{12,8},{9,1... | collective-permute-start | bytes 3072008 | tf_op jit(solution)/shard_map/ppermute | solution.py:32
  205.4 92.7 %collective-permute-start.20 = (bf16[128,2560]{1,0:T(8,128)(2,1)S(1)}, bf16[128,2560]{1,0:T(8,128)(2,1)S(1)}, u32[]{:S(2)}, u32[]{:S(2)}) collective-permute-start(bf16[128,2560]{1,0:T(8,128)(2,1)S(1)} %copy-done.16), channel_id=1, source_target_pairs={{0,4},{4,0},{1,5},{5,1},{2,6},{6,2},{3,7},{7,3},{8,12},{12,8},{9,1... | collective-permute-start | bytes 1966088 | tf_op jit(solution)/shard_map/ppermute | solution.py:32
  205.4 93.7 %collective-permute-start.21 = (bf16[128,2560]{1,0:T(8,128)(2,1)S(1)}, bf16[128,2560]{1,0:T(8,128)(2,1)S(1)}, u32[]{:S(2)}, u32[]{:S(2)}) collective-permute-start(bf16[128,2560]{1,0:T(8,128)(2,1)S(1)} %copy-done.16), channel_id=1, source_target_pairs={{0,2},{1,3},{2,0},{3,1},{4,6},{5,7},{6,4},{7,5},{8,10},{9,11},{10,... | collective-permute-start | bytes 1966088 | tf_op jit(solution)/shard_map/ppermute | solution.py:40
  298.1 15.4 %collective-permute-start.22 = (bf16[64,2560]{1,0:T(8,128)(2,1)S(1)}, bf16[64,2560]{1,0:T(8,128)(2,1)S(1)}, u32[]{:S(2)}, u32[]{:S(2)}) collective-permute-start(bf16[64,2560]{1,0:T(8,128)(2,1)S(1)} %slice.448), channel_id=1, source_target_pairs={{0,2},{1,3},{2,0},{3,1},{4,6},{5,7},{6,4},{7,5},{8,10},{9,11},{10,... | collective-permute-start | bytes 983048 | tf_op jit(solution)/shard_map/ppermute | solution.py:40
  299.1 17.5 %collective-permute-start.23 = (bf16[64,2560]{1,0:T(8,128)(2,1)S(1)}, bf16[64,2560]{1,0:T(8,128)(2,1)S(1)}, u32[]{:S(2)}, u32[]{:S(2)}) collective-permute-start(bf16[64,2560]{1,0:T(8,128)(2,1)S(1)} %slice.449), channel_id=1, source_target_pairs={{0,4},{4,0},{1,5},{5,1},{2,6},{6,2},{3,7},{7,3},{8,12},{12,8},{9,1... | collective-permute-start | bytes 983048 | tf_op jit(solution)/shard_map/ppermute | solution.py:32
  300.8 61.0 %collective-permute-start.28 = (bf16[400,1280]{1,0:T(8,128)(2,1)}, bf16[400,1280]{1,0:T(8,128)(2,1)S(1)}, u32[]{:S(2)}, u32[]{:S(2)}) collective-permute-start(bf16[400,1280]{1,0:T(8,128)(2,1)} %collective-permute-done.27), channel_id=1, source_target_pairs={{0,8},{8,0},{16,24},{24,16},{1,9},{9,1},{17,25},{25,17},{2,10},{10... | collective-permute-start | bytes 3072008 | tf_op jit(solution)/shard_map/ppermute | solution.py:96
  302.6 92.2 %collective-permute-start.26 = (bf16[400,1280]{1,0:T(8,128)(2,1)}, bf16[400,1280]{1,0:T(8,128)(2,1)S(1)}, u32[]{:S(2)}, u32[]{:S(2)}) collective-permute-start(bf16[400,1280]{1,0:T(8,128)(2,1)} %collective-permute-done.25), channel_id=1, source_target_pairs={{0,8},{8,0},{16,24},{24,16},{1,9},{9,1},{17,25},{25,17},{2,10},{10... | collective-permute-start | bytes 3072008 | tf_op jit(solution)/shard_map/ppermute | solution.py:96
  302.9 147.4 %collective-permute-start.19 = (bf16[400,1280]{1,0:T(8,128)(2,1)}, bf16[400,1280]{1,0:T(8,128)(2,1)S(1)}, u32[]{:S(2)}, u32[]{:S(2)}) collective-permute-start(bf16[400,1280]{1,0:T(8,128)(2,1)} %collective-permute-done.18), channel_id=1, source_target_pairs={{0,8},{8,0},{16,24},{24,16},{1,9},{9,1},{17,25},{25,17},{2,10},{10... | collective-permute-start | bytes 3072008 | tf_op jit(solution)/shard_map/ppermute | solution.py:96
  313.6 25.5 %collective-permute-start.30 = (bf16[128,2560]{1,0:T(8,128)(2,1)S(1)}, bf16[128,2560]{1,0:T(8,128)(2,1)S(1)}, u32[]{:S(2)}, u32[]{:S(2)}) collective-permute-start(bf16[128,2560]{1,0:T(8,128)(2,1)S(1)} %copy-done.17), channel_id=1, source_target_pairs={{0,4},{4,0},{1,5},{5,1},{2,6},{6,2},{3,7},{7,3},{8,12},{12,8},{9,1... | collective-permute-start | bytes 1966088 | tf_op jit(solution)/shard_map/ppermute | solution.py:32
  316.7 22.4 %collective-permute-start.31 = (bf16[128,2560]{1,0:T(8,128)(2,1)S(1)}, bf16[128,2560]{1,0:T(8,128)(2,1)S(1)}, u32[]{:S(2)}, u32[]{:S(2)}) collective-permute-start(bf16[128,2560]{1,0:T(8,128)(2,1)S(1)} %copy-done.17), channel_id=1, source_target_pairs={{0,2},{1,3},{2,0},{3,1},{4,6},{5,7},{6,4},{7,5},{8,10},{9,11},{10,... | collective-permute-start | bytes 1966088 | tf_op jit(solution)/shard_map/ppermute | solution.py:40
  339.1 118.7 %collective-permute-start.24 = (bf16[512,2560]{1,0:T(8,128)(2,1)S(1)}, bf16[512,2560]{1,0:T(8,128)(2,1)S(1)}, u32[]{:S(2)}, u32[]{:S(2)}) collective-permute-start(bf16[512,2560]{1,0:T(8,128)(2,1)S(1)} %get-tuple-element.169), channel_id=1, source_target_pairs={{0,1},{1,0},{2,3},{3,2},{4,5},{5,4},{6,7},{7,6},{8,9},{9,8},{10,11... | collective-permute-start | bytes 7864328 | tf_op jit(solution)/shard_map/ppermute | solution.py:36
  339.1 10.2 collective-permute-start.32
  349.3 9.4 collective-permute-start.33
  359.5 99.9 %collective-permute-start.34 = (bf16[512,2560]{1,0:T(8,128)(2,1)}, bf16[512,2560]{1,0:T(8,128)(2,1)S(1)}, u32[]{:S(2)}, u32[]{:S(2)}) collective-permute-start(bf16[512,2560]{1,0:T(8,128)(2,1)} %get-tuple-element.165), channel_id=1, source_target_pairs={{0,1},{1,0},{2,3},{3,2},{4,5},{5,4},{6,7},{7,6},{8,9},{9,8},{10,11... | collective-permute-start | bytes 7864328 | tf_op jit(solution)/shard_map/ppermute | solution.py:36
  503.2 13.1 %collective-permute-start.36 = (bf16[64,2560]{1,0:T(8,128)(2,1)S(1)}, bf16[64,2560]{1,0:T(8,128)(2,1)S(1)}, u32[]{:S(2)}, u32[]{:S(2)}) collective-permute-start(bf16[64,2560]{1,0:T(8,128)(2,1)S(1)} %get-tuple-element.93), channel_id=1, source_target_pairs={{0,2},{1,3},{2,0},{3,1},{4,6},{5,7},{6,4},{7,5},{8,10},{9,11},{10,... | collective-permute-start | bytes 983048 | tf_op jit(solution)/shard_map/ppermute | solution.py:40
  504.8 11.5 %collective-permute-start.38 = (bf16[64,2560]{1,0:T(8,128)(2,1)S(1)}, bf16[64,2560]{1,0:T(8,128)(2,1)S(1)}, u32[]{:S(2)}, u32[]{:S(2)}) collective-permute-start(bf16[64,2560]{1,0:T(8,128)(2,1)S(1)} %get-tuple-element.92), channel_id=1, source_target_pairs={{0,4},{4,0},{1,5},{5,1},{2,6},{6,2},{3,7},{7,3},{8,12},{12,8},{9,1... | collective-permute-start | bytes 983048 | tf_op jit(solution)/shard_map/ppermute | solution.py:32
  517.3 18.6 %collective-permute-start.39 = (bf16[128,2560]{1,0:T(8,128)(2,1)}, bf16[128,2560]{1,0:T(8,128)(2,1)}, u32[]{:S(2)}, u32[]{:S(2)}) collective-permute-start(bf16[128,2560]{1,0:T(8,128)(2,1)} %pad_maximum_fusion.12), channel_id=1, source_target_pairs={{0,2},{1,3},{2,0},{3,1},{4,6},{5,7},{6,4},{7,5},{8,10},{9,11},{10,... | collective-permute-start | bytes 1966088 | tf_op jit(solution)/shard_map/ppermute | solution.py:40
  519.5 16.8 %collective-permute-start.37 = (bf16[128,2560]{1,0:T(8,128)(2,1)}, bf16[128,2560]{1,0:T(8,128)(2,1)}, u32[]{:S(2)}, u32[]{:S(2)}) collective-permute-start(bf16[128,2560]{1,0:T(8,128)(2,1)} %pad_maximum_fusion.11), channel_id=1, source_target_pairs={{0,4},{4,0},{1,5},{5,1},{2,6},{6,2},{3,7},{7,3},{8,12},{12,8},{9,1... | collective-permute-start | bytes 1966088 | tf_op jit(solution)/shard_map/ppermute | solution.py:32
  547.4 9.8 collective-permute-start.41
  548.0 9.5 collective-permute-start.43
  557.7 15.7 %collective-permute-start.44 = (bf16[128,2560]{1,0:T(8,128)(2,1)S(1)}, bf16[128,2560]{1,0:T(8,128)(2,1)S(1)}, u32[]{:S(2)}, u32[]{:S(2)}) collective-permute-start(bf16[128,2560]{1,0:T(8,128)(2,1)S(1)} %pad_maximum_fusion.14), channel_id=1, source_target_pairs={{0,2},{1,3},{2,0},{3,1},{4,6},{5,7},{6,4},{7,5},{8,10},{9,11},{10,... | collective-permute-start | bytes 1966088 | tf_op jit(solution)/shard_map/ppermute | solution.py:40
  559.3 15.4 %collective-permute-start.42 = (bf16[128,2560]{1,0:T(8,128)(2,1)S(1)}, bf16[128,2560]{1,0:T(8,128)(2,1)S(1)}, u32[]{:S(2)}, u32[]{:S(2)}) collective-permute-start(bf16[128,2560]{1,0:T(8,128)(2,1)S(1)} %pad_maximum_fusion.13), channel_id=1, source_target_pairs={{0,4},{4,0},{1,5},{5,1},{2,6},{6,2},{3,7},{7,3},{8,12},{12,8},{9,1... | collective-permute-start | bytes 1966088 | tf_op jit(solution)/shard_map/ppermute | solution.py:32
  578.2 14.4 %collective-permute-start.47 = (bf16[128,2560]{1,0:T(8,128)(2,1)S(1)}, bf16[128,2560]{1,0:T(8,128)(2,1)S(1)}, u32[]{:S(2)}, u32[]{:S(2)}) collective-permute-start(bf16[128,2560]{1,0:T(8,128)(2,1)S(1)} %get-tuple-element.71), channel_id=1, source_target_pairs={{0,4},{4,0},{1,5},{5,1},{2,6},{6,2},{3,7},{7,3},{8,12},{12,8},{9,1... | collective-permute-start | bytes 1966088 | tf_op jit(solution)/shard_map/ppermute | solution.py:32
  579.1 15.2 %collective-permute-start.48 = (bf16[128,2560]{1,0:T(8,128)(2,1)S(1)}, bf16[128,2560]{1,0:T(8,128)(2,1)S(1)}, u32[]{:S(2)}, u32[]{:S(2)}) collective-permute-start(bf16[128,2560]{1,0:T(8,128)(2,1)S(1)} %get-tuple-element.71), channel_id=1, source_target_pairs={{0,2},{1,3},{2,0},{3,1},{4,6},{5,7},{6,4},{7,5},{8,10},{9,11},{10,... | collective-permute-start | bytes 1966088 | tf_op jit(solution)/shard_map/ppermute | solution.py:40
  604.6 40.1 %collective-permute-start.51 = (bf16[512,2560]{1,0:T(8,128)(2,1)}, bf16[512,2560]{1,0:T(8,128)(2,1)}, u32[]{:S(2)}, u32[]{:S(2)}) collective-permute-start(bf16[512,2560]{1,0:T(8,128)(2,1)} %get-tuple-element.161), channel_id=1, source_target_pairs={{0,1},{1,0},{2,3},{3,2},{4,5},{5,4},{6,7},{7,6},{8,9},{9,8},{10,11... | collective-permute-start | bytes 7864328 | tf_op jit(solution)/shard_map/ppermute | solution.py:36
  604.6 17.5 %collective-permute-start.66 = (bf16[256,1280]{1,0:T(8,128)(2,1)}, bf16[256,1280]{1,0:T(8,128)(2,1)}, u32[]{:S(2)}, u32[]{:S(2)}) collective-permute-start(bf16[256,1280]{1,0:T(8,128)(2,1)} %multiply_convert_fusion.9), channel_id=1, source_target_pairs={{0,2},{1,3},{2,0},{3,1},{4,6},{5,7},{6,4},{7,5},{8,10},{9,11},{10,... | collective-permute-start | bytes 1966088 | tf_op jit(solution)/shard_map/ppermute | solution.py:40
  624.5 204.6 %collective-permute-start.67 = (bf16[512,1280]{1,0:T(8,128)(2,1)}, bf16[512,1280]{1,0:T(8,128)(2,1)}, u32[]{:S(2)}, u32[]{:S(2)}) collective-permute-start(bf16[512,1280]{1,0:T(8,128)(2,1)} %pad_maximum_fusion.7), channel_id=1, source_target_pairs={{0,1},{1,0},{2,3},{3,2},{4,5},{5,4},{6,7},{7,6},{8,9},{9,8},{10,11... | collective-permute-start | bytes 3932168 | tf_op jit(solution)/shard_map/ppermute | solution.py:36
  625.6 18.1 %collective-permute-start.45 = (bf16[128,1280]{1,0:T(8,128)(2,1)S(1)}, bf16[128,1280]{1,0:T(8,128)(2,1)S(1)}, u32[]{:S(2)}, u32[]{:S(2)}) collective-permute-start(bf16[128,1280]{1,0:T(8,128)(2,1)S(1)} %get-tuple-element.136), channel_id=1, source_target_pairs={{0,4},{4,0},{1,5},{5,1},{2,6},{6,2},{3,7},{7,3},{8,12},{12,8},{9,1... | collective-permute-start | bytes 983048 | tf_op jit(solution)/shard_map/ppermute | solution.py:32
  628.0 14.8 %collective-permute-start.46 = (bf16[128,1280]{1,0:T(8,128)(2,1)S(1)}, bf16[128,1280]{1,0:T(8,128)(2,1)S(1)}, u32[]{:S(2)}, u32[]{:S(2)}) collective-permute-start(bf16[128,1280]{1,0:T(8,128)(2,1)S(1)} %dynamic-slice_convert_fusion), channel_id=1, source_target_pairs={{0,4},{4,0},{1,5},{5,1},{2,6},{6,2},{3,7},{7,3},{8,12},{12,8},{9,1... | collective-permute-start | bytes 983048 | tf_op jit(solution)/shard_map/ppermute | solution.py:32
  693.5 29.0 %collective-permute-start.52 = (bf16[512,1056]{0,1:T(8,128)(2,1)}, bf16[512,1056]{0,1:T(8,128)(2,1)}, u32[]{:S(2)}, u32[]{:S(2)}) collective-permute-start(bf16[512,1056]{0,1:T(8,128)(2,1)} %copy.59), channel_id=1, source_target_pairs={{0,1},{1,0},{2,3},{3,2},{4,5},{5,4},{6,7},{7,6},{8,9},{9,8},{10,11... | collective-permute-start | bytes 3244040 | tf_op jit(solution)/shard_map/ppermute | solution.py:36
  695.7 35.5 %collective-permute-start.73 = (bf16[384,480]{0,1:T(8,128)(2,1)}, bf16[384,480]{0,1:T(8,128)(2,1)}, u32[]{:S(2)}, u32[]{:S(2)}) collective-permute-start(bf16[384,480]{0,1:T(8,128)(2,1)} %get-tuple-element.128), channel_id=1, source_target_pairs={{0,4},{4,0},{1,5},{5,1},{2,6},{6,2},{3,7},{7,3},{8,12},{12,8},{9,1... | collective-permute-start | bytes 1105928 | tf_op jit(solution)/shard_map/ppermute | solution.py:32
  697.0 30.2 %collective-permute-start.74 = (bf16[256,640]{1,0:T(8,128)(2,1)}, bf16[256,640]{1,0:T(8,128)(2,1)}, u32[]{:S(2)}, u32[]{:S(2)}) collective-permute-start(bf16[256,640]{1,0:T(8,128)(2,1)} %fusion.61), channel_id=1, source_target_pairs={{0,4},{4,0},{1,5},{5,1},{2,6},{6,2},{3,7},{7,3},{8,12},{12,8},{9,1... | collective-permute-start | bytes 983048 | tf_op jit(solution)/shard_map/ppermute | solution.py:32
  699.0 37.4 %collective-permute-start.75 = (bf16[320,1280]{1,0:T(8,128)(2,1)}, bf16[320,1280]{1,0:T(8,128)(2,1)}, u32[]{:S(2)}, u32[]{:S(2)}) collective-permute-start(bf16[320,1280]{1,0:T(8,128)(2,1)} %get-tuple-element.111), channel_id=1, source_target_pairs={{0,4},{4,0},{1,5},{5,1},{2,6},{6,2},{3,7},{7,3},{8,12},{12,8},{9,1... | collective-permute-start | bytes 2457608 | tf_op jit(solution)/shard_map/ppermute | solution.py:32
  734.6 8.5 collective-permute-start.56
  788.7 9.2 collective-permute-start.57
  790.8 52.2 %collective-permute-start.77 = (bf16[400,1280]{1,0:T(8,128)(2,1)S(1)}, bf16[400,1280]{1,0:T(8,128)(2,1)}, u32[]{:S(2)}, u32[]{:S(2)}) collective-permute-start(bf16[400,1280]{1,0:T(8,128)(2,1)S(1)} %get-tuple-element.107), channel_id=1, source_target_pairs={{0,4},{4,0},{1,5},{5,1},{2,6},{6,2},{3,7},{7,3},{8,12},{12,8},{9,1... | collective-permute-start | bytes 3072008 | tf_op jit(solution)/shard_map/ppermute | solution.py:32
  791.8 54.1 %collective-permute-start.76 = (bf16[400,1280]{1,0:T(8,128)(2,1)S(1)}, bf16[400,1280]{1,0:T(8,128)(2,1)S(1)}, u32[]{:S(2)}, u32[]{:S(2)}) collective-permute-start(bf16[400,1280]{1,0:T(8,128)(2,1)S(1)} %get-tuple-element.106), channel_id=1, source_target_pairs={{0,8},{8,0},{16,24},{24,16},{1,9},{9,1},{17,25},{25,17},{2,10},{10... | collective-permute-start | bytes 3072008 | tf_op jit(solution)/shard_map/ppermute | solution.py:512
  795.6 22.5 %collective-permute-start.70 = (f32[28,128]{1,0:T(8,128)S(1)}, f32[28,128]{1,0:T(8,128)S(1)}, u32[]{:S(2)}, u32[]{:S(2)}) collective-permute-start(f32[28,128]{1,0:T(8,128)S(1)} %fusion.102), channel_id=1, source_target_pairs={{0,4},{4,0},{1,5},{5,1},{2,6},{6,2},{3,7},{7,3},{8,12},{12,8},{9,1... | collective-permute-start | bytes 43016 | tf_op jit(solution)/shard_map/ppermute | solution.py:32
  800.3 17.9 %collective-permute-start.59 = (f32[10,128]{1,0:T(8,128)S(1)}, f32[10,128]{1,0:T(8,128)S(1)}, u32[]{:S(2)}, u32[]{:S(2)}) collective-permute-start(f32[10,128]{1,0:T(8,128)S(1)} %bitcast.92), channel_id=1, source_target_pairs={{0,1},{1,0},{2,3},{3,2},{4,5},{5,4},{6,7},{7,6},{8,9},{9,8},{10,11... | collective-permute-start | bytes 15368 | tf_op jit(solution)/shard_map/ppermute | solution.py:36
  827.4 25.9 %collective-permute-start.80 = (bf16[400,1280]{1,0:T(8,128)(2,1)}, bf16[400,1280]{1,0:T(8,128)(2,1)}, u32[]{:S(2)}, u32[]{:S(2)}) collective-permute-start(bf16[400,1280]{1,0:T(8,128)(2,1)} %get-tuple-element.105), channel_id=1, source_target_pairs={{0,4},{4,0},{1,5},{5,1},{2,6},{6,2},{3,7},{7,3},{8,12},{12,8},{9,1... | collective-permute-start | bytes 3072008 | tf_op jit(solution)/shard_map/ppermute | solution.py:32
  837.4 44.7 %collective-permute-start.79 = (bf16[400,1280]{1,0:T(8,128)(2,1)S(1)}, bf16[400,1280]{1,0:T(8,128)(2,1)}, u32[]{:S(2)}, u32[]{:S(2)}) collective-permute-start(bf16[400,1280]{1,0:T(8,128)(2,1)S(1)} %get-tuple-element.104), channel_id=1, source_target_pairs={{0,8},{8,0},{16,24},{24,16},{1,9},{9,1},{17,25},{25,17},{2,10},{10... | collective-permute-start | bytes 3072008 | tf_op jit(solution)/shard_map/ppermute | solution.py:512
  842.0 28.6 %collective-permute-start.83 = (bf16[400,1280]{1,0:T(8,128)(2,1)}, bf16[400,1280]{1,0:T(8,128)(2,1)}, u32[]{:S(2)}, u32[]{:S(2)}) collective-permute-start(bf16[400,1280]{1,0:T(8,128)(2,1)} %get-tuple-element.103), channel_id=1, source_target_pairs={{0,4},{4,0},{1,5},{5,1},{2,6},{6,2},{3,7},{7,3},{8,12},{12,8},{9,1... | collective-permute-start | bytes 3072008 | tf_op jit(solution)/shard_map/ppermute | solution.py:32
  843.0 97.5 %collective-permute-start.82 = (bf16[400,1280]{1,0:T(8,128)(2,1)S(1)}, bf16[400,1280]{1,0:T(8,128)(2,1)}, u32[]{:S(2)}, u32[]{:S(2)}) collective-permute-start(bf16[400,1280]{1,0:T(8,128)(2,1)S(1)} %get-tuple-element.102), channel_id=1, source_target_pairs={{0,8},{8,0},{16,24},{24,16},{1,9},{9,1},{17,25},{25,17},{2,10},{10... | collective-permute-start | bytes 3072008 | tf_op jit(solution)/shard_map/ppermute | solution.py:512
  846.9 120.4 %collective-permute-start.78 = (bf16[400,1280]{1,0:T(8,128)(2,1)}, bf16[400,1280]{1,0:T(8,128)(2,1)}, u32[]{:S(2)}, u32[]{:S(2)}) collective-permute-start(bf16[400,1280]{1,0:T(8,128)(2,1)} %collective-permute-done.77), channel_id=1, source_target_pairs={{0,8},{8,0},{16,24},{24,16},{1,9},{9,1},{17,25},{25,17},{2,10},{10... | collective-permute-start | bytes 3072008 | tf_op jit(solution)/shard_map/ppermute | solution.py:512
  853.2 146.2 %collective-permute-start.81 = (bf16[400,1280]{1,0:T(8,128)(2,1)}, bf16[400,1280]{1,0:T(8,128)(2,1)S(1)}, u32[]{:S(2)}, u32[]{:S(2)}) collective-permute-start(bf16[400,1280]{1,0:T(8,128)(2,1)} %collective-permute-done.80), channel_id=1, source_target_pairs={{0,8},{8,0},{16,24},{24,16},{1,9},{9,1},{17,25},{25,17},{2,10},{10... | collective-permute-start | bytes 3072008 | tf_op jit(solution)/shard_map/ppermute | solution.py:512
  870.6 193.0 %collective-permute-start.84 = (bf16[400,1280]{1,0:T(8,128)(2,1)}, bf16[400,1280]{1,0:T(8,128)(2,1)S(1)}, u32[]{:S(2)}, u32[]{:S(2)}) collective-permute-start(bf16[400,1280]{1,0:T(8,128)(2,1)} %collective-permute-done.83), channel_id=1, source_target_pairs={{0,8},{8,0},{16,24},{24,16},{1,9},{9,1},{17,25},{25,17},{2,10},{10... | collective-permute-start | bytes 3072008 | tf_op jit(solution)/shard_map/ppermute | solution.py:512
  (127 other events, 1431.3 us)
Sparse Core Ops, SparseCore 0:
  92.8 167.8 all-gather.2
  264.2 187.9 all-gather.4
  850.4 219.9 all-reduce.8

commit v2 on v1

--- a/solution.py
+++ b/solution.py
@@ -52,10 +52,6 @@
     return lax.dynamic_slice_in_dim(values, start, length, 0)
 
 
-def put(target, piece, row, column):
-    return lax.dynamic_update_slice(target, piece, (row, column))
-
-
 def pair(first_is_own, own, other, axis):
     return jnp.where(
         first_is_own,
@@ -64,21 +60,42 @@
     )
 
 
+def together(*values):
+    return lax.optimization_barrier(values)
+
+
+def gather_near(own):
+    return own, px(own), py(own)
+
+
+def gather_far(own, from_x, from_y):
+    half = own.shape[0] // 2
+    return [own, from_x, from_y, py(from_x[:half]), px(from_y[half:])]
+
+
+def gather_core(pieces):
+    same_core = jnp.concatenate(pieces, 0)
+    return jnp.concatenate([same_core, pc(same_core)], 0)
+
+
 def gather_plane(own):
-    half = own.shape[0] // 2
-    from_x, from_y = px(own), py(own)
-    far = [py(from_x[:half]), px(from_y[half:])]
-    same_core = jnp.concatenate([own, from_x, from_y] + far, 0)
-    return jnp.concatenate([same_core, pc(same_core)], 0)
-
-
-def scatter_plane(partial):
-    rows = partial.shape[0] // 8
+    return gather_core(gather_far(*gather_near(own)))
+
+
+def scatter_core(partial):
+    half = partial.shape[0] // 2
+    return (partial[:half].astype(F32) + pc(partial[half:]).astype(F32)).astype(BF16)
+
+
+def scatter_far(total):
+    rows = total.shape[0] // 4
     half = rows // 2
-    other = pc(partial[4 * rows :])
-    total = (partial[: 4 * rows].astype(F32) + other.astype(F32)).astype(BF16)
     own, to_x, to_y, far = (total[i * rows : (i + 1) * rows] for i in range(4))
-    for_y, for_x = px(far[:half]), py(far[half:])
+    return own, to_x, to_y, px(far[:half]), py(far[half:])
+
+
+def scatter_near(own, to_x, to_y, for_y, for_x):
+    half = for_y.shape[0]
     y_top = (to_y[:half].astype(F32) + for_y.astype(F32)).astype(BF16)
     x_low = (to_x[half:].astype(F32) + for_x.astype(F32)).astype(BF16)
     from_x = px(jnp.concatenate([to_x[:half], x_low], 0))
@@ -86,31 +103,8 @@
     return own.astype(F32) + from_x.astype(F32) + from_y.astype(F32)
 
 
-def swap_over_x(values, dp_place, dp_size):
-    if dp_size % 2:
-        return px(values)
-    half = values.shape[0] // 2
-    odd = dp_place % 2
-    mine = px(rows_at(values, odd * half, half))
-    pairs = [(i, i ^ 1) for i in range(dp_size)]
-    other = lax.ppermute(mine, "dp", pairs)
-    return pair(odd == 0, mine, other, 0)
-
-
-def total_over(values, axes, dp_size):
-    if "core" in axes:
-        values = values + pc(values)
-    if "y" in axes:
-        values = values + py(values)
-    if "x" in axes:
-        values = values + px(values)
-    if dp_size & (dp_size - 1):
-        return lax.psum(values, "dp")
-    step = 1
-    while step < dp_size:
-        values = values + lax.ppermute(values, "dp", [(i, i ^ step) for i in range(dp_size)])
-        step *= 2
-    return values
+def scatter_plane(partial):
+    return scatter_near(*scatter_far(scatter_core(partial)))
 
 
 def rms_norm(values, scaling):
@@ -207,7 +201,8 @@
             rope_total = rope_total + part
             keyval_grad[:, h * SLOT : h * SLOT + NOPE] = part[:, :NOPE].astype(BF16)
             keyval_grad[:, h * SLOT + NOPE : (h + 1) * SLOT] = value_total[:, h * VD : (h + 1) * VD].astype(BF16)
-        rope_grad[...] = rope_total[:, NOPE : NOPE + RD]
+        lanes = lax.broadcasted_iota(jnp.int32, rope_total.shape, 1)
+        rope_grad[...] = jnp.where(lanes >= NOPE, rope_total, 0.0).astype(BF16)
 
 
 def row_tile(rows, width):
@@ -218,15 +213,16 @@
     return pl.BlockSpec(shape, lambda i: (0, 0))
 
 
-def attend(comp, lat, rope, turns, w_query, w_keyval, marks, heads, tile):
-    rows = comp.shape[0]
+def attend(latents, turns, w_query, w_keyval, marks, heads, tile):
+    rows = latents.shape[0]
     column = row_tile(tile, 1)
     line = whole((1, rows))
     return pl.pallas_call(
         lambda *refs: attend_kernel(heads, *refs),
         grid=(rows // tile,),
         in_specs=[
-            row_tile(tile, QR), whole((rows, KVR)), whole((rows, SLOT)),
+            row_tile(tile, QR), pl.BlockSpec((rows, KVR), lambda i: (0, QR // KVR)),
+            pl.BlockSpec((rows, SLOT), lambda i: (0, (QR + KVR) // SLOT)),
             row_tile(tile, SLOT), row_tile(tile, SLOT), row_tile(tile, SLOT),
             whole(w_query.shape), whole(w_keyval.shape), column, column, line, line,
         ],
@@ -247,7 +243,7 @@
             transcendentals=heads * rows * rows,
         ),
         name="attend",
-    )(comp, lat, rope, *turns, w_query, w_keyval, *marks)
+    )(latents, latents, latents, *turns, w_query, w_keyval, *marks)
 
 
 def attend_back(query, key, value, lse, grad_out, turns, marks, heads, tile):
@@ -263,12 +259,12 @@
             row_tile(tile, SLOT), row_tile(tile, SLOT), row_tile(tile, SLOT), column, column, line, line,
         ],
         out_specs=[
-            row_tile(tile, heads * SLOT), whole((rows, heads * SLOT)), whole((rows, RD)),
+            row_tile(tile, heads * SLOT), whole((rows, heads * SLOT)), whole((rows, SLOT)),
         ],
         out_shape=[
             jax.ShapeDtypeStruct((rows, heads * SLOT), BF16),
             jax.ShapeDtypeStruct((rows, heads * SLOT), BF16),
-            jax.ShapeDtypeStruct((rows, RD), F32),
+            jax.ShapeDtypeStruct((rows, SLOT), BF16),
         ],
         scratch_shapes=[pltpu.VMEM((rows, heads * SLOT), F32), pltpu.VMEM((rows, heads * VD), F32)],
         compiler_params=pltpu.CompilerParams(vmem_limit_bytes=48 << 20),
@@ -279,24 +275,11 @@
     )(query, key, value, lse, grad_out, *turns, *marks)
 
 
-def feedforward(rows, grad_rows, gate_up, down):
-    units = down.shape[0]
-    both = dot(gate_up, rows, (1, 1))
-    return activate(both[:units], both[units:], dot(down, grad_rows, (1, 1)))
-
-
 def activate(gate, up, grad_act):
     sigmoid_gate = jax.nn.sigmoid(gate)
     swish = gate * sigmoid_gate
     grad_gate = grad_act * up * sigmoid_gate * (1.0 + gate * (1.0 - sigmoid_gate))
-    return (
-        (swish * up).astype(BF16),
-        jnp.concatenate([grad_gate.astype(BF16), (grad_act * swish).astype(BF16)], 0),
-    )
-
-
-def together(*values):
-    return lax.optimization_barrier(values)
+    return (swish * up).astype(BF16), grad_gate.astype(BF16), (grad_act * swish).astype(BF16)
 
 
 def per_device(
@@ -319,32 +302,51 @@
         length = values.shape[axis] // 2
         return lax.dynamic_slice_in_dim(values, which * length, length, axis)
 
-    stream = pair(first_x, half_of(hidden, 0, row), px(half_of(hidden, 0, 1 - row)), 1).astype(F32)
+    middle_plane = (dp_place == 1) | (dp_place == 2)
+
+    def add(a, b):
+        return (a.astype(F32) + b.astype(F32)).astype(BF16)
+
+    def inward(part):
+        return part, lax.ppermute(part, "dp", ((0, 1), (3, 2)))
+
+    def across(part, arrived):
+        near = add(part, arrived)
+        return near, lax.ppermute(near, "dp", ((1, 2), (2, 1)))
+
+    def outward(near, far):
+        total = add(near, far)
+        return total, lax.ppermute(total, "dp", ((1, 0), (2, 3)))
+
+    def settled(total, back):
+        return jnp.where(middle_plane, total, back)
+
+    pairs = [(i, i ^ 1) for i in range(dp_size)]
+    odd = dp_place % 2
+    barrier = lax.optimization_barrier
+
+    gain_in = attention_gain.astype(F32)
+    hidden_wide = hidden.astype(F32)
+    squares = jnp.sum(hidden_wide * hidden_wide, axis=1)[None, :]
+    inverse_half = lax.rsqrt((squares + px(squares))[0] / (2 * half_width) + EPSILON)
+    inverse_in = half_of(inverse_half, 0, row)
+    scaled_in = hidden_wide * inverse_half[:, None]
+    normed_half = (scaled_in * gain_in[None, :]).astype(BF16)
+
+    by_factors = dp_size == 4
+    every = ("dp", "row", "col")
+
     latent_tile = jnp.concatenate([query_down.T, latent_down.T], 0)
     tile_width = latent_tile.shape[0]
     near_tiles = jnp.concatenate([latent_tile, py(latent_tile)], 0)
+
+    tiles = [gate_weight.T, up_weight.T, down_weight]
+    count = units // dp_size
+    wanted = [rows_at(t, (1 - row) * units + dp_place * count, count) for t in tiles]
+    fetched = px(jnp.concatenate(wanted, 0))
     latent_weights = jnp.concatenate([near_tiles, pc(near_tiles)], 0)
-
     query_columns = query_up.shape[1] // 2
-    other_query = px(half_of(query_up, 1, 1 - row))
-    w_query = pair(first_x, half_of(query_up, 1, row), other_query, 0)
-    w_query = jnp.pad(w_query.reshape(QR, heads, NOPE + RD), ((0, 0), (0, 0), (0, SLOT - NOPE - RD)))
-    w_query = w_query.reshape(QR, heads * SLOT)
     w_keyval = half_of(latent_up, 1, row)
-    w_out = pair(first_x, half_of(attention_out, 0, row), px(half_of(attention_out, 0, 1 - row)), 1)
-
-    def whole_units(tile_t):
-        other = swap_over_x(rows_at(tile_t, (1 - row) * units, units), dp_place, dp_size)
-        return pair(first_x, rows_at(tile_t, row * units, units), other, 1)
-
-    gate_up = jnp.concatenate([whole_units(gate_weight.T), whole_units(up_weight.T)], 0)
-    down = whole_units(down_weight)
-
-    incoming = pair(first_x, half_of(cotangent, 0, row), px(half_of(cotangent, 0, 1 - row)), 1).astype(F32)
-    grad_down_own = (RESIDUAL_SCALE * incoming).astype(BF16)
-    grad_down = gather_plane(grad_down_own)
-    by_factors = dp_size == 4
-    every = ("dp", "row", "col")
 
     second = jnp.sum((sequence_index == sequence_index[0]).astype(jnp.int32))
     inverse_rate = -2.0 * math.log(10000.0) / RD
@@ -367,13 +369,13 @@
     own_cosine = cosine[:own_rows, NOPE : NOPE + RD // 2]
     own_sine = sine[:own_rows, NOPE : NOPE + RD // 2]
 
-    gain_in = attention_gain.astype(F32)
-    inverse_in = lax.rsqrt(jnp.mean(stream * stream, axis=1) + EPSILON)
-    inverse_half = pair(first_x, inverse_in, px(inverse_in[None, :])[0], 0)
-    scaled_in = hidden.astype(F32) * inverse_half[:, None]
-    normed_half = (scaled_in * gain_in[None, :]).astype(BF16)
     latent_part = dot(normed_half, latent_weights, (1, 1))
-    latent_raw = half_of(latent_part, 0, row) + px(half_of(latent_part, 0, 1 - row))
+    latent_other, query_other = together(half_of(latent_part, 0, 1 - row), half_of(query_up, 1, 1 - row))
+    latent_other, query_other = px(latent_other), px(query_other)
+    normed_y = py(normed_half)
+    latent_raw = half_of(latent_part, 0, row) + latent_other
+    latent_raw, fetched = together(latent_raw, fetched)
+    others = lax.all_gather(fetched, "dp", axis=0, tiled=True)
 
     def in_place(values):
         blocks = [values[:, i * tile_width : (i + 1) * tile_width] for i in range(4)]
@@ -400,70 +402,109 @@
     own_latents, latent_back = jax.vjp(
         latent_norms, query_latent, kv_latent, query_gain.astype(F32), latent_gain.astype(F32)
     )
-    latents = gather_plane(jnp.concatenate(own_latents, 1).astype(BF16))
-    if by_factors:
-        grad_down_late, latents = together(grad_down_own, latents)
-        grads_all = lax.all_gather(grad_down_late, every, axis=0, tiled=True)
+    side = ((0, 0), (NOPE, SLOT - NOPE - RD))
+    latents_near = gather_near(jnp.concatenate([*own_latents[:2], jnp.pad(own_latents[2], side)], 1).astype(BF16))
+    *latents_near, query_other = together(*latents_near, query_other)
+    w_query = pair(first_x, half_of(query_up, 1, row), query_other, 0)
+    w_query = jnp.pad(w_query.reshape(QR, heads, NOPE + RD), ((0, 0), (0, 0), (0, SLOT - NOPE - RD)))
+    w_query = w_query.reshape(QR, heads * SLOT)
+    latents = gather_core(gather_far(*latents_near))
+    latents, w_query, out_late, hidden_late, cotangent_late, gain_late = together(
+        latents, w_query, half_of(attention_out, 0, 1 - row), half_of(hidden, 0, 1 - row),
+        half_of(cotangent, 0, 1 - row), feedforward_gain,
+    )
+    gain_mid = pair(first_x, feedforward_gain, px(gain_late), 0).astype(F32)
+    out_other, hidden_other, cotangent_other = px(out_late), px(hidden_late), px(cotangent_late)
     compressed, latent = latents[:, :QR], latents[:, QR : QR + KVR]
-    rope = jnp.pad(latents[:, QR + KVR :], ((0, 0), (NOPE, SLOT - NOPE - RD)))
-
     query, key, value, attended, lse = attend(
-        compressed, latent, rope, turns, w_query, w_keyval, marks, heads, tile
-    )
-
-    middle = stream + RESIDUAL_SCALE * scatter_plane(dot(attended, w_out, (1, 0), BF16))
-    gain_mid = pair(first_x, feedforward_gain, px(feedforward_gain), 0).astype(F32)
+        latents, turns, w_query, w_keyval, marks, heads, tile
+    )
+
+    attended, out_other, hidden_other, cotangent_other, normed_y = together(
+        attended, out_other, hidden_other, cotangent_other, normed_y
+    )
+    incoming = pair(first_x, half_of(cotangent, 0, row), cotangent_other, 1).astype(F32)
+    grad_down_own = (RESIDUAL_SCALE * incoming).astype(BF16)
+    normed_rows = jnp.concatenate([normed_half, normed_y], 0)
+    w_out = pair(first_x, half_of(attention_out, 0, row), out_other, 1)
+    stream = pair(first_x, half_of(hidden, 0, row), hidden_other, 1).astype(F32)
+    branch = scatter_core(dot(attended, w_out, (1, 0), BF16))
+    middle = stream + RESIDUAL_SCALE * scatter_near(*scatter_far(branch))
     inverse_mid = lax.rsqrt(jnp.mean(middle * middle, axis=1, keepdims=True) + EPSILON)
     scaled_mid = middle * inverse_mid
     normed_mid_own = (scaled_mid * gain_mid[None, :]).astype(BF16)
-    normed_mid = gather_plane(normed_mid_own)
+
+    def assembled(weights, start, which):
+        own = rows_at(tiles[which], row * units, units)
+        weights = lax.dynamic_update_slice(weights, own, (start, row * half_width))
+        for k in range(dp_size):
+            other = others[(3 * k + which) * count : (3 * k + which + 1) * count]
+            weights = lax.dynamic_update_slice(weights, other, (start + k * count, (1 - row) * half_width))
+        return weights
 
     if by_factors:
         rows_all = lax.all_gather(normed_mid_own, every, axis=0, tiled=True)
-
-    activation, grad_both = feedforward(normed_mid, grad_down, gate_up, down)
-    mid_part = dot(grad_both, gate_up, (0, 0), BF16)
-    output_part = dot(activation, down, (0, 0), BF16)
+    normed_near = gather_near(normed_mid_own)
+    *normed_near, others, normed_rows, grad_down_own = together(*normed_near, others, normed_rows, grad_down_own)
     if by_factors:
-        mid_part, grads_all = together(mid_part, grads_all)
-        odd = dp_place % 2
-        own_units = units // 2
-
-        def own_half(weights):
-            return rows_at(weights, odd * own_units, own_units)
-
-        down_half = own_half(down)
-        gate_up_half = jnp.concatenate([own_half(gate_up[:units]), own_half(gate_up[units:])], 0)
-        grad_act_all = dot(down_half, grads_all, (1, 1))
-    upstream_mid = scatter_plane(mid_part)
-    if by_factors:
-        upstream_mid, grad_act_all, output_part = together(upstream_mid, grad_act_all, output_part)
+        grads_all = lax.all_gather(grad_down_own, every, axis=0, tiled=True)
+    normed_far = gather_far(*normed_near)
+    grad_down_near = gather_near(grad_down_own)
+    gate_up = jnp.zeros((2 * units, 2 * half_width), BF16)
+    gate_up = assembled(assembled(gate_up, 0, 0), units, 1)
+    down = assembled(jnp.zeros((units, 2 * half_width), BF16), 0, 2)
+    normed_mid = gather_core(normed_far)
+    normed_mid, *grad_down_near = together(normed_mid, *grad_down_near)
+    grad_down_far = gather_far(*grad_down_near)
+    normed_rows = jnp.concatenate([normed_rows, pc(normed_rows)], 0)
+    both, *grad_down_far = together(dot(gate_up, normed_mid, (1, 1)), *grad_down_far)
+    grad_down = gather_core(grad_down_far)
+    grad_act = dot(down, grad_down, (1, 1))
+    activation, grad_gate, grad_up = activate(both[:units], both[units:], grad_act)
+    activation, grad_both = together(activation, jnp.concatenate([grad_gate, grad_up], 0))
+
+    mid_total = scatter_core(dot(grad_both, gate_up, (0, 0), BF16))
+    mid_total, activation = together(mid_total, activation)
+    mid_steps = scatter_far(mid_total)
+    upstream_mid = scatter_near(*mid_steps)
     weighted = upstream_mid * gain_mid[None, :]
     mean_inner = jnp.mean(weighted * scaled_mid, axis=1, keepdims=True)
     gain_mid_part = jnp.sum(upstream_mid * scaled_mid, axis=0)
     grad_middle = incoming + inverse_mid * (weighted - scaled_mid * mean_inner)
-    grad_branch = gather_plane((RESIDUAL_SCALE * grad_middle).astype(BF16))
+    branch_near = gather_near((RESIDUAL_SCALE * grad_middle).astype(BF16))
+    *branch_near, activation_late = together(*branch_near, activation)
+    branch_far = gather_far(*branch_near)
+    output_part = dot(activation_late, down, (0, 0), BF16)
+    *branch_far, output_part = together(*branch_far, output_part)
+    grad_branch = gather_core(branch_far)
 
     grad_attended = dot(grad_branch, w_out, (1, 1), BF16)
+    out_part = dot(attended, grad_branch, (0, 0), BF16)
+    grad_attended, out_part = together(grad_attended, out_part)
+    out_other = px(half_of(out_part, 1, 1 - row))
     query_grad, keyval_grad, rope_grad = attend_back(
         query, key, value, lse, grad_attended, turns, marks, heads, tile
     )
+    query_grad, keyval_grad, rope_grad, out_other = together(query_grad, keyval_grad, rope_grad, out_other)
+    out_part = pair(first_x, half_of(out_part, 1, row), out_other, 0)
     latent_grad_part = jnp.concatenate(
         [
             dot(query_grad, w_query, (1, 1), BF16),
             dot(keyval_grad, w_keyval, (1, 1), BF16),
-            rope_grad.astype(BF16),
+            rope_grad,
         ],
         1,
     )
+    latent_steps = scatter_far(scatter_core(latent_grad_part))
     if by_factors:
-        latent_grad_part, rows_all = together(latent_grad_part, rows_all)
-        both_all = dot(gate_up_half, rows_all, (1, 1))
-    latent_grad = scatter_plane(latent_grad_part)
+        *latent_steps, rows_all = together(*latent_steps, rows_all)
+        gate_all = dot(gate_up[:units], rows_all, (1, 1))
+    latent_steps = list(latent_steps)
+    latent_grad = scatter_near(*latent_steps)
     if by_factors:
-        latent_grad, both_all = together(latent_grad, both_all)
+        latent_grad, gate_all, output_part = together(latent_grad, gate_all, output_part)
     query_latent_grad, kv_latent_grad, query_gain_part, latent_gain_part = latent_back(
-        (latent_grad[:, :QR], latent_grad[:, QR : QR + KVR], latent_grad[:, QR + KVR :])
+        (latent_grad[:, :QR], latent_grad[:, QR : QR + KVR], latent_grad[:, QR + KVR + NOPE : QR + KVR + NOPE + RD])
     )
     kv_tile = latent_down.shape[1]
     query_low, kv_low = query_latent_grad.astype(BF16), kv_latent_grad.astype(BF16)
@@ -483,8 +524,13 @@
     )
     g0, g1, g2, g3 = in_place(in_blocks)
     latent_low = jnp.concatenate([g0, g2, g1, g3], 1)
-    latent_low = pair(first_x, latent_low, px(latent_low), 0)
-    inner_half = pair(first_x, inner_in, px(inner_in[None, :])[0], 0)
+    low_other, inner_other = px(latent_low), px(inner_in[None, :])[0]
+    if by_factors:
+        out_1 = inward(out_part)
+        up_all = dot(gate_up[units:], rows_all, (1, 1))
+        low_other, up_all, out_1 = barrier((low_other, up_all, out_1))
+    latent_low = pair(first_x, latent_low, low_other, 0)
+    inner_half = pair(first_x, inner_in, inner_other, 0)
     grad_normed = dot(latent_low, latent_weights, (1, 0))
     grad_middle_half = pair(
         first_x,
@@ -494,59 +540,85 @@
     )
     grad_in = inverse_half[:, None] * (grad_normed * gain_in[None, :] - scaled_in * inner_half[:, None])
     input_gradient = (grad_middle_half + grad_in).astype(BF16)
-    gain_in_total = total_over(
-        jnp.sum(grad_normed * scaled_in, axis=0).reshape(-1, SLOT), ("core", "y"), dp_size
-    ).reshape(-1)
+    gain_in_part = jnp.sum(grad_normed * scaled_in, axis=0)
 
     output_own = (middle + RESIDUAL_SCALE * scatter_plane(output_part)).astype(BF16)
     output = pair(first_x, half_of(output_own, 1, row), px(half_of(output_own, 1, 1 - row)), 0)
 
+    up_part = dot(compressed, query_grad, (0, 0), BF16).reshape(QR, heads, SLOT)[:, :, : NOPE + RD]
+    up_part = up_part.reshape(QR, query_columns)
+    up_part = pair(first_x, half_of(up_part, 0, row), px(half_of(up_part, 0, 1 - row)), 1)
+    latent_up_part = dot(latent, keyval_grad, (0, 0), BF16)
+    latent_up_part = pair(first_x, latent_up_part, px(latent_up_part), 1)
+    low_blocks = [latent_low[:, i * tile_width : (i + 1) * tile_width] for i in range(4)]
+    low_rows = jnp.concatenate([low_blocks[0], py(low_blocks[1]), pc(low_blocks[2]), pyc(low_blocks[3])], 0)
+    latent_down_part = dot(low_rows, normed_rows, (0, 0), BF16)
+
+    gains = jnp.concatenate([gain_in_part, gain_mid_part, query_gain_part, latent_gain_part]).reshape(-1, SLOT)
+    gains = gains + pc(gains)
+    gains = gains + py(gains)
+    own_gains = half_width // SLOT
+    gains = jnp.concatenate([gains[:own_gains], gains[own_gains:] + px(gains[own_gains:])], 0).reshape(-1)
+    gain_count = gains.shape[0]
+    gains = jnp.pad(gains, (0, -gain_count % half_width)).reshape(-1, half_width).astype(BF16)
+    latent_down_part = jnp.concatenate([latent_down_part, gains], 0)
     if by_factors:
-        act_all, grad_both_all = together(*activate(both_all[:own_units], both_all[own_units:], grad_act_all))
-        up_total = dot(grad_both_all[own_units:], rows_all, (1, 0), BF16)
-        gate_total = dot(grad_both_all[:own_units], rows_all, (1, 0), BF16)
-        down_total_ff = dot(act_all, grads_all, (1, 0), BF16)
-        pairs = [(i, i ^ 1) for i in range(dp_size)]
+        input_gradient, grads_all, up_part = barrier((input_gradient, grads_all, up_part))
+        out_2, up_1 = across(*out_1), inward(up_part)
+        grad_act_all = dot(down, grads_all, (1, 1))
+        gate_all, up_all, grad_act_all, out_2, up_1, latent_up_part, output = barrier(
+            (gate_all, up_all, grad_act_all, out_2, up_1, latent_up_part, output)
+        )
+        out_3, up_2, latent_1 = outward(*out_2), across(*up_1), inward(latent_up_part)
+        act_all, grad_gate_all, grad_up_all = activate(gate_all, up_all, grad_act_all)
+        act_all, grad_gate_all, grad_up_all, up_2, latent_1, latent_down_part = barrier(
+            (act_all, grad_gate_all, grad_up_all, up_2, latent_1, latent_down_part)
+        )
+        up_3, latent_2, down_1 = outward(*up_2), across(*latent_1), inward(latent_down_part)
+        own_units = units // 2
+
+        def to_send(total):
+            return rows_at(half_of(total, 1, 1 - row), odd * own_units, own_units)
 
         def pz(values):
             return lax.ppermute(values, "dp", pairs)
 
-        def to_tile(total):
-            kept = half_of(total, 1, row)
-            fetched = px(half_of(total, 1, 1 - row))
-            kept, fetched = pair(odd == 0, kept, pz(kept), 0), pair(odd == 0, fetched, pz(fetched), 0)
-            return pair(first_x, kept, fetched, 0).astype(F32)
-
-        up_grad_t, gate_grad_t, down_grad = (to_tile(g) for g in (up_total, gate_total, down_total_ff))
+        up_total = dot(grad_up_all, rows_all, (1, 0), BF16)
+        up_total, grad_gate_all, latent_2, down_1 = barrier((up_total, grad_gate_all, latent_2, down_1))
+        latent_3, down_2 = outward(*latent_2), across(*down_1)
+        up_other = px(to_send(up_total))
+        gate_total = dot(grad_gate_all, rows_all, (1, 0), BF16)
+        gate_total, act_all, down_2, up_other = barrier((gate_total, act_all, down_2, up_other))
+        down_3 = outward(*down_2)
+        up_far, gate_other = pz(up_other), px(to_send(gate_total))
+        down_ff = dot(act_all, grads_all, (1, 0), BF16)
+        down_ff, up_far, gate_other = barrier((down_ff, up_far, gate_other))
+        gate_far, down_other = pz(gate_other), px(to_send(down_ff))
+        unit_grads = [up_total, gate_total, down_ff]
+        up_other, gate_other, down_other = (
+            pair(odd == 0, other, far, 0)
+            for other, far in ((up_other, up_far), (gate_other, gate_far), (down_other, pz(down_other)))
+        )
+        unit_others = [up_other, gate_other, down_other]
+        out_grad, query_up_grad = settled(*out_3), settled(*up_3)
+        latent_up_grad, down_total = settled(*latent_3), settled(*down_3)
     else:
-
-        def to_tile(part):
-            total = lax.psum(part, "dp")
-            return pair(first_x, half_of(total, 1, row), px(half_of(total, 1, 1 - row)), 0).astype(F32)
-
-        up_grad_t, gate_grad_t, down_grad = (
-            to_tile(dot(a, b, (1, 0), BF16))
+        unit_grads = [
+            lax.psum(dot(a, b, (1, 0), BF16), "dp")
             for a, b in (
                 (grad_both[units:], normed_mid), (grad_both[:units], normed_mid), (activation, grad_down),
             )
+        ]
+        unit_others = [px(half_of(total, 1, 1 - row)) for total in unit_grads]
+        out_grad, query_up_grad, latent_up_grad, down_total = (
+            lax.psum(part, "dp") for part in (out_part, up_part, latent_up_part, latent_down_part)
         )
-
-    out_part = dot(attended, grad_branch, (0, 0), BF16)
-    out_grad = lax.psum(pair(first_x, half_of(out_part, 1, row), px(half_of(out_part, 1, 1 - row)), 0), "dp")
-    up_part = dot(compressed, query_grad, (0, 0), BF16).reshape(QR, heads, SLOT)[:, :, : NOPE + RD]
-    up_part = up_part.reshape(QR, query_columns)
-    query_up_grad = lax.psum(pair(first_x, half_of(up_part, 0, row), px(half_of(up_part, 0, 1 - row)), 1), "dp")
-    latent_part_grad = dot(latent, keyval_grad, (0, 0), BF16)
-    latent_up_grad = lax.psum(pair(first_x, latent_part_grad, px(latent_part_grad), 1), "dp")
-    normed_rows = jnp.concatenate([normed_half, py(normed_half)], 0)
-    normed_rows = jnp.concatenate([normed_rows, pc(normed_rows)], 0)
-    low_blocks = [latent_low[:, i * tile_width : (i + 1) * tile_width] for i in range(4)]
-    low_rows = jnp.concatenate([low_blocks[0], py(low_blocks[1]), pc(low_blocks[2]), pyc(low_blocks[3])], 0)
-    down_part = dot(low_rows, normed_rows, (0, 0), BF16)
-    down_total = lax.psum(down_part, "dp").astype(F32)
-
-    own_gains = jnp.concatenate([gain_mid_part, query_gain_part, latent_gain_part]).reshape(-1, SLOT)
-    gain_totals = total_over(own_gains, ("core", "y", "x"), dp_size).reshape(-1)
+    up_grad_t, gate_grad_t, down_grad = (
+        pair(first_x, half_of(total, 1, row), other, 0).astype(F32) for total, other in zip(unit_grads, unit_others)
+    )
+    down_total = down_total.astype(F32)
+    gain_totals = down_total[tile_width:].reshape(-1)
+    gain_in_total, gain_totals = gain_totals[:half_width], gain_totals[half_width:gain_count]
     width = 2 * half_width
     return (
         output,
@@ -555,7 +627,7 @@
         down_total[:query_tile].T,
         gain_totals[width : width + QR],
         query_up_grad.astype(F32),
-        down_total[query_tile:].T,
+        down_total[query_tile:tile_width].T,
         gain_totals[width + QR :],
         latent_up_grad.astype(F32),
         out_grad.astype(F32),

time: 1100 us -> 851 us (0.77)
  waiting for transfers between devices: 607 us -> 263 us
  matrix products: 155 us -> 218 us
  starting transfers between devices: 78.3 us -> 102 us
  local copies, waits for them, and re-layouts: 93.1 us -> 107 us
    ppermute x6 -> x3, waiting for transfers between devices: 183 us -> 18 us  [pz(): return lax.ppermute(values, 'dp', pairs)]
    ppermute x37 -> x35, waiting for transfers between devices: 230 us -> 146 us  [px(): return lax.ppermute(values, 'row', OVER_X)]
    ppermute x7 -> x12, waiting for transfers between devices: 88.5 us -> 11.2 us  [the longest x4 11.2 us: outward(): return (total, lax.ppermute(total, 'dp', ((1, 0), (2, 3))))]
    dot_general x19 -> x20, matrix products: 155 us -> 218 us  [dot(): lax.dot_general(a, b, ((contract[:1], contract[1:]), ((), ())), preferred...]
    ppermute x21 -> x20, waiting for transfers between devices: 87.7 us -> 58.4 us  [py(): return lax.ppermute(values, 'col', OVER_Y)]
    ppermute x7 -> x12, starting transfers between devices: 7.99 us -> 34.5 us  [the longest x4 23.7 us: inward(): return (part, lax.ppermute(part, 'dp', ((0, 1), (3, 2))))]
    select_n x20 -> x10, other arithmetic: 36.2 us -> 12.9 us  [pair(): jnp.where(first_is_own, jnp.concatenate([own, other], axis), jnp.concaten...]
    convert_element_type x13 -> x25, other arithmetic: 18 us -> 38.8 us  [the longest x1 16.9 us: activate(): (grad_act * swish).astype(BF16)]
  transfers between devices with their start and end apart: 88 -> 86, of which waited for: 52 -> 40; matrix products, arithmetic and copies ran while one was open for 29% -> 46% of each run, Pallas kernels for 4% -> 5%
where the time goes in v2:
time: 851 us; the launch traced here: 844 us
  waiting for transfers between devices  263 us (31%)
  matrix products  218 us (26%)
  local copies, waits for them, and re-layouts  107 us (13%)
  starting transfers between devices  102 us (12%)
  other arithmetic  94.4 us (11%)
  Pallas kernels  43.1 us (5%)
  between operations  16.1 us (2%)
    dot_general x20, matrix products, dot(): lax.dot_general(a, b, ((contract[:1], contract[1:]), ((), ())), preferred...  218 us
    ppermute x35, waiting for transfers between devices, px(): return lax.ppermute(values, 'row', OVER_X)  146 us
    ppermute x20, waiting for transfers between devices, py(): return lax.ppermute(values, 'col', OVER_Y)  58.4 us
    unnamed x249, local copies, waits for them, and re-layouts  37.3 us
    ppermute x35, starting transfers between devices, px(): return lax.ppermute(values, 'row', OVER_X)  37 us
    pallas_call x1, Pallas kernels, attend_back(): pl.pallas_call(lambda *refs: attend_back_kernel(heads, *refs), grid=(rows...  25.6 us
    ppermute x4, starting transfers between devices, inward(): return (part, lax.ppermute(part, 'dp', ((0, 1), (3, 2))))  23.7 us
    ppermute x20, starting transfers between devices, py(): return lax.ppermute(values, 'col', OVER_Y)  20 us
  transfers between devices with their start and end apart: 86, of which 40 were waited for; matrix products, arithmetic and copies ran while one was open for 46% of the time, Pallas kernels for 5%

profile of v2, /device:TPU:0, one launch (start us, length us, event | category | flops | bytes accessed | tf_op | source)
XLA Modules:
  0.0 843.5 jit_solution(15016787215463025291)
XLA Ops:
  9.3 3.0 collective-permute-start.1
  20.3 7.5 collective-permute-done.1
  33.5 2.5 fusion.35
  40.2 3.1 fusion.36
  45.7 21.5 %collective-permute-done.3 = f32[128,1056]{0,1:T(8,128)} collective-permute-done((f32[128,1056]{0,1:T(8,128)}, f32[128,1056]{0,1:T(8,128)}, u32[]{:S(2)}, u32[]{:S(2)}) %collective-permute-start.3) | collective-permute-done | bytes 540704 | tf_op jit(solution)/shard_map/ppermute | solution.py:32
  77.4 6.4 collective-permute-done.5
  114.6 17.5 %attend.1 = (bf16[1024,640]{1,0:T(8,128)(2,1)}, bf16[1024,640]{1,0:T(8,128)(2,1)}, bf16[1024,320]{1,0:T(8,128)(2,1)S(1)}, bf16[1024,320]{1,0:T(8,128)(2,1)S(1)}, f32[1024,8]{1,0:T(8,128)S(1)}) custom-call(bf16[1024,1152]{1,0:T(8,128)(2,1)} %copy-done.73, bf16[1024,1152]{1,0:T(8,128)(2,1)} %copy-done.73, bf16[1024,1152]{1,0:T(8,128)(2,1)} %copy-done.73, ...), custom_call_target="tpu_custom_call" | custom-call | flops 3690987520 | bytes 8388608 | tf_op jit(solution)/shard_map/attend/pallas_call | solution.py:220
  132.1 2.6 collective-permute-done.12
  134.7 6.6 collective-permute-done.13
  141.4 4.7 fusion.40
  146.4 4.9 collective-permute-done.15
  154.7 7.2 collective-permute-done.16
  166.1 13.2 %collective-permute-done.20 = bf16[1280]{0:T(1024)(128)(2,1)S(1)} collective-permute-done((bf16[1280]{0:T(1024)(128)(2,1)S(1)}, bf16[1280]{0:T(1024)(128)(2,1)S(1)}, u32[]{:S(2)}, u32[]{:S(2)}) %collective-permute-start.20) | collective-permute-done | bytes 2592 | tf_op jit(solution)/shard_map/ppermute | solution.py:32
  183.0 4.1 broadcast_in_dim.78
  196.4 7.1 collective-permute-done.21
  204.3 10.4 %all-gather.4.cloned.1.call-done = bf16[2400,1280]{1,0:T(8,128)(2,1)} async-done(((bf16[600,1280]{1,0:T(8,128)(2,1)}), bf16[2400,1280]{1,0:T(8,128)(2,1)}) %all-gather.4.cloned.1.call-update) | async-done | bytes 6144016 | tf_op jit(solution)/shard_map/all_gather | solution.py:378
  228.4 15.9 %collective-permute-done.23 = bf16[64,2560]{1,0:T(8,128)(2,1)S(1)} collective-permute-done((bf16[64,2560]{1,0:T(8,128)(2,1)S(1)}, bf16[64,2560]{1,0:T(8,128)(2,1)S(1)}, u32[]{:S(2)}, u32[]{:S(2)}) %collective-permute-start.23) | collective-permute-done | bytes 327712 | tf_op jit(solution)/shard_map/ppermute | solution.py:40
  253.2 12.7 %fusion.62 = f32[1600,1024]{1,0:T(8,128)} fusion(bf16[1600,2560]{1,0:T(8,128)(2,1)} %get-tuple-element.255, bf16[1024,2560]{1,0:T(8,128)(2,1)S(1)} %constant_dynamic-update-slice_fusion.19), kind=kOutput, calls=%fused_computation.319 | convolution fusion | flops 8388608000 | bytes 19988480 | tf_op jit(solution)/shard_map/dot_general | solution.py:48
  276.7 5.2 collective-permute-done.30
  281.9 3.4 constant_dynamic-update-slice_fusion.30
  285.3 11.1 %multiply_convert_fusion.4 = (bf16[800,1024]{1,0:T(8,128)(2,1)S(1)}, bf16[800,1024]{1,0:T(8,128)(2,1)S(1)}, bf16[800,1024]{1,0:T(8,128)(2,1)S(1)}) fusion(f32[1600,1024]{1,0:T(8,128)} %fusion.62, bf16[800,2560]{1,0:T(8,128)(2,1)} %get-tuple-element.254, bf16[1024,2560]{1,0:T(8,128)(2,1)} %constant_dynamic-update-slice_fusion.30), kind=kOutput, calls=%fused_computation.22 | convolution fusion | flops 4206592000 | bytes 20807680 | tf_op jit(solution)/shard_map/dot_general | solution.py:48
  296.8 13.0 %fusion.63 = bf16[1024,2560]{1,0:T(8,128)(2,1)S(1)} fusion(bf16[1600,1024]{1,0:T(8,128)(2,1)S(1)} %pad_maximum_fusion, bf16[1600,2560]{1,0:T(8,128)(2,1)} %get-tuple-element.255), kind=kOutput, calls=%fused_computation.320 | convolution fusion | flops 8388608000 | bytes 16711680 | tf_op jit(solution)/shard_map/dot_general | solution.py:48
  310.1 4.8 collective-permute-done.31
  318.0 15.0 %collective-permute-done.32 = bf16[64,2560]{1,0:T(8,128)(2,1)S(1)} collective-permute-done((bf16[64,2560]{1,0:T(8,128)(2,1)S(1)}, bf16[64,2560]{1,0:T(8,128)(2,1)S(1)}, u32[]{:S(2)}, u32[]{:S(2)}) %collective-permute-start.32) | collective-permute-done | bytes 327712 | tf_op jit(solution)/shard_map/ppermute | solution.py:40
  336.8 18.5 %collective-permute-done.33 = bf16[128,2560]{1,0:T(8,128)(2,1)S(1)} collective-permute-done((bf16[128,2560]{1,0:T(8,128)(2,1)S(1)}, bf16[128,2560]{1,0:T(8,128)(2,1)S(1)}, u32[]{:S(2)}, u32[]{:S(2)}) %collective-permute-start.33) | collective-permute-done | bytes 655392 | tf_op jit(solution)/shard_map/ppermute | solution.py:32
  359.8 14.2 %collective-permute-done.36 = bf16[128,2560]{1,0:T(8,128)(2,1)S(1)} collective-permute-done((bf16[128,2560]{1,0:T(8,128)(2,1)S(1)}, bf16[128,2560]{1,0:T(8,128)(2,1)S(1)}, u32[]{:S(2)}, u32[]{:S(2)}) %collective-permute-start.36) | collective-permute-done | bytes 655392 | tf_op jit(solution)/shard_map/ppermute | solution.py:32
  377.4 9.7 %fusion.64 = bf16[1024,2560]{1,0:T(8,128)(2,1)} fusion(bf16[800,1024]{1,0:T(8,128)(2,1)S(1)} %get-tuple-element.170, bf16[800,2560]{1,0:T(8,128)(2,1)} %get-tuple-element.254), kind=kOutput, calls=%fused_computation.321 | convolution fusion | flops 4194304000 | bytes 10977280 | tf_op jit(solution)/shard_map/dot_general | solution.py:48
  396.0 3.0 collective-permute-done.40
  399.0 3.5 constant_dynamic-update-slice_fusion.41
  402.5 4.5 fusion.65
  407.0 4.2 fusion.39
  419.8 25.6 %attend_back.1 = (bf16[1024,640]{1,0:T(8,128)(2,1)}, bf16[1024,640]{1,0:T(8,128)(2,1)}, bf16[1024,128]{1,0:T(8,128)(2,1)S(1)}) custom-call(bf16[1024,640]{1,0:T(8,128)(2,1)} %get-tuple-element.133.refs_0_, bf16[1024,640]{1,0:T(8,128)(2,1)} %get-tuple-element.134.refs_1_, bf16[1024,320]{1,0:T(8,128)(2,1)S(1)} %copy-done.7, f32[1024,8]{1,0:T(8,128)S(1)} %copy-done.9, ...), custom_call_target="tpu_custom_call" | custom-call | flops 6710886400 | bytes 8388608 | tf_op jit(solution)/shard_map/attend_back/pallas_call | solution.py:253
  447.3 2.7 fusion.66
  458.8 4.6 collective-permute-start.48
  463.4 3.9 collective-permute-done.54
  468.4 13.9 %collective-permute-done.51 = bf16[384,480]{0,1:T(8,128)(2,1)S(1)} collective-permute-done((bf16[384,480]{0,1:T(8,128)(2,1)S(1)}, bf16[384,480]{0,1:T(8,128)(2,1)S(1)}, u32[]{:S(2)}, u32[]{:S(2)}) %collective-permute-start.51) | collective-permute-done | bytes 368672 | tf_op jit(solution)/shard_map/ppermute | solution.py:32
  486.0 6.5 collective-permute-done.43
  496.6 23.3 %fusion.3 = f32[800,4096]{1,0:T(8,128)} fusion(bf16[4096,2560]{1,0:T(8,128)(2,1)} %all-gather.6.cloned.1.call-done, bf16[1600,2560]{1,0:T(8,128)(2,1)} %get-tuple-element.255), kind=kOutput, calls=%fused_computation.12 | convolution fusion | flops 16777216000 | bytes 38174720 | tf_op jit(solution)/shard_map/dot_general | solution.py:48
  527.5 23.3 %fusion.1 = f32[800,4096]{1,0:T(8,128)} fusion(bf16[4096,2560]{1,0:T(8,128)(2,1)} %all-gather.6.cloned.1.call-done, bf16[1600,2560]{1,0:T(8,128)(2,1)} %get-tuple-element.255), kind=kOutput, calls=%fused_computation.10 | convolution fusion | flops 16777216000 | bytes 38174720 | tf_op jit(solution)/shard_map/dot_general | solution.py:48
  551.0 3.8 fusion.21
  561.7 3.0 add_convert_fusion.4
  564.8 5.2 collective-permute-done.56
  578.9 3.0 fusion.7
  582.8 5.5 collective-permute-start.53
  588.3 3.9 collective-permute-done.57
  596.1 23.9 %fusion.68 = f32[800,4096]{1,0:T(8,128)} fusion(bf16[800,2560]{1,0:T(8,128)(2,1)} %get-tuple-element.254, bf16[4096,2560]{1,0:T(8,128)(2,1)} %all-gather.8.cloned.1.call-done), kind=kOutput, calls=%fused_computation.325 | convolution fusion | flops 16777216000 | bytes 38174720 | tf_op jit(solution)/shard_map/dot_general | solution.py:48
  622.7 6.1 collective-permute-start.62
  628.8 3.0 add_convert_fusion.3
  633.3 16.9 %multiply_convert_fusion = (bf16[800,4096]{1,0:T(8,128)(2,1)}, bf16[800,4096]{1,0:T(8,128)(2,1)}, bf16[800,4096]{1,0:T(8,128)(2,1)S(1)}) fusion(f32[800,4096]{1,0:T(8,128)} %fusion.68, f32[800,4096]{1,0:T(8,128)S(1)} %bitcast.77, f32[800,4096]{1,0:T(8,128)} %fusion.1), kind=kLoop, calls=%fused_computation | loop fusion | flops 49152000 | bytes 58982400 | tf_op jit(solution)/shard_map/convert_element_type | solution.py:282
  652.2 7.5 collective-permute-start.71
  659.7 24.5 %fusion.69 = bf16[800,2560]{1,0:T(8,128)(2,1)} fusion(bf16[800,4096]{1,0:T(8,128)(2,1)} %get-tuple-element.210, bf16[4096,2560]{1,0:T(8,128)(2,1)} %all-gather.6.cloned.1.call-done), kind=kOutput, calls=%fused_computation.326 | convolution fusion | flops 16777216000 | bytes 31621120 | tf_op jit(solution)/shard_map/dot_general | solution.py:48
  687.9 24.4 %fusion.70 = bf16[800,2560]{1,0:T(8,128)(2,1)} fusion(bf16[800,4096]{1,0:T(8,128)(2,1)} %get-tuple-element.215, bf16[4096,2560]{1,0:T(8,128)(2,1)} %all-gather.6.cloned.1.call-done), kind=kOutput, calls=%fused_computation.327 | convolution fusion | flops 16777216000 | bytes 31621120 | tf_op jit(solution)/shard_map/dot_general | solution.py:48
  718.6 3.4 select_convert_fusion
  722.0 11.2 %collective-permute-done.76 = bf16[256,1280]{1,0:T(8,128)(2,1)S(1)} collective-permute-done((bf16[256,1280]{1,0:T(8,128)(2,1)S(1)}, bf16[256,1280]{1,0:T(8,128)(2,1)S(1)}, u32[]{:S(2)}, u32[]{:S(2)}) %collective-permute-start.76) | collective-permute-done | bytes 655392 | tf_op jit(solution)/shard_map/ppermute | solution.py:319
  738.8 22.6 %fusion.71 = bf16[800,2560]{1,0:T(8,128)(2,1)} fusion(bf16[800,4096]{1,0:T(8,128)(2,1)S(1)} %get-tuple-element.229, bf16[4096,2560]{1,0:T(8,128)(2,1)} %all-gather.8.cloned.1.call-done), kind=kOutput, calls=%fused_computation.328 | convolution fusion | flops 16777216000 | bytes 31621120 | tf_op jit(solution)/shard_map/dot_general | solution.py:48
  763.2 4.7 collective-permute-start.78
  773.7 11.1 %collective-permute-done.79 = bf16[400,1280]{1,0:T(8,128)(2,1)} collective-permute-done((bf16[400,1280]{1,0:T(8,128)(2,1)}, bf16[400,1280]{1,0:T(8,128)(2,1)}, u32[]{:S(2)}, u32[]{:S(2)}) %collective-permute-start.79) | collective-permute-done | bytes 1024032 | tf_op jit(solution)/shard_map/ppermute | solution.py:32
  792.2 2.6 maximum_select_fusion.4
  795.0 3.9 convert_bitcast_fusion
  798.9 10.2 %collective-permute-done.81 = bf16[400,1280]{1,0:T(8,128)(2,1)S(1)} collective-permute-done((bf16[400,1280]{1,0:T(8,128)(2,1)S(1)}, bf16[400,1280]{1,0:T(8,128)(2,1)S(1)}, u32[]{:S(2)}, u32[]{:S(2)}) %collective-permute-start.81) | collective-permute-done | bytes 1024032 | tf_op jit(solution)/shard_map/ppermute | solution.py:32
  810.5 3.5 collective-permute-done.80
  816.2 3.7 convert_bitcast_fusion.1
  820.0 12.1 %collective-permute-done.82 = bf16[400,1280]{1,0:T(8,128)(2,1)S(1)} collective-permute-done((bf16[400,1280]{1,0:T(8,128)(2,1)S(1)}, bf16[400,1280]{1,0:T(8,128)(2,1)S(1)}, u32[]{:S(2)}, u32[]{:S(2)}) %collective-permute-start.82) | collective-permute-done | bytes 1024032 | tf_op jit(solution)/shard_map/ppermute | solution.py:584
  833.0 3.7 fusion.5
  (594 shorter events, 239.1 us)
Async XLA Ops:
  7.2 207.5 %all-gather.4.cloned.1.call-start = ((), (), s32[]{:S(2)}) async-start(), calls=%async_computation | async-start | bytes 7680000 | tf_op jit(solution)/shard_map/all_gather | solution.py:378
  9.3 18.5 %collective-permute-start.1 = (bf16[264,1280]{1,0:T(8,128)(2,1)}, bf16[264,1280]{1,0:T(8,128)(2,1)}, u32[]{:S(2)}, u32[]{:S(2)}) collective-permute-start(bf16[264,1280]{1,0:T(8,128)(2,1)} %pad_maximum_fusion.7), channel_id=1, source_target_pairs={{0,2},{1,3},{2,0},{3,1},{4,6},{5,7},{6,4},{7,5},{8,10},{9,11},{10,... | collective-permute-start | bytes 2027528 | tf_op jit(solution)/shard_map/ppermute | solution.py:40
  13.6 19.5 %collective-permute-start = (f32[1,256]{1,0:T(1,128)S(1)}, f32[1,256]{1,0:T(1,128)S(1)}, u32[]{:S(2)}, u32[]{:S(2)}) collective-permute-start(f32[1,256]{1,0:T(1,128)S(1)} %bitcast.93), channel_id=1, source_target_pairs={{0,4},{4,0},{1,5},{5,1},{2,6},{6,2},{3,7},{7,3},{8,12},{12,8},{9,1... | collective-permute-start | bytes 3080 | tf_op jit(solution)/shard_map/ppermute | solution.py:32
  18.8 52.7 %collective-permute-start.4 = (bf16[600,1280]{1,0:T(8,128)(2,1)}, bf16[600,1280]{1,0:T(8,128)(2,1)}, u32[]{:S(2)}, u32[]{:S(2)}) collective-permute-start(bf16[600,1280]{1,0:T(8,128)(2,1)} %pad_maximum_fusion.3), channel_id=1, source_target_pairs={{0,4},{4,0},{1,5},{5,1},{2,6},{6,2},{3,7},{7,3},{8,12},{12,8},{9,1... | collective-permute-start | bytes 4608008 | tf_op jit(solution)/shard_map/ppermute | solution.py:32
  37.1 30.2 %collective-permute-start.3 = (f32[128,1056]{0,1:T(8,128)}, f32[128,1056]{0,1:T(8,128)}, u32[]{:S(2)}, u32[]{:S(2)}) collective-permute-start(f32[128,1056]{0,1:T(8,128)} %get-tuple-element.124), channel_id=1, source_target_pairs={{0,4},{4,0},{1,5},{5,1},{2,6},{6,2},{3,7},{7,3},{8,12},{12,8},{9,1... | collective-permute-start | bytes 1622024 | tf_op jit(solution)/shard_map/ppermute | solution.py:32
  45.4 32.0 %collective-permute-start.7 = (bf16[384,480]{0,1:T(8,128)(2,1)}, bf16[384,480]{0,1:T(8,128)(2,1)}, u32[]{:S(2)}, u32[]{:S(2)}) collective-permute-start(bf16[384,480]{0,1:T(8,128)(2,1)} %get-tuple-element.126), channel_id=1, source_target_pairs={{0,4},{4,0},{1,5},{5,1},{2,6},{6,2},{3,7},{7,3},{8,12},{12,8},{9,1... | collective-permute-start | bytes 1105928 | tf_op jit(solution)/shard_map/ppermute | solution.py:32
  100.7 393.7 %all-gather.6.cloned.1.call-start = ((), (), s32[]{:S(2)}) async-start(), calls=%async_computation.1 | async-start | bytes 21626880 | tf_op jit(solution)/shard_map/all_gather | solution.py:446
  106.5 34.9 %collective-permute-start.11 = (bf16[320,1280]{1,0:T(8,128)(2,1)}, bf16[320,1280]{1,0:T(8,128)(2,1)}, u32[]{:S(2)}, u32[]{:S(2)}) collective-permute-start(bf16[320,1280]{1,0:T(8,128)(2,1)} %get-tuple-element.138), channel_id=1, source_target_pairs={{0,4},{4,0},{1,5},{5,1},{2,6},{6,2},{3,7},{7,3},{8,12},{12,8},{9,1... | collective-permute-start | bytes 2457608 | tf_op jit(solution)/shard_map/ppermute | solution.py:32
  107.8 24.3 %collective-permute-start.14 = (bf16[256,1280]{1,0:T(8,128)(2,1)}, bf16[256,1280]{1,0:T(8,128)(2,1)}, u32[]{:S(2)}, u32[]{:S(2)}) collective-permute-start(bf16[256,1280]{1,0:T(8,128)(2,1)} %copy-done.36), channel_id=1, source_target_pairs={{0,2},{1,3},{2,0},{3,1},{4,6},{5,7},{6,4},{7,5},{8,10},{9,11},{10,... | collective-permute-start | bytes 1966088 | tf_op jit(solution)/shard_map/ppermute | solution.py:40
  111.5 23.3 %collective-permute-start.12 = (bf16[128,1280]{1,0:T(8,128)(2,1)}, bf16[128,1280]{1,0:T(8,128)(2,1)S(1)}, u32[]{:S(2)}, u32[]{:S(2)}) collective-permute-start(bf16[128,1280]{1,0:T(8,128)(2,1)} %get-tuple-element.139), channel_id=1, source_target_pairs={{0,4},{4,0},{1,5},{5,1},{2,6},{6,2},{3,7},{7,3},{8,12},{12,8},{9,1... | collective-permute-start | bytes 983048 | tf_op jit(solution)/shard_map/ppermute | solution.py:32
  112.5 28.8 %collective-permute-start.13 = (bf16[128,1280]{1,0:T(8,128)(2,1)}, bf16[128,1280]{1,0:T(8,128)(2,1)S(1)}, u32[]{:S(2)}, u32[]{:S(2)}) collective-permute-start(bf16[128,1280]{1,0:T(8,128)(2,1)} %get-tuple-element.140), channel_id=1, source_target_pairs={{0,4},{4,0},{1,5},{5,1},{2,6},{6,2},{3,7},{7,3},{8,12},{12,8},{9,1... | collective-permute-start | bytes 983048 | tf_op jit(solution)/shard_map/ppermute | solution.py:32
  163.4 15.9 %collective-permute-start.17 = (bf16[128,2560]{1,0:T(8,128)(2,1)S(1)}, bf16[128,2560]{1,0:T(8,128)(2,1)S(1)}, u32[]{:S(2)}, u32[]{:S(2)}) collective-permute-start(bf16[128,2560]{1,0:T(8,128)(2,1)S(1)} %pad_maximum_fusion.8), channel_id=1, source_target_pairs={{0,4},{4,0},{1,5},{5,1},{2,6},{6,2},{3,7},{7,3},{8,12},{12,8},{9,1... | collective-permute-start | bytes 1966088 | tf_op jit(solution)/shard_map/ppermute | solution.py:32
  164.5 15.5 %collective-permute-start.19 = (bf16[128,2560]{1,0:T(8,128)(2,1)S(1)}, bf16[128,2560]{1,0:T(8,128)(2,1)S(1)}, u32[]{:S(2)}, u32[]{:S(2)}) collective-permute-start(bf16[128,2560]{1,0:T(8,128)(2,1)S(1)} %pad_maximum_fusion.9), channel_id=1, source_target_pairs={{0,2},{1,3},{2,0},{3,1},{4,6},{5,7},{6,4},{7,5},{8,10},{9,11},{10,... | collective-permute-start | bytes 1966088 | tf_op jit(solution)/shard_map/ppermute | solution.py:40
  165.1 14.2 %collective-permute-start.20 = (bf16[1280]{0:T(1024)(128)(2,1)S(1)}, bf16[1280]{0:T(1024)(128)(2,1)S(1)}, u32[]{:S(2)}, u32[]{:S(2)}) collective-permute-start(bf16[1280]{0:T(1024)(128)(2,1)S(1)} %copy-done.85), channel_id=1, source_target_pairs={{0,4},{4,0},{1,5},{5,1},{2,6},{6,2},{3,7},{7,3},{8,12},{12,8},{9,1... | collective-permute-start | bytes 7688 | tf_op jit(solution)/shard_map/ppermute | solution.py:32
  182.8 400.1 %all-gather.8.cloned.1.call-start = ((), (), s32[]{:S(2)}) async-start(), calls=%async_computation.2 | async-start | bytes 21626880 | tf_op jit(solution)/shard_map/all_gather | solution.py:450
  188.6 14.9 %collective-permute-start.21 = (bf16[128,2560]{1,0:T(8,128)(2,1)}, bf16[128,2560]{1,0:T(8,128)(2,1)}, u32[]{:S(2)}, u32[]{:S(2)}) collective-permute-start(bf16[128,2560]{1,0:T(8,128)(2,1)} %multiply_convert_fusion.7), channel_id=1, source_target_pairs={{0,4},{4,0},{1,5},{5,1},{2,6},{6,2},{3,7},{7,3},{8,12},{12,8},{9,1... | collective-permute-start | bytes 1966088 | tf_op jit(solution)/shard_map/ppermute | solution.py:32
  189.6 14.7 %collective-permute-start.22 = (bf16[128,2560]{1,0:T(8,128)(2,1)}, bf16[128,2560]{1,0:T(8,128)(2,1)}, u32[]{:S(2)}, u32[]{:S(2)}) collective-permute-start(bf16[128,2560]{1,0:T(8,128)(2,1)} %multiply_convert_fusion.7), channel_id=1, source_target_pairs={{0,2},{1,3},{2,0},{3,1},{4,6},{5,7},{6,4},{7,5},{8,10},{9,11},{10,... | collective-permute-start | bytes 1966088 | tf_op jit(solution)/shard_map/ppermute | solution.py:40
  214.7 36.3 %collective-permute-start.26 = (bf16[128,2560]{1,0:T(8,128)(2,1)S(1)}, bf16[128,2560]{1,0:T(8,128)(2,1)S(1)}, u32[]{:S(2)}, u32[]{:S(2)}) collective-permute-start(bf16[128,2560]{1,0:T(8,128)(2,1)S(1)} %fusion.23), channel_id=1, source_target_pairs={{0,4},{4,0},{1,5},{5,1},{2,6},{6,2},{3,7},{7,3},{8,12},{12,8},{9,1... | collective-permute-start | bytes 1966088 | tf_op jit(solution)/shard_map/ppermute | solution.py:32
  216.2 34.8 %collective-permute-start.27 = (bf16[128,2560]{1,0:T(8,128)(2,1)S(1)}, bf16[128,2560]{1,0:T(8,128)(2,1)S(1)}, u32[]{:S(2)}, u32[]{:S(2)}) collective-permute-start(bf16[128,2560]{1,0:T(8,128)(2,1)S(1)} %fusion.23), channel_id=1, source_target_pairs={{0,2},{1,3},{2,0},{3,1},{4,6},{5,7},{6,4},{7,5},{8,10},{9,11},{10,... | collective-permute-start | bytes 1966088 | tf_op jit(solution)/shard_map/ppermute | solution.py:40
  218.8 25.5 %collective-permute-start.23 = (bf16[64,2560]{1,0:T(8,128)(2,1)S(1)}, bf16[64,2560]{1,0:T(8,128)(2,1)S(1)}, u32[]{:S(2)}, u32[]{:S(2)}) collective-permute-start(bf16[64,2560]{1,0:T(8,128)(2,1)S(1)} %slice.409), channel_id=1, source_target_pairs={{0,2},{1,3},{2,0},{3,1},{4,6},{5,7},{6,4},{7,5},{8,10},{9,11},{10,... | collective-permute-start | bytes 983048 | tf_op jit(solution)/shard_map/ppermute | solution.py:40
  220.5 23.8 %collective-permute-start.24 = (bf16[64,2560]{1,0:T(8,128)(2,1)S(1)}, bf16[64,2560]{1,0:T(8,128)(2,1)S(1)}, u32[]{:S(2)}, u32[]{:S(2)}) collective-permute-start(bf16[64,2560]{1,0:T(8,128)(2,1)S(1)} %slice.410), channel_id=1, source_target_pairs={{0,4},{4,0},{1,5},{5,1},{2,6},{6,2},{3,7},{7,3},{8,12},{12,8},{9,1... | collective-permute-start | bytes 983048 | tf_op jit(solution)/shard_map/ppermute | solution.py:32
  251.1 17.2 %collective-permute-start.28 = (bf16[64,2560]{1,0:T(8,128)(2,1)S(1)}, bf16[64,2560]{1,0:T(8,128)(2,1)S(1)}, u32[]{:S(2)}, u32[]{:S(2)}) collective-permute-start(bf16[64,2560]{1,0:T(8,128)(2,1)S(1)} %slice.411), channel_id=1, source_target_pairs={{0,2},{1,3},{2,0},{3,1},{4,6},{5,7},{6,4},{7,5},{8,10},{9,11},{10,... | collective-permute-start | bytes 983048 | tf_op jit(solution)/shard_map/ppermute | solution.py:40
  252.6 17.4 %collective-permute-start.29 = (bf16[64,2560]{1,0:T(8,128)(2,1)S(1)}, bf16[64,2560]{1,0:T(8,128)(2,1)S(1)}, u32[]{:S(2)}, u32[]{:S(2)}) collective-permute-start(bf16[64,2560]{1,0:T(8,128)(2,1)S(1)} %slice.412), channel_id=1, source_target_pairs={{0,4},{4,0},{1,5},{5,1},{2,6},{6,2},{3,7},{7,3},{8,12},{12,8},{9,1... | collective-permute-start | bytes 983048 | tf_op jit(solution)/shard_map/ppermute | solution.py:32
  315.7 17.4 %collective-permute-start.32 = (bf16[64,2560]{1,0:T(8,128)(2,1)S(1)}, bf16[64,2560]{1,0:T(8,128)(2,1)S(1)}, u32[]{:S(2)}, u32[]{:S(2)}) collective-permute-start(bf16[64,2560]{1,0:T(8,128)(2,1)S(1)} %get-tuple-element.271), channel_id=1, source_target_pairs={{0,2},{1,3},{2,0},{3,1},{4,6},{5,7},{6,4},{7,5},{8,10},{9,11},{10,... | collective-permute-start | bytes 983048 | tf_op jit(solution)/shard_map/ppermute | solution.py:40
  317.2 17.2 %collective-permute-start.34 = (bf16[64,2560]{1,0:T(8,128)(2,1)S(1)}, bf16[64,2560]{1,0:T(8,128)(2,1)S(1)}, u32[]{:S(2)}, u32[]{:S(2)}) collective-permute-start(bf16[64,2560]{1,0:T(8,128)(2,1)S(1)} %get-tuple-element.270), channel_id=1, source_target_pairs={{0,4},{4,0},{1,5},{5,1},{2,6},{6,2},{3,7},{7,3},{8,12},{12,8},{9,1... | collective-permute-start | bytes 983048 | tf_op jit(solution)/shard_map/ppermute | solution.py:32
  334.6 20.7 %collective-permute-start.33 = (bf16[128,2560]{1,0:T(8,128)(2,1)S(1)}, bf16[128,2560]{1,0:T(8,128)(2,1)S(1)}, u32[]{:S(2)}, u32[]{:S(2)}) collective-permute-start(bf16[128,2560]{1,0:T(8,128)(2,1)S(1)} %pad_maximum_fusion.10), channel_id=1, source_target_pairs={{0,4},{4,0},{1,5},{5,1},{2,6},{6,2},{3,7},{7,3},{8,12},{12,8},{9,1... | collective-permute-start | bytes 1966088 | tf_op jit(solution)/shard_map/ppermute | solution.py:32
  335.6 19.8 %collective-permute-start.35 = (bf16[128,2560]{1,0:T(8,128)(2,1)S(1)}, bf16[128,2560]{1,0:T(8,128)(2,1)S(1)}, u32[]{:S(2)}, u32[]{:S(2)}) collective-permute-start(bf16[128,2560]{1,0:T(8,128)(2,1)S(1)} %pad_maximum_fusion.11), channel_id=1, source_target_pairs={{0,2},{1,3},{2,0},{3,1},{4,6},{5,7},{6,4},{7,5},{8,10},{9,11},{10,... | collective-permute-start | bytes 1966088 | tf_op jit(solution)/shard_map/ppermute | solution.py:40
  357.8 16.2 %collective-permute-start.36 = (bf16[128,2560]{1,0:T(8,128)(2,1)S(1)}, bf16[128,2560]{1,0:T(8,128)(2,1)S(1)}, u32[]{:S(2)}, u32[]{:S(2)}) collective-permute-start(bf16[128,2560]{1,0:T(8,128)(2,1)S(1)} %get-tuple-element.171), channel_id=1, source_target_pairs={{0,4},{4,0},{1,5},{5,1},{2,6},{6,2},{3,7},{7,3},{8,12},{12,8},{9,1... | collective-permute-start | bytes 1966088 | tf_op jit(solution)/shard_map/ppermute | solution.py:32
  359.2 15.9 %collective-permute-start.37 = (bf16[128,2560]{1,0:T(8,128)(2,1)S(1)}, bf16[128,2560]{1,0:T(8,128)(2,1)S(1)}, u32[]{:S(2)}, u32[]{:S(2)}) collective-permute-start(bf16[128,2560]{1,0:T(8,128)(2,1)S(1)} %get-tuple-element.171), channel_id=1, source_target_pairs={{0,2},{1,3},{2,0},{3,1},{4,6},{5,7},{6,4},{7,5},{8,10},{9,11},{10,... | collective-permute-start | bytes 1966088 | tf_op jit(solution)/shard_map/ppermute | solution.py:40
  375.1 11.9 %collective-permute-start.38 = (bf16[64,2560]{1,0:T(8,128)(2,1)S(1)}, bf16[64,2560]{1,0:T(8,128)(2,1)S(1)}, u32[]{:S(2)}, u32[]{:S(2)}) collective-permute-start(bf16[64,2560]{1,0:T(8,128)(2,1)S(1)} %slice.428), channel_id=1, source_target_pairs={{0,2},{1,3},{2,0},{3,1},{4,6},{5,7},{6,4},{7,5},{8,10},{9,11},{10,... | collective-permute-start | bytes 983048 | tf_op jit(solution)/shard_map/ppermute | solution.py:40
  393.7 181.0 %collective-permute-start.66 = (bf16[512,1280]{1,0:T(8,128)(2,1)}, bf16[512,1280]{1,0:T(8,128)(2,1)}, u32[]{:S(2)}, u32[]{:S(2)}) collective-permute-start(bf16[512,1280]{1,0:T(8,128)(2,1)} %pad_maximum_fusion.5), channel_id=1, source_target_pairs={{0,1},{1,0},{2,3},{3,2},{4,5},{5,4},{6,7},{7,6},{8,9},{9,8},{10,11... | collective-permute-start | bytes 3932168 | tf_op jit(solution)/shard_map/ppermute | solution.py:36
  395.4 18.8 %collective-permute-start.49 = (bf16[128,1280]{1,0:T(8,128)(2,1)S(1)}, bf16[128,1280]{1,0:T(8,128)(2,1)S(1)}, u32[]{:S(2)}, u32[]{:S(2)}) collective-permute-start(bf16[128,1280]{1,0:T(8,128)(2,1)S(1)} %dynamic-slice_convert_fusion), channel_id=1, source_target_pairs={{0,4},{4,0},{1,5},{5,1},{2,6},{6,2},{3,7},{7,3},{8,12},{12,8},{9,1... | collective-permute-start | bytes 983048 | tf_op jit(solution)/shard_map/ppermute | solution.py:32
  412.6 32.8 %collective-permute-start.41 = (bf16[320,1280]{1,0:T(8,128)(2,1)}, bf16[320,1280]{1,0:T(8,128)(2,1)}, u32[]{:S(2)}, u32[]{:S(2)}) collective-permute-start(bf16[320,1280]{1,0:T(8,128)(2,1)} %get-tuple-element.283), channel_id=1, source_target_pairs={{0,4},{4,0},{1,5},{5,1},{2,6},{6,2},{3,7},{7,3},{8,12},{12,8},{9,1... | collective-permute-start | bytes 2457608 | tf_op jit(solution)/shard_map/ppermute | solution.py:32
  450.3 33.1 %collective-permute-start.42 = (bf16[512,1152]{1,0:T(8,128)(2,1)S(1)}, bf16[512,1152]{1,0:T(8,128)(2,1)S(1)}, u32[]{:S(2)}, u32[]{:S(2)}) collective-permute-start(bf16[512,1152]{1,0:T(8,128)(2,1)S(1)} %slice.504), channel_id=1, source_target_pairs={{0,1},{1,0},{2,3},{3,2},{4,5},{5,4},{6,7},{7,6},{8,9},{9,8},{10,11... | collective-permute-start | bytes 3538952 | tf_op jit(solution)/shard_map/ppermute | solution.py:36
  452.6 14.7 %collective-permute-start.54 = (bf16[256,640]{1,0:T(8,128)(2,1)S(1)}, bf16[256,640]{1,0:T(8,128)(2,1)S(1)}, u32[]{:S(2)}, u32[]{:S(2)}) collective-permute-start(bf16[256,640]{1,0:T(8,128)(2,1)S(1)} %fusion.32), channel_id=1, source_target_pairs={{0,4},{4,0},{1,5},{5,1},{2,6},{6,2},{3,7},{7,3},{8,12},{12,8},{9,1... | collective-permute-start | bytes 983048 | tf_op jit(solution)/shard_map/ppermute | solution.py:32
  455.4 26.8 %collective-permute-start.51 = (bf16[384,480]{0,1:T(8,128)(2,1)S(1)}, bf16[384,480]{0,1:T(8,128)(2,1)S(1)}, u32[]{:S(2)}, u32[]{:S(2)}) collective-permute-start(bf16[384,480]{0,1:T(8,128)(2,1)S(1)} %get-tuple-element.298), channel_id=1, source_target_pairs={{0,4},{4,0},{1,5},{5,1},{2,6},{6,2},{3,7},{7,3},{8,12},{12,8},{9,1... | collective-permute-start | bytes 1105928 | tf_op jit(solution)/shard_map/ppermute | solution.py:32
  458.8 92.0 %collective-permute-start.48 = (bf16[640,1280]{1,0:T(8,128)(2,1)S(1)}, bf16[640,1280]{1,0:T(8,128)(2,1)}, u32[]{:S(2)}, u32[]{:S(2)}) collective-permute-start(bf16[640,1280]{1,0:T(8,128)(2,1)S(1)} %maximum_select_fusion.7), channel_id=1, source_target_pairs={{0,8},{24,16},{1,9},{25,17},{2,10},{26,18},{3,11},{27,19},{4,12},{... | collective-permute-start | bytes 4915208 | tf_op jit(solution)/shard_map/ppermute | solution.py:311
  495.5 24.5 %collective-permute-start.45 = (bf16[128,1152]{1,0:T(8,128)(2,1)S(1)}, bf16[128,1152]{1,0:T(8,128)(2,1)S(1)}, u32[]{:S(2)}, u32[]{:S(2)}) collective-permute-start(bf16[128,1152]{1,0:T(8,128)(2,1)S(1)} %pad_maximum_fusion.17), channel_id=1, source_target_pairs={{0,4},{4,0},{1,5},{5,1},{2,6},{6,2},{3,7},{7,3},{8,12},{12,8},{9,1... | collective-permute-start | bytes 884744 | tf_op jit(solution)/shard_map/ppermute | solution.py:32
  495.9 24.1 %collective-permute-start.46 = (bf16[128,1152]{1,0:T(8,128)(2,1)S(1)}, bf16[128,1152]{1,0:T(8,128)(2,1)S(1)}, u32[]{:S(2)}, u32[]{:S(2)}) collective-permute-start(bf16[128,1152]{1,0:T(8,128)(2,1)S(1)} %pad_maximum_fusion.18), channel_id=1, source_target_pairs={{0,2},{1,3},{2,0},{3,1},{4,6},{5,7},{6,4},{7,5},{8,10},{9,11},{10,... | collective-permute-start | bytes 884744 | tf_op jit(solution)/shard_map/ppermute | solution.py:40
  523.3 27.5 %collective-permute-start.47 = (bf16[128,1056]{1,0:T(8,128)(2,1)S(1)}, bf16[128,1056]{1,0:T(8,128)(2,1)S(1)}, u32[]{:S(2)}, u32[]{:S(2)}) collective-permute-start(bf16[128,1056]{1,0:T(8,128)(2,1)S(1)} %concatenate.314), channel_id=1, source_target_pairs={{0,4},{4,0},{1,5},{5,1},{2,6},{6,2},{3,7},{7,3},{8,12},{12,8},{9,1... | collective-permute-start | bytes 811016 | tf_op jit(solution)/shard_map/ppermute | solution.py:32
  524.7 26.1 %collective-permute-start.50 = (f32[1,128]{1,0:T(1,128)S(1)}, f32[1,128]{1,0:T(1,128)S(1)}, u32[]{:S(2)}, u32[]{:S(2)}) collective-permute-start(f32[1,128]{1,0:T(1,128)S(1)} %bitcast.97), channel_id=1, source_target_pairs={{0,4},{4,0},{1,5},{5,1},{2,6},{6,2},{3,7},{7,3},{8,12},{12,8},{9,1... | collective-permute-start | bytes 1544 | tf_op jit(solution)/shard_map/ppermute | solution.py:32
  527.4 30.4 %collective-permute-start.55 = (bf16[512,2560]{1,0:T(8,128)(2,1)S(1)}, bf16[512,2560]{1,0:T(8,128)(2,1)S(1)}, u32[]{:S(2)}, u32[]{:S(2)}) collective-permute-start(bf16[512,2560]{1,0:T(8,128)(2,1)S(1)} %slice.457), channel_id=1, source_target_pairs={{0,1},{1,0},{2,3},{3,2},{4,5},{5,4},{6,7},{7,6},{8,9},{9,8},{10,11... | collective-permute-start | bytes 7864328 | tf_op jit(solution)/shard_map/ppermute | solution.py:36
  555.5 20.1 %collective-permute-start.63 = (bf16[256,264]{1,0:T(8,128)(2,1)S(1)}, bf16[256,264]{1,0:T(8,128)(2,1)S(1)}, u32[]{:S(2)}, u32[]{:S(2)}) collective-permute-start(bf16[256,264]{1,0:T(8,128)(2,1)S(1)} %get-tuple-element.328), channel_id=1, source_target_pairs={{0,2},{1,3},{2,0},{3,1},{4,6},{5,7},{6,4},{7,5},{8,10},{9,11},{10,... | collective-permute-start | bytes 405512 | tf_op jit(solution)/shard_map/ppermute | solution.py:40
  564.7 12.8 %collective-permute-start.64 = (bf16[256,264]{1,0:T(8,128)(2,1)S(1)}, bf16[256,264]{1,0:T(8,128)(2,1)S(1)}, u32[]{:S(2)}, u32[]{:S(2)}) collective-permute-start(bf16[256,264]{1,0:T(8,128)(2,1)S(1)} %get-tuple-element.327), channel_id=1, source_target_pairs={{0,1},{1,0},{2,3},{3,2},{4,5},{5,4},{6,7},{7,6},{8,9},{9,8},{10,11... | collective-permute-start | bytes 405512 | tf_op jit(solution)/shard_map/ppermute | solution.py:36
  574.7 17.5 %collective-permute-start.57 = (bf16[128,2560]{1,0:T(8,128)(2,1)}, bf16[128,2560]{1,0:T(8,128)(2,1)}, u32[]{:S(2)}, u32[]{:S(2)}) collective-permute-start(bf16[128,2560]{1,0:T(8,128)(2,1)} %pad_maximum_fusion.12), channel_id=1, source_target_pairs={{0,4},{4,0},{1,5},{5,1},{2,6},{6,2},{3,7},{7,3},{8,12},{12,8},{9,1... | collective-permute-start | bytes 1966088 | tf_op jit(solution)/shard_map/ppermute | solution.py:32
  574.9 17.4 %collective-permute-start.59 = (bf16[128,2560]{1,0:T(8,128)(2,1)}, bf16[128,2560]{1,0:T(8,128)(2,1)}, u32[]{:S(2)}, u32[]{:S(2)}) collective-permute-start(bf16[128,2560]{1,0:T(8,128)(2,1)} %pad_maximum_fusion.13), channel_id=1, source_target_pairs={{0,2},{1,3},{2,0},{3,1},{4,6},{5,7},{6,4},{7,5},{8,10},{9,11},{10,... | collective-permute-start | bytes 1966088 | tf_op jit(solution)/shard_map/ppermute | solution.py:40
  575.7 45.3 %collective-permute-start.52 = (bf16[640,1280]{1,0:T(8,128)(2,1)S(1)}, bf16[640,1280]{1,0:T(8,128)(2,1)}, u32[]{:S(2)}, u32[]{:S(2)}) collective-permute-start(bf16[640,1280]{1,0:T(8,128)(2,1)S(1)} %copy-done.15), channel_id=1, source_target_pairs={{8,16},{16,8},{9,17},{17,9},{10,18},{18,10},{11,19},{19,11},{12,20... | collective-permute-start | bytes 4915208 | tf_op jit(solution)/shard_map/ppermute | solution.py:315
  582.8 38.2 %collective-permute-start.53 = (bf16[384,960]{0,1:T(8,128)(2,1)}, bf16[384,960]{0,1:T(8,128)(2,1)S(1)}, u32[]{:S(2)}, u32[]{:S(2)}) collective-permute-start(bf16[384,960]{0,1:T(8,128)(2,1)} %maximum_select_fusion.10), channel_id=1, source_target_pairs={{0,8},{24,16},{1,9},{25,17},{2,10},{26,18},{3,11},{27,19},{4,12},{... | collective-permute-start | bytes 2211848 | tf_op jit(solution)/shard_map/ppermute | solution.py:311
  594.4 25.6 %collective-permute-start.60 = (bf16[128,1280]{1,0:T(8,128)(2,1)S(1)}, bf16[128,1280]{1,0:T(8,128)(2,1)S(1)}, u32[]{:S(2)}, u32[]{:S(2)}) collective-permute-start(bf16[128,1280]{1,0:T(8,128)(2,1)S(1)} %get-tuple-element.302), channel_id=1, source_target_pairs={{0,4},{4,0},{1,5},{5,1},{2,6},{6,2},{3,7},{7,3},{8,12},{12,8},{9,1... | collective-permute-start | bytes 983048 | tf_op jit(solution)/shard_map/ppermute | solution.py:32
  621.2 29.0 %collective-permute-start.61 = (bf16[384,960]{0,1:T(8,128)(2,1)S(1)}, bf16[384,960]{0,1:T(8,128)(2,1)}, u32[]{:S(2)}, u32[]{:S(2)}) collective-permute-start(bf16[384,960]{0,1:T(8,128)(2,1)S(1)} %add_convert_fusion.7), channel_id=1, source_target_pairs={{8,16},{16,8},{9,17},{17,9},{10,18},{18,10},{11,19},{19,11},{12,20... | collective-permute-start | bytes 2211848 | tf_op jit(solution)/shard_map/ppermute | solution.py:315
  622.7 27.5 %collective-permute-start.62 = (bf16[256,1280]{1,0:T(8,128)(2,1)S(1)}, bf16[256,1280]{1,0:T(8,128)(2,1)}, u32[]{:S(2)}, u32[]{:S(2)}) collective-permute-start(bf16[256,1280]{1,0:T(8,128)(2,1)S(1)} %copy-done.38), channel_id=1, source_target_pairs={{0,8},{24,16},{1,9},{25,17},{2,10},{26,18},{3,11},{27,19},{4,12},{... | collective-permute-start | bytes 1966088 | tf_op jit(solution)/shard_map/ppermute | solution.py:311
  631.9 86.7 %collective-permute-start.77 = (bf16[640,1280]{1,0:T(8,128)(2,1)}, bf16[640,1280]{1,0:T(8,128)(2,1)}, u32[]{:S(2)}, u32[]{:S(2)}) collective-permute-start(bf16[640,1280]{1,0:T(8,128)(2,1)} %add_convert_fusion.3), channel_id=1, source_target_pairs={{8,0},{16,24},{9,1},{17,25},{10,2},{18,26},{11,3},{19,27},{12,4},{... | collective-permute-start | bytes 4915208 | tf_op jit(solution)/shard_map/ppermute | solution.py:319
  651.5 35.4 %collective-permute-start.70 = (bf16[256,1280]{1,0:T(8,128)(2,1)S(1)}, bf16[256,1280]{1,0:T(8,128)(2,1)S(1)}, u32[]{:S(2)}, u32[]{:S(2)}) collective-permute-start(bf16[256,1280]{1,0:T(8,128)(2,1)S(1)} %add_convert_fusion.11), channel_id=1, source_target_pairs={{8,16},{16,8},{9,17},{17,9},{10,18},{18,10},{11,19},{19,11},{12,20... | collective-permute-start | bytes 1966088 | tf_op jit(solution)/shard_map/ppermute | solution.py:315
  652.2 34.6 %collective-permute-start.71 = (bf16[268,1280]{1,0:T(8,128)(2,1)S(1)}, bf16[268,1280]{1,0:T(8,128)(2,1)S(1)}, u32[]{:S(2)}, u32[]{:S(2)}) collective-permute-start(bf16[268,1280]{1,0:T(8,128)(2,1)S(1)} %copy-done.33), channel_id=1, source_target_pairs={{0,8},{24,16},{1,9},{25,17},{2,10},{26,18},{3,11},{27,19},{4,12},{... | collective-permute-start | bytes 2058248 | tf_op jit(solution)/shard_map/ppermute | solution.py:311
  685.5 31.8 %collective-permute-start.75 = (bf16[384,960]{0,1:T(8,128)(2,1)S(1)}, bf16[384,960]{0,1:T(8,128)(2,1)S(1)}, u32[]{:S(2)}, u32[]{:S(2)}) collective-permute-start(bf16[384,960]{0,1:T(8,128)(2,1)S(1)} %add_convert_fusion.6), channel_id=1, source_target_pairs={{8,0},{16,24},{9,1},{17,25},{10,2},{18,26},{11,3},{19,27},{12,4},{... | collective-permute-start | bytes 2211848 | tf_op jit(solution)/shard_map/ppermute | solution.py:319
  687.0 47.3 %collective-permute-start.72 = (bf16[268,1280]{1,0:T(8,128)(2,1)S(1)}, bf16[268,1280]{1,0:T(8,128)(2,1)S(1)}, u32[]{:S(2)}, u32[]{:S(2)}) collective-permute-start(bf16[268,1280]{1,0:T(8,128)(2,1)S(1)} %add_convert_fusion.9), channel_id=1, source_target_pairs={{8,16},{16,8},{9,17},{17,9},{10,18},{18,10},{11,19},{19,11},{12,20... | collective-permute-start | bytes 2058248 | tf_op jit(solution)/shard_map/ppermute | solution.py:315
  714.1 22.7 %collective-permute-start.73 = (bf16[400,1280]{1,0:T(8,128)(2,1)S(1)}, bf16[400,1280]{1,0:T(8,128)(2,1)}, u32[]{:S(2)}, u32[]{:S(2)}) collective-permute-start(bf16[400,1280]{1,0:T(8,128)(2,1)S(1)} %dynamic_slice.220), channel_id=1, source_target_pairs={{0,4},{4,0},{1,5},{5,1},{2,6},{6,2},{3,7},{7,3},{8,12},{12,8},{9,1... | collective-permute-start | bytes 3072008 | tf_op jit(solution)/shard_map/ppermute | solution.py:32
  714.4 18.8 %collective-permute-start.76 = (bf16[256,1280]{1,0:T(8,128)(2,1)S(1)}, bf16[256,1280]{1,0:T(8,128)(2,1)S(1)}, u32[]{:S(2)}, u32[]{:S(2)}) collective-permute-start(bf16[256,1280]{1,0:T(8,128)(2,1)S(1)} %add_convert_fusion.10), channel_id=1, source_target_pairs={{8,0},{16,24},{9,1},{17,25},{10,2},{18,26},{11,3},{19,27},{12,4},{... | collective-permute-start | bytes 1966088 | tf_op jit(solution)/shard_map/ppermute | solution.py:319
  736.9 32.4 %collective-permute-start.74 = (bf16[268,1280]{1,0:T(8,128)(2,1)S(1)}, bf16[268,1280]{1,0:T(8,128)(2,1)S(1)}, u32[]{:S(2)}, u32[]{:S(2)}) collective-permute-start(bf16[268,1280]{1,0:T(8,128)(2,1)S(1)} %add_convert_fusion.8), channel_id=1, source_target_pairs={{8,0},{16,24},{9,1},{17,25},{10,2},{18,26},{11,3},{19,27},{12,4},{... | collective-permute-start | bytes 2058248 | tf_op jit(solution)/shard_map/ppermute | solution.py:319
  762.9 21.9 %collective-permute-start.79 = (bf16[400,1280]{1,0:T(8,128)(2,1)}, bf16[400,1280]{1,0:T(8,128)(2,1)}, u32[]{:S(2)}, u32[]{:S(2)}) collective-permute-start(bf16[400,1280]{1,0:T(8,128)(2,1)} %dynamic_slice.223), channel_id=1, source_target_pairs={{0,4},{4,0},{1,5},{5,1},{2,6},{6,2},{3,7},{7,3},{8,12},{12,8},{9,1... | collective-permute-start | bytes 3072008 | tf_op jit(solution)/shard_map/ppermute | solution.py:32
  763.2 24.0 %collective-permute-start.78 = (bf16[400,1280]{1,0:T(8,128)(2,1)}, bf16[400,1280]{1,0:T(8,128)(2,1)}, u32[]{:S(2)}, u32[]{:S(2)}) collective-permute-start(bf16[400,1280]{1,0:T(8,128)(2,1)} %collective-permute-done.73), channel_id=1, source_target_pairs={{0,8},{8,0},{16,24},{24,16},{1,9},{9,1},{17,25},{25,17},{2,10},{10... | collective-permute-start | bytes 3072008 | tf_op jit(solution)/shard_map/ppermute | solution.py:584
  788.9 20.1 %collective-permute-start.81 = (bf16[400,1280]{1,0:T(8,128)(2,1)S(1)}, bf16[400,1280]{1,0:T(8,128)(2,1)S(1)}, u32[]{:S(2)}, u32[]{:S(2)}) collective-permute-start(bf16[400,1280]{1,0:T(8,128)(2,1)S(1)} %dynamic_slice.226), channel_id=1, source_target_pairs={{0,4},{4,0},{1,5},{5,1},{2,6},{6,2},{3,7},{7,3},{8,12},{12,8},{9,1... | collective-permute-start | bytes 3072008 | tf_op jit(solution)/shard_map/ppermute | solution.py:32
  790.5 23.5 %collective-permute-start.80 = (bf16[400,1280]{1,0:T(8,128)(2,1)}, bf16[400,1280]{1,0:T(8,128)(2,1)S(1)}, u32[]{:S(2)}, u32[]{:S(2)}) collective-permute-start(bf16[400,1280]{1,0:T(8,128)(2,1)} %collective-permute-done.79), channel_id=1, source_target_pairs={{0,8},{8,0},{16,24},{24,16},{1,9},{9,1},{17,25},{25,17},{2,10},{10... | collective-permute-start | bytes 3072008 | tf_op jit(solution)/shard_map/ppermute | solution.py:584
  809.0 23.0 %collective-permute-start.82 = (bf16[400,1280]{1,0:T(8,128)(2,1)S(1)}, bf16[400,1280]{1,0:T(8,128)(2,1)S(1)}, u32[]{:S(2)}, u32[]{:S(2)}) collective-permute-start(bf16[400,1280]{1,0:T(8,128)(2,1)S(1)} %collective-permute-done.81), channel_id=1, source_target_pairs={{0,8},{8,0},{16,24},{24,16},{1,9},{9,1},{17,25},{25,17},{2,10},{10... | collective-permute-start | bytes 3072008 | tf_op jit(solution)/shard_map/ppermute | solution.py:584
  (128 other events, 1564.5 us)
Sparse Core Ops, SparseCore 0:
  100.9 113.8 all-gather.3
  218.1 154.6 all-gather.5
  375.7 172.7 all-gather.7

commit v3 on v2

--- a/solution.py
+++ b/solution.py
@@ -344,6 +344,7 @@
     count = units // dp_size
     wanted = [rows_at(t, (1 - row) * units + dp_place * count, count) for t in tiles]
     fetched = px(jnp.concatenate(wanted, 0))
+    near_tiles, fetched = together(near_tiles, fetched)
     latent_weights = jnp.concatenate([near_tiles, pc(near_tiles)], 0)
     query_columns = query_up.shape[1] // 2
     w_keyval = half_of(latent_up, 1, row)
@@ -374,7 +375,6 @@
     latent_other, query_other = px(latent_other), px(query_other)
     normed_y = py(normed_half)
     latent_raw = half_of(latent_part, 0, row) + latent_other
-    latent_raw, fetched = together(latent_raw, fetched)
     others = lax.all_gather(fetched, "dp", axis=0, tiled=True)
 
     def in_place(values):
@@ -425,6 +425,8 @@
     )
     incoming = pair(first_x, half_of(cotangent, 0, row), cotangent_other, 1).astype(F32)
     grad_down_own = (RESIDUAL_SCALE * incoming).astype(BF16)
+    if by_factors:
+        grads_all = lax.all_gather(grad_down_own, every, axis=0, tiled=True)
     normed_rows = jnp.concatenate([normed_half, normed_y], 0)
     w_out = pair(first_x, half_of(attention_out, 0, row), out_other, 1)
     stream = pair(first_x, half_of(hidden, 0, row), hidden_other, 1).astype(F32)
@@ -446,8 +448,6 @@
         rows_all = lax.all_gather(normed_mid_own, every, axis=0, tiled=True)
     normed_near = gather_near(normed_mid_own)
     *normed_near, others, normed_rows, grad_down_own = together(*normed_near, others, normed_rows, grad_down_own)
-    if by_factors:
-        grads_all = lax.all_gather(grad_down_own, every, axis=0, tiled=True)
     normed_far = gather_far(*normed_near)
     grad_down_near = gather_near(grad_down_own)
     gate_up = jnp.zeros((2 * units, 2 * half_width), BF16)
@@ -497,12 +497,12 @@
     )
     latent_steps = scatter_far(scatter_core(latent_grad_part))
     if by_factors:
-        *latent_steps, rows_all = together(*latent_steps, rows_all)
-        gate_all = dot(gate_up[:units], rows_all, (1, 1))
+        *latent_steps, grads_all = together(*latent_steps, grads_all)
+        grad_act_all = dot(down, grads_all, (1, 1))
     latent_steps = list(latent_steps)
     latent_grad = scatter_near(*latent_steps)
     if by_factors:
-        latent_grad, gate_all, output_part = together(latent_grad, gate_all, output_part)
+        latent_grad, grad_act_all, output_part = together(latent_grad, grad_act_all, output_part)
     query_latent_grad, kv_latent_grad, query_gain_part, latent_gain_part = latent_back(
         (latent_grad[:, :QR], latent_grad[:, QR : QR + KVR], latent_grad[:, QR + KVR + NOPE : QR + KVR + NOPE + RD])
     )
@@ -527,8 +527,9 @@
     low_other, inner_other = px(latent_low), px(inner_in[None, :])[0]
     if by_factors:
         out_1 = inward(out_part)
-        up_all = dot(gate_up[units:], rows_all, (1, 1))
-        low_other, up_all, out_1 = barrier((low_other, up_all, out_1))
+        output_core = scatter_core(output_part)
+        gate_all = dot(gate_up[:units], rows_all, (1, 1))
+        low_other, gate_all, out_1, output_core = barrier((low_other, gate_all, out_1, output_core))
     latent_low = pair(first_x, latent_low, low_other, 0)
     inner_half = pair(first_x, inner_in, inner_other, 0)
     grad_normed = dot(latent_low, latent_weights, (1, 0))
@@ -541,9 +542,6 @@
     grad_in = inverse_half[:, None] * (grad_normed * gain_in[None, :] - scaled_in * inner_half[:, None])
     input_gradient = (grad_middle_half + grad_in).astype(BF16)
     gain_in_part = jnp.sum(grad_normed * scaled_in, axis=0)
-
-    output_own = (middle + RESIDUAL_SCALE * scatter_plane(output_part)).astype(BF16)
-    output = pair(first_x, half_of(output_own, 1, row), px(half_of(output_own, 1, 1 - row)), 0)
 
     up_part = dot(compressed, query_grad, (0, 0), BF16).reshape(QR, heads, SLOT)[:, :, : NOPE + RD]
     up_part = up_part.reshape(QR, query_columns)
@@ -563,17 +561,19 @@
     gains = jnp.pad(gains, (0, -gain_count % half_width)).reshape(-1, half_width).astype(BF16)
     latent_down_part = jnp.concatenate([latent_down_part, gains], 0)
     if by_factors:
-        input_gradient, grads_all, up_part = barrier((input_gradient, grads_all, up_part))
-        out_2, up_1 = across(*out_1), inward(up_part)
-        grad_act_all = dot(down, grads_all, (1, 1))
-        gate_all, up_all, grad_act_all, out_2, up_1, latent_up_part, output = barrier(
-            (gate_all, up_all, grad_act_all, out_2, up_1, latent_up_part, output)
+        input_gradient, up_part = barrier((input_gradient, up_part))
+        out_2, up_1, output_far = across(*out_1), inward(up_part), scatter_far(output_core)
+        up_all = dot(gate_up[units:], rows_all, (1, 1))
+        gate_all, up_all, out_2, up_1, latent_up_part, output_far = barrier(
+            (gate_all, up_all, out_2, up_1, latent_up_part, output_far)
         )
         out_3, up_2, latent_1 = outward(*out_2), across(*up_1), inward(latent_up_part)
+        output_own = (middle + RESIDUAL_SCALE * scatter_near(*output_far)).astype(BF16)
         act_all, grad_gate_all, grad_up_all = activate(gate_all, up_all, grad_act_all)
-        act_all, grad_gate_all, grad_up_all, up_2, latent_1, latent_down_part = barrier(
-            (act_all, grad_gate_all, grad_up_all, up_2, latent_1, latent_down_part)
+        act_all, grad_gate_all, grad_up_all, up_2, latent_1, latent_down_part, output_own = barrier(
+            (act_all, grad_gate_all, grad_up_all, up_2, latent_1, latent_down_part, output_own)
         )
+        output = pair(first_x, half_of(output_own, 1, row), px(half_of(output_own, 1, 1 - row)), 0)
         up_3, latent_2, down_1 = outward(*up_2), across(*latent_1), inward(latent_down_part)
         own_units = units // 2
 
@@ -610,6 +610,8 @@
             )
         ]
         unit_others = [px(half_of(total, 1, 1 - row)) for total in unit_grads]
+        output_own = (middle + RESIDUAL_SCALE * scatter_plane(output_part)).astype(BF16)
+        output = pair(first_x, half_of(output_own, 1, row), px(half_of(output_own, 1, 1 - row)), 0)
         out_grad, query_up_grad, latent_up_grad, down_total = (
             lax.psum(part, "dp") for part in (out_part, up_part, latent_up_part, latent_down_part)
         )

time: 851 us -> 831 us (0.976)
  waiting for transfers between devices: 263 us -> 236 us
  matrix products: 218 us -> 205 us
    dot_general x20, matrix products: 218 us -> 205 us  [dot(): lax.dot_general(a, b, ((contract[:1], contract[1:]), ((), ())), preferred...]
    ppermute x20, waiting for transfers between devices: 58.4 us -> 46.6 us  [py(): return lax.ppermute(values, 'col', OVER_Y)]
    ppermute x4, waiting for transfers between devices: 11.2 us -> 0.01 us  [outward(): return (total, lax.ppermute(total, 'dp', ((1, 0), (2, 3))))]
    all_gather x1, waiting for transfers between devices: 10.4 us -> 0.01 us  [per_device(): others = lax.all_gather(fetched, 'dp', axis=0, tiled=True)]
    unnamed x249 -> x242, local copies, waits for them, and re-layouts: 37.3 us -> 39.6 us
  transfers between devices with their start and end apart: 86 -> 86, of which waited for: 40 -> 44; matrix products, arithmetic and copies ran while one was open for 46% -> 47% of each run, Pallas kernels for 5% -> 5%
where the time goes in v3:
time: 831 us; the launch traced here: 820 us
  waiting for transfers between devices  236 us (28%)
  matrix products  205 us (25%)
  local copies, waits for them, and re-layouts  115 us (14%)
  starting transfers between devices  103 us (12%)
  other arithmetic  102 us (12%)
  Pallas kernels  43.2 us (5%)
  between operations  15.9 us (2%)
    dot_general x20, matrix products, dot(): lax.dot_general(a, b, ((contract[:1], contract[1:]), ((), ())), preferred...  205 us
    ppermute x35, waiting for transfers between devices, px(): return lax.ppermute(values, 'row', OVER_X)  151 us
    ppermute x20, waiting for transfers between devices, py(): return lax.ppermute(values, 'col', OVER_Y)  46.6 us
    unnamed x242, local copies, waits for them, and re-layouts  39.6 us
    ppermute x35, starting transfers between devices, px(): return lax.ppermute(values, 'row', OVER_X)  38.5 us
    pallas_call x1, Pallas kernels, attend_back(): pl.pallas_call(lambda *refs: attend_back_kernel(heads, *refs), grid=(rows...  25.7 us
    ppermute x20, starting transfers between devices, py(): return lax.ppermute(values, 'col', OVER_Y)  24.1 us
    ppermute x4, starting transfers between devices, inward(): return (part, lax.ppermute(part, 'dp', ((0, 1), (3, 2))))  21 us
  transfers between devices with their start and end apart: 86, of which 44 were waited for; matrix products, arithmetic and copies ran while one was open for 47% of the time, Pallas kernels for 5%

profile of v3, /device:TPU:0, one launch (start us, length us, event | category | flops | bytes accessed | tf_op | source)
XLA Modules:
  0.0 820.1 jit_solution(14574314806141705419)
XLA Ops:
  11.0 2.9 collective-permute-start.2
  19.9 11.9 %collective-permute-done.1 = bf16[264,1280]{1,0:T(8,128)(2,1)} collective-permute-done((bf16[264,1280]{1,0:T(8,128)(2,1)}, bf16[264,1280]{1,0:T(8,128)(2,1)}, u32[]{:S(2)}, u32[]{:S(2)}) %collective-permute-start.1) | collective-permute-done | bytes 675872 | tf_op jit(solution)/shard_map/ppermute | solution.py:40
  34.0 13.8 %collective-permute-done.2 = bf16[600,1280]{1,0:T(8,128)(2,1)} collective-permute-done((bf16[600,1280]{1,0:T(8,128)(2,1)}, bf16[600,1280]{1,0:T(8,128)(2,1)}, u32[]{:S(2)}, u32[]{:S(2)}) %collective-permute-start.2) | collective-permute-done | bytes 1536032 | tf_op jit(solution)/shard_map/ppermute | solution.py:32
  58.1 3.1 fusion.34
  63.7 6.7 collective-permute-done.4
  82.1 4.4 collective-permute-done.5
  117.2 17.5 %attend.1 = (bf16[1024,640]{1,0:T(8,128)(2,1)}, bf16[1024,640]{1,0:T(8,128)(2,1)}, bf16[1024,320]{1,0:T(8,128)(2,1)S(1)}, bf16[1024,320]{1,0:T(8,128)(2,1)S(1)}, f32[1024,8]{1,0:T(8,128)S(1)}) custom-call(bf16[1024,1152]{1,0:T(8,128)(2,1)} %copy-done.76, bf16[1024,1152]{1,0:T(8,128)(2,1)} %copy-done.76, bf16[1024,1152]{1,0:T(8,128)(2,1)} %copy-done.76, ...), custom_call_target="tpu_custom_call" | custom-call | flops 3690987520 | bytes 8388608 | tf_op jit(solution)/shard_map/attend/pallas_call | solution.py:220
  137.9 6.6 collective-permute-done.13
  146.9 5.0 fusion.38
  152.2 4.9 collective-permute-done.15
  159.9 7.8 collective-permute-done.16
  173.4 16.4 %collective-permute-done.20 = bf16[1280]{0:T(1024)(128)(2,1)S(1)} collective-permute-done((bf16[1280]{0:T(1024)(128)(2,1)S(1)}, bf16[1280]{0:T(1024)(128)(2,1)S(1)}, u32[]{:S(2)}, u32[]{:S(2)}) %collective-permute-start.20) | collective-permute-done | bytes 2592 | tf_op jit(solution)/shard_map/ppermute | solution.py:32
  197.8 3.9 broadcast_in_dim.78
  210.6 14.8 %collective-permute-done.21 = bf16[128,2560]{1,0:T(8,128)(2,1)} collective-permute-done((bf16[128,2560]{1,0:T(8,128)(2,1)}, bf16[128,2560]{1,0:T(8,128)(2,1)}, u32[]{:S(2)}, u32[]{:S(2)}) %collective-permute-start.21) | collective-permute-done | bytes 655392 | tf_op jit(solution)/shard_map/ppermute | solution.py:32
  241.2 2.9 collective-permute-done.23
  244.2 6.3 collective-permute-done.24
  259.8 11.2 %fusion.60 = f32[1600,1024]{1,0:T(8,128)S(1)} fusion(bf16[1600,2560]{1,0:T(8,128)(2,1)} %get-tuple-element.263, bf16[1024,2560]{1,0:T(8,128)(2,1)S(1)} %constant_dynamic-update-slice_fusion.21), kind=kOutput, calls=%fused_computation.318 | convolution fusion | flops 8388608000 | bytes 19988480 | tf_op jit(solution)/shard_map/dot_general | solution.py:48
  271.0 4.0 collective-permute-done.28
  277.4 4.9 collective-permute-done.30
  282.5 7.8 multiply_convert_fusion.4
  290.6 12.8 %fusion.61 = bf16[1024,2560]{1,0:T(8,128)(2,1)S(1)} fusion(bf16[1600,1024]{1,0:T(8,128)(2,1)S(1)} %pad_maximum_fusion, bf16[1600,2560]{1,0:T(8,128)(2,1)} %get-tuple-element.263), kind=kOutput, calls=%fused_computation.319 | convolution fusion | flops 8388608000 | bytes 16711680 | tf_op jit(solution)/shard_map/dot_general | solution.py:48
  303.7 4.8 collective-permute-done.31
  310.0 9.1 %collective-permute-done.32 = bf16[64,2560]{1,0:T(8,128)(2,1)S(1)} collective-permute-done((bf16[64,2560]{1,0:T(8,128)(2,1)S(1)}, bf16[64,2560]{1,0:T(8,128)(2,1)S(1)}, u32[]{:S(2)}, u32[]{:S(2)}) %collective-permute-start.32) | collective-permute-done | bytes 327712 | tf_op jit(solution)/shard_map/ppermute | solution.py:40
  321.7 13.8 %collective-permute-done.33 = bf16[128,2560]{1,0:T(8,128)(2,1)S(1)} collective-permute-done((bf16[128,2560]{1,0:T(8,128)(2,1)S(1)}, bf16[128,2560]{1,0:T(8,128)(2,1)S(1)}, u32[]{:S(2)}, u32[]{:S(2)}) %collective-permute-start.33) | collective-permute-done | bytes 655392 | tf_op jit(solution)/shard_map/ppermute | solution.py:32
  341.1 15.1 %collective-permute-done.36 = bf16[128,2560]{1,0:T(8,128)(2,1)S(1)} collective-permute-done((bf16[128,2560]{1,0:T(8,128)(2,1)S(1)}, bf16[128,2560]{1,0:T(8,128)(2,1)S(1)}, u32[]{:S(2)}, u32[]{:S(2)}) %collective-permute-start.36) | collective-permute-done | bytes 655392 | tf_op jit(solution)/shard_map/ppermute | solution.py:32
  358.7 10.0 %fusion.62 = bf16[1024,2560]{1,0:T(8,128)(2,1)} fusion(bf16[800,1024]{1,0:T(8,128)(2,1)S(1)} %get-tuple-element.174, bf16[800,2560]{1,0:T(8,128)(2,1)} %get-tuple-element.262), kind=kOutput, calls=%fused_computation.320 | convolution fusion | flops 4194304000 | bytes 10977280 | tf_op jit(solution)/shard_map/dot_general | solution.py:48
  368.7 3.3 collective-permute-done.38
  385.6 3.6 constant_dynamic-update-slice_fusion.43
  389.2 4.5 fusion.63
  393.8 4.2 fusion.37
  407.3 25.7 %attend_back.1 = (bf16[1024,640]{1,0:T(8,128)(2,1)}, bf16[1024,640]{1,0:T(8,128)(2,1)}, bf16[1024,128]{1,0:T(8,128)(2,1)S(1)}) custom-call(bf16[1024,640]{1,0:T(8,128)(2,1)} %get-tuple-element.137.refs_0_, bf16[1024,640]{1,0:T(8,128)(2,1)} %get-tuple-element.138.refs_1_, bf16[1024,320]{1,0:T(8,128)(2,1)S(1)} %copy-done.7, f32[1024,8]{1,0:T(8,128)S(1)} %copy-done.9, ...), custom_call_target="tpu_custom_call" | custom-call | flops 6710886400 | bytes 8388608 | tf_op jit(solution)/shard_map/attend_back/pallas_call | solution.py:253
  433.0 2.7 collective-permute-done.41
  437.7 2.7 fusion.64
  447.7 3.1 maximum_select_fusion.7
  450.7 3.8 collective-permute-start.48
  454.5 6.3 collective-permute-done.55
  461.8 10.3 %collective-permute-done.53 = bf16[384,480]{0,1:T(8,128)(2,1)S(1)} collective-permute-done((bf16[384,480]{0,1:T(8,128)(2,1)S(1)}, bf16[384,480]{0,1:T(8,128)(2,1)S(1)}, u32[]{:S(2)}, u32[]{:S(2)}) %collective-permute-start.53) | collective-permute-done | bytes 368672 | tf_op jit(solution)/shard_map/ppermute | solution.py:32
  476.1 2.8 collective-permute-done.43
  481.8 23.1 %fusion.66 = f32[800,4096]{1,0:T(8,128)} fusion(bf16[800,2560]{1,0:T(8,128)(2,1)} %get-tuple-element.262, bf16[4096,2560]{1,0:T(8,128)(2,1)} %all-gather.6.cloned.1.call-done), kind=kOutput, calls=%fused_computation.324 | convolution fusion | flops 16777216000 | bytes 38174720 | tf_op jit(solution)/shard_map/dot_general | solution.py:48
  505.1 3.6 slice.453
  514.6 3.2 add_convert_fusion
  517.9 23.3 %fusion.3 = f32[800,4096]{1,0:T(8,128)} fusion(bf16[4096,2560]{1,0:T(8,128)(2,1)} %all-gather.8.cloned.1.call-done, bf16[1600,2560]{1,0:T(8,128)(2,1)} %get-tuple-element.263), kind=kOutput, calls=%fused_computation.12 | convolution fusion | flops 16777216000 | bytes 38174720 | tf_op jit(solution)/shard_map/dot_general | solution.py:48
  544.8 4.7 collective-permute-start.54
  549.4 3.5 add_convert_fusion.4
  559.2 23.4 %fusion.1 = f32[800,4096]{1,0:T(8,128)} fusion(bf16[4096,2560]{1,0:T(8,128)(2,1)} %all-gather.8.cloned.1.call-done, bf16[1600,2560]{1,0:T(8,128)(2,1)} %get-tuple-element.263), kind=kOutput, calls=%fused_computation.10 | convolution fusion | flops 16777216000 | bytes 38174720 | tf_op jit(solution)/shard_map/dot_general | solution.py:48
  588.8 4.9 collective-permute-done.62
  593.8 2.9 fusion.7
  597.2 2.8 collective-permute-done.57
  607.6 4.0 collective-permute-start.59
  611.6 3.5 add_convert_fusion.3
  616.6 16.7 %multiply_convert_fusion = (bf16[800,4096]{1,0:T(8,128)(2,1)}, bf16[800,4096]{1,0:T(8,128)(2,1)S(1)}, bf16[800,4096]{1,0:T(8,128)(2,1)}) fusion(f32[800,4096]{1,0:T(8,128)} %fusion.66, f32[800,4096]{1,0:T(8,128)} %fusion.3, f32[800,4096]{1,0:T(8,128)S(1)} %copy-done.13), kind=kLoop, calls=%fused_computation | loop fusion | flops 49152000 | bytes 58982400 | tf_op jit(solution)/shard_map/convert_element_type | solution.py:282
  636.9 8.6 %collective-permute-start.71 = (bf16[268,1280]{1,0:T(8,128)(2,1)S(1)}, bf16[268,1280]{1,0:T(8,128)(2,1)S(1)}, u32[]{:S(2)}, u32[]{:S(2)}) collective-permute-start(bf16[268,1280]{1,0:T(8,128)(2,1)S(1)} %pad_maximum_fusion.5), channel_id=1, source_target_pairs={{0,8},{24,16},{1,9},{25,17},{2,10},{26,18},{3,11},{27,19},{4,12},{... | collective-permute-start | bytes 2058248 | tf_op jit(solution)/shard_map/ppermute | solution.py:311
  648.5 21.9 %fusion.67 = bf16[800,2560]{1,0:T(8,128)(2,1)S(1)} fusion(bf16[800,4096]{1,0:T(8,128)(2,1)} %get-tuple-element.218, bf16[4096,2560]{1,0:T(8,128)(2,1)} %all-gather.8.cloned.1.call-done), kind=kOutput, calls=%fused_computation.325 | convolution fusion | flops 16777216000 | bytes 31621120 | tf_op jit(solution)/shard_map/dot_general | solution.py:48
  679.9 22.6 %fusion.68 = bf16[800,2560]{1,0:T(8,128)(2,1)} fusion(bf16[800,4096]{1,0:T(8,128)(2,1)S(1)} %get-tuple-element.223, bf16[4096,2560]{1,0:T(8,128)(2,1)} %all-gather.8.cloned.1.call-done), kind=kOutput, calls=%fused_computation.326 | convolution fusion | flops 16777216000 | bytes 31621120 | tf_op jit(solution)/shard_map/dot_general | solution.py:48
  706.8 3.5 select_convert_fusion
  715.6 22.5 %fusion.69 = bf16[800,2560]{1,0:T(8,128)(2,1)} fusion(bf16[800,4096]{1,0:T(8,128)(2,1)S(1)} %bitcast.79, bf16[4096,2560]{1,0:T(8,128)(2,1)} %all-gather.6.cloned.1.call-done), kind=kOutput, calls=%fused_computation.327 | convolution fusion | flops 16777216000 | bytes 31621120 | tf_op jit(solution)/shard_map/dot_general | solution.py:48
  739.8 3.0 collective-permute-start.78
  748.6 13.2 %collective-permute-done.79 = bf16[400,1280]{1,0:T(8,128)(2,1)} collective-permute-done((bf16[400,1280]{1,0:T(8,128)(2,1)}, bf16[400,1280]{1,0:T(8,128)(2,1)}, u32[]{:S(2)}, u32[]{:S(2)}) %collective-permute-start.79) | collective-permute-done | bytes 1024032 | tf_op jit(solution)/shard_map/ppermute | solution.py:32
  768.0 2.7 maximum_select_fusion.4
  770.8 3.9 convert_bitcast_fusion
  774.7 11.2 %collective-permute-done.81 = bf16[400,1280]{1,0:T(8,128)(2,1)S(1)} collective-permute-done((bf16[400,1280]{1,0:T(8,128)(2,1)S(1)}, bf16[400,1280]{1,0:T(8,128)(2,1)S(1)}, u32[]{:S(2)}, u32[]{:S(2)}) %collective-permute-start.81) | collective-permute-done | bytes 1024032 | tf_op jit(solution)/shard_map/ppermute | solution.py:32
  791.7 3.7 convert_bitcast_fusion.1
  795.5 13.3 %collective-permute-done.82 = bf16[400,1280]{1,0:T(8,128)(2,1)S(1)} collective-permute-done((bf16[400,1280]{1,0:T(8,128)(2,1)S(1)}, bf16[400,1280]{1,0:T(8,128)(2,1)S(1)}, u32[]{:S(2)}, u32[]{:S(2)}) %collective-permute-start.82) | collective-permute-done | bytes 1024032 | tf_op jit(solution)/shard_map/ppermute | solution.py:584
  809.6 3.7 fusion.5
  (591 shorter events, 255.5 us)
Async XLA Ops:
  7.2 218.2 %all-gather.4.cloned.1.call-start = ((), (), s32[]{:S(2)}) async-start(), calls=%async_computation | async-start | bytes 7680000 | tf_op jit(solution)/shard_map/all_gather | solution.py:378
  11.0 36.9 %collective-permute-start.2 = (bf16[600,1280]{1,0:T(8,128)(2,1)}, bf16[600,1280]{1,0:T(8,128)(2,1)}, u32[]{:S(2)}, u32[]{:S(2)}) collective-permute-start(bf16[600,1280]{1,0:T(8,128)(2,1)} %pad_maximum_fusion.2), channel_id=1, source_target_pairs={{0,4},{4,0},{1,5},{5,1},{2,6},{6,2},{3,7},{7,3},{8,12},{12,8},{9,1... | collective-permute-start | bytes 4608008 | tf_op jit(solution)/shard_map/ppermute | solution.py:32
  14.8 16.9 %collective-permute-start.1 = (bf16[264,1280]{1,0:T(8,128)(2,1)}, bf16[264,1280]{1,0:T(8,128)(2,1)}, u32[]{:S(2)}, u32[]{:S(2)}) collective-permute-start(bf16[264,1280]{1,0:T(8,128)(2,1)} %pad_maximum_fusion.6), channel_id=1, source_target_pairs={{0,2},{1,3},{2,0},{3,1},{4,6},{5,7},{6,4},{7,5},{8,10},{9,11},{10,... | collective-permute-start | bytes 2027528 | tf_op jit(solution)/shard_map/ppermute | solution.py:40
  16.6 32.6 %collective-permute-start = (f32[1,256]{1,0:T(1,128)S(1)}, f32[1,256]{1,0:T(1,128)S(1)}, u32[]{:S(2)}, u32[]{:S(2)}) collective-permute-start(f32[1,256]{1,0:T(1,128)S(1)} %bitcast.89), channel_id=1, source_target_pairs={{0,4},{4,0},{1,5},{5,1},{2,6},{6,2},{3,7},{7,3},{8,12},{12,8},{9,1... | collective-permute-start | bytes 3080 | tf_op jit(solution)/shard_map/ppermute | solution.py:32
  47.9 432.0 %all-gather.6.cloned.1.call-start = ((), (), s32[]{:S(2)}) async-start(), calls=%async_computation.1 | async-start | bytes 21626880 | tf_op jit(solution)/shard_map/all_gather | solution.py:429
  54.9 15.4 %collective-permute-start.4 = (f32[128,1056]{0,1:T(8,128)}, f32[128,1056]{0,1:T(8,128)}, u32[]{:S(2)}, u32[]{:S(2)}) collective-permute-start(f32[128,1056]{0,1:T(8,128)} %get-tuple-element.129), channel_id=1, source_target_pairs={{0,4},{4,0},{1,5},{5,1},{2,6},{6,2},{3,7},{7,3},{8,12},{12,8},{9,1... | collective-permute-start | bytes 1622024 | tf_op jit(solution)/shard_map/ppermute | solution.py:32
  63.3 18.8 %collective-permute-start.7 = (bf16[384,480]{0,1:T(8,128)(2,1)}, bf16[384,480]{0,1:T(8,128)(2,1)}, u32[]{:S(2)}, u32[]{:S(2)}) collective-permute-start(bf16[384,480]{0,1:T(8,128)(2,1)} %get-tuple-element.130), channel_id=1, source_target_pairs={{0,4},{4,0},{1,5},{5,1},{2,6},{6,2},{3,7},{7,3},{8,12},{12,8},{9,1... | collective-permute-start | bytes 1105928 | tf_op jit(solution)/shard_map/ppermute | solution.py:32
  109.6 34.9 %collective-permute-start.11 = (bf16[320,1280]{1,0:T(8,128)(2,1)}, bf16[320,1280]{1,0:T(8,128)(2,1)}, u32[]{:S(2)}, u32[]{:S(2)}) collective-permute-start(bf16[320,1280]{1,0:T(8,128)(2,1)} %get-tuple-element.142), channel_id=1, source_target_pairs={{0,4},{4,0},{1,5},{5,1},{2,6},{6,2},{3,7},{7,3},{8,12},{12,8},{9,1... | collective-permute-start | bytes 2457608 | tf_op jit(solution)/shard_map/ppermute | solution.py:32
  111.5 25.8 %collective-permute-start.14 = (bf16[256,1280]{1,0:T(8,128)(2,1)}, bf16[256,1280]{1,0:T(8,128)(2,1)}, u32[]{:S(2)}, u32[]{:S(2)}) collective-permute-start(bf16[256,1280]{1,0:T(8,128)(2,1)} %copy-done.35), channel_id=1, source_target_pairs={{0,2},{1,3},{2,0},{3,1},{4,6},{5,7},{6,4},{7,5},{8,10},{9,11},{10,... | collective-permute-start | bytes 1966088 | tf_op jit(solution)/shard_map/ppermute | solution.py:40
  114.0 23.9 %collective-permute-start.12 = (bf16[128,1280]{1,0:T(8,128)(2,1)}, bf16[128,1280]{1,0:T(8,128)(2,1)S(1)}, u32[]{:S(2)}, u32[]{:S(2)}) collective-permute-start(bf16[128,1280]{1,0:T(8,128)(2,1)} %get-tuple-element.143), channel_id=1, source_target_pairs={{0,4},{4,0},{1,5},{5,1},{2,6},{6,2},{3,7},{7,3},{8,12},{12,8},{9,1... | collective-permute-start | bytes 983048 | tf_op jit(solution)/shard_map/ppermute | solution.py:32
  114.5 30.1 %collective-permute-start.13 = (bf16[128,1280]{1,0:T(8,128)(2,1)}, bf16[128,1280]{1,0:T(8,128)(2,1)S(1)}, u32[]{:S(2)}, u32[]{:S(2)}) collective-permute-start(bf16[128,1280]{1,0:T(8,128)(2,1)} %get-tuple-element.144), channel_id=1, source_target_pairs={{0,4},{4,0},{1,5},{5,1},{2,6},{6,2},{3,7},{7,3},{8,12},{12,8},{9,1... | collective-permute-start | bytes 983048 | tf_op jit(solution)/shard_map/ppermute | solution.py:32
  146.4 371.5 %all-gather.8.cloned.1.call-start = ((), (), s32[]{:S(2)}) async-start(), calls=%async_computation.2 | async-start | bytes 21626880 | tf_op jit(solution)/shard_map/all_gather | solution.py:448
  157.9 9.8 %collective-permute-start.16 = (bf16[64,2560]{1,0:T(8,128)(2,1)S(1)}, bf16[64,2560]{1,0:T(8,128)(2,1)S(1)}, u32[]{:S(2)}, u32[]{:S(2)}) collective-permute-start(bf16[64,2560]{1,0:T(8,128)(2,1)S(1)} %get-tuple-element.284), channel_id=1, source_target_pairs={{0,2},{1,3},{2,0},{3,1},{4,6},{5,7},{6,4},{7,5},{8,10},{9,11},{10,... | collective-permute-start | bytes 983048 | tf_op jit(solution)/shard_map/ppermute | solution.py:40
  168.8 20.9 %collective-permute-start.17 = (bf16[128,2560]{1,0:T(8,128)(2,1)}, bf16[128,2560]{1,0:T(8,128)(2,1)}, u32[]{:S(2)}, u32[]{:S(2)}) collective-permute-start(bf16[128,2560]{1,0:T(8,128)(2,1)} %pad_maximum_fusion.7), channel_id=1, source_target_pairs={{0,4},{4,0},{1,5},{5,1},{2,6},{6,2},{3,7},{7,3},{8,12},{12,8},{9,1... | collective-permute-start | bytes 1966088 | tf_op jit(solution)/shard_map/ppermute | solution.py:32
  171.3 20.3 %collective-permute-start.19 = (bf16[128,2560]{1,0:T(8,128)(2,1)}, bf16[128,2560]{1,0:T(8,128)(2,1)S(1)}, u32[]{:S(2)}, u32[]{:S(2)}) collective-permute-start(bf16[128,2560]{1,0:T(8,128)(2,1)} %pad_maximum_fusion.8), channel_id=1, source_target_pairs={{0,2},{1,3},{2,0},{3,1},{4,6},{5,7},{6,4},{7,5},{8,10},{9,11},{10,... | collective-permute-start | bytes 1966088 | tf_op jit(solution)/shard_map/ppermute | solution.py:40
  172.8 16.9 %collective-permute-start.20 = (bf16[1280]{0:T(1024)(128)(2,1)S(1)}, bf16[1280]{0:T(1024)(128)(2,1)S(1)}, u32[]{:S(2)}, u32[]{:S(2)}) collective-permute-start(bf16[1280]{0:T(1024)(128)(2,1)S(1)} %copy-done.88), channel_id=1, source_target_pairs={{0,4},{4,0},{1,5},{5,1},{2,6},{6,2},{3,7},{7,3},{8,12},{12,8},{9,1... | collective-permute-start | bytes 7688 | tf_op jit(solution)/shard_map/ppermute | solution.py:32
  195.9 29.5 %collective-permute-start.21 = (bf16[128,2560]{1,0:T(8,128)(2,1)}, bf16[128,2560]{1,0:T(8,128)(2,1)}, u32[]{:S(2)}, u32[]{:S(2)}) collective-permute-start(bf16[128,2560]{1,0:T(8,128)(2,1)} %multiply_convert_fusion.7), channel_id=1, source_target_pairs={{0,4},{4,0},{1,5},{5,1},{2,6},{6,2},{3,7},{7,3},{8,12},{12,8},{9,1... | collective-permute-start | bytes 1966088 | tf_op jit(solution)/shard_map/ppermute | solution.py:32
  196.4 29.0 %collective-permute-start.22 = (bf16[128,2560]{1,0:T(8,128)(2,1)}, bf16[128,2560]{1,0:T(8,128)(2,1)}, u32[]{:S(2)}, u32[]{:S(2)}) collective-permute-start(bf16[128,2560]{1,0:T(8,128)(2,1)} %multiply_convert_fusion.7), channel_id=1, source_target_pairs={{0,2},{1,3},{2,0},{3,1},{4,6},{5,7},{6,4},{7,5},{8,10},{9,11},{10,... | collective-permute-start | bytes 1966088 | tf_op jit(solution)/shard_map/ppermute | solution.py:40
  225.4 31.8 %collective-permute-start.26 = (bf16[128,2560]{1,0:T(8,128)(2,1)S(1)}, bf16[128,2560]{1,0:T(8,128)(2,1)S(1)}, u32[]{:S(2)}, u32[]{:S(2)}) collective-permute-start(bf16[128,2560]{1,0:T(8,128)(2,1)S(1)} %copy-done.19), channel_id=1, source_target_pairs={{0,4},{4,0},{1,5},{5,1},{2,6},{6,2},{3,7},{7,3},{8,12},{12,8},{9,1... | collective-permute-start | bytes 1966088 | tf_op jit(solution)/shard_map/ppermute | solution.py:32
  226.0 31.1 %collective-permute-start.27 = (bf16[128,2560]{1,0:T(8,128)(2,1)S(1)}, bf16[128,2560]{1,0:T(8,128)(2,1)S(1)}, u32[]{:S(2)}, u32[]{:S(2)}) collective-permute-start(bf16[128,2560]{1,0:T(8,128)(2,1)S(1)} %copy-done.19), channel_id=1, source_target_pairs={{0,2},{1,3},{2,0},{3,1},{4,6},{5,7},{6,4},{7,5},{8,10},{9,11},{10,... | collective-permute-start | bytes 1966088 | tf_op jit(solution)/shard_map/ppermute | solution.py:40
  229.9 14.3 %collective-permute-start.23 = (bf16[64,2560]{1,0:T(8,128)(2,1)S(1)}, bf16[64,2560]{1,0:T(8,128)(2,1)S(1)}, u32[]{:S(2)}, u32[]{:S(2)}) collective-permute-start(bf16[64,2560]{1,0:T(8,128)(2,1)S(1)} %slice.409), channel_id=1, source_target_pairs={{0,2},{1,3},{2,0},{3,1},{4,6},{5,7},{6,4},{7,5},{8,10},{9,11},{10,... | collective-permute-start | bytes 983048 | tf_op jit(solution)/shard_map/ppermute | solution.py:40
  231.4 19.0 %collective-permute-start.24 = (bf16[64,2560]{1,0:T(8,128)(2,1)S(1)}, bf16[64,2560]{1,0:T(8,128)(2,1)S(1)}, u32[]{:S(2)}, u32[]{:S(2)}) collective-permute-start(bf16[64,2560]{1,0:T(8,128)(2,1)S(1)} %slice.410), channel_id=1, source_target_pairs={{0,4},{4,0},{1,5},{5,1},{2,6},{6,2},{3,7},{7,3},{8,12},{12,8},{9,1... | collective-permute-start | bytes 983048 | tf_op jit(solution)/shard_map/ppermute | solution.py:32
  257.2 17.8 %collective-permute-start.28 = (bf16[64,2560]{1,0:T(8,128)(2,1)S(1)}, bf16[64,2560]{1,0:T(8,128)(2,1)S(1)}, u32[]{:S(2)}, u32[]{:S(2)}) collective-permute-start(bf16[64,2560]{1,0:T(8,128)(2,1)S(1)} %slice.411), channel_id=1, source_target_pairs={{0,2},{1,3},{2,0},{3,1},{4,6},{5,7},{6,4},{7,5},{8,10},{9,11},{10,... | collective-permute-start | bytes 983048 | tf_op jit(solution)/shard_map/ppermute | solution.py:40
  259.6 17.4 %collective-permute-start.29 = (bf16[64,2560]{1,0:T(8,128)(2,1)S(1)}, bf16[64,2560]{1,0:T(8,128)(2,1)S(1)}, u32[]{:S(2)}, u32[]{:S(2)}) collective-permute-start(bf16[64,2560]{1,0:T(8,128)(2,1)S(1)} %slice.412), channel_id=1, source_target_pairs={{0,4},{4,0},{1,5},{5,1},{2,6},{6,2},{3,7},{7,3},{8,12},{12,8},{9,1... | collective-permute-start | bytes 983048 | tf_op jit(solution)/shard_map/ppermute | solution.py:32
  319.5 16.0 %collective-permute-start.33 = (bf16[128,2560]{1,0:T(8,128)(2,1)S(1)}, bf16[128,2560]{1,0:T(8,128)(2,1)S(1)}, u32[]{:S(2)}, u32[]{:S(2)}) collective-permute-start(bf16[128,2560]{1,0:T(8,128)(2,1)S(1)} %pad_maximum_fusion.9), channel_id=1, source_target_pairs={{0,4},{4,0},{1,5},{5,1},{2,6},{6,2},{3,7},{7,3},{8,12},{12,8},{9,1... | collective-permute-start | bytes 1966088 | tf_op jit(solution)/shard_map/ppermute | solution.py:32
  320.0 15.8 %collective-permute-start.35 = (bf16[128,2560]{1,0:T(8,128)(2,1)S(1)}, bf16[128,2560]{1,0:T(8,128)(2,1)S(1)}, u32[]{:S(2)}, u32[]{:S(2)}) collective-permute-start(bf16[128,2560]{1,0:T(8,128)(2,1)S(1)} %pad_maximum_fusion.10), channel_id=1, source_target_pairs={{0,2},{1,3},{2,0},{3,1},{4,6},{5,7},{6,4},{7,5},{8,10},{9,11},{10,... | collective-permute-start | bytes 1966088 | tf_op jit(solution)/shard_map/ppermute | solution.py:40
  338.1 18.2 %collective-permute-start.36 = (bf16[128,2560]{1,0:T(8,128)(2,1)S(1)}, bf16[128,2560]{1,0:T(8,128)(2,1)S(1)}, u32[]{:S(2)}, u32[]{:S(2)}) collective-permute-start(bf16[128,2560]{1,0:T(8,128)(2,1)S(1)} %get-tuple-element.175), channel_id=1, source_target_pairs={{0,4},{4,0},{1,5},{5,1},{2,6},{6,2},{3,7},{7,3},{8,12},{12,8},{9,1... | collective-permute-start | bytes 1966088 | tf_op jit(solution)/shard_map/ppermute | solution.py:32
  339.7 16.8 %collective-permute-start.37 = (bf16[128,2560]{1,0:T(8,128)(2,1)S(1)}, bf16[128,2560]{1,0:T(8,128)(2,1)S(1)}, u32[]{:S(2)}, u32[]{:S(2)}) collective-permute-start(bf16[128,2560]{1,0:T(8,128)(2,1)S(1)} %get-tuple-element.175), channel_id=1, source_target_pairs={{0,2},{1,3},{2,0},{3,1},{4,6},{5,7},{6,4},{7,5},{8,10},{9,11},{10,... | collective-permute-start | bytes 1966088 | tf_op jit(solution)/shard_map/ppermute | solution.py:40
  356.5 15.5 %collective-permute-start.38 = (bf16[64,2560]{1,0:T(8,128)(2,1)S(1)}, bf16[64,2560]{1,0:T(8,128)(2,1)S(1)}, u32[]{:S(2)}, u32[]{:S(2)}) collective-permute-start(bf16[64,2560]{1,0:T(8,128)(2,1)S(1)} %slice.428), channel_id=1, source_target_pairs={{0,2},{1,3},{2,0},{3,1},{4,6},{5,7},{6,4},{7,5},{8,10},{9,11},{10,... | collective-permute-start | bytes 983048 | tf_op jit(solution)/shard_map/ppermute | solution.py:40
  357.8 15.8 %collective-permute-start.39 = (bf16[64,2560]{1,0:T(8,128)(2,1)S(1)}, bf16[64,2560]{1,0:T(8,128)(2,1)S(1)}, u32[]{:S(2)}, u32[]{:S(2)}) collective-permute-start(bf16[64,2560]{1,0:T(8,128)(2,1)S(1)} %slice.429), channel_id=1, source_target_pairs={{0,4},{4,0},{1,5},{5,1},{2,6},{6,2},{3,7},{7,3},{8,12},{12,8},{9,1... | collective-permute-start | bytes 983048 | tf_op jit(solution)/shard_map/ppermute | solution.py:32
  380.4 204.6 %collective-permute-start.63 = (bf16[512,1280]{1,0:T(8,128)(2,1)}, bf16[512,1280]{1,0:T(8,128)(2,1)}, u32[]{:S(2)}, u32[]{:S(2)}) collective-permute-start(bf16[512,1280]{1,0:T(8,128)(2,1)} %pad_maximum_fusion.4), channel_id=1, source_target_pairs={{0,1},{1,0},{2,3},{3,2},{4,5},{5,4},{6,7},{7,6},{8,9},{9,8},{10,11... | collective-permute-start | bytes 3932168 | tf_op jit(solution)/shard_map/ppermute | solution.py:36
  382.0 19.3 %collective-permute-start.51 = (bf16[128,1280]{1,0:T(8,128)(2,1)S(1)}, bf16[128,1280]{1,0:T(8,128)(2,1)S(1)}, u32[]{:S(2)}, u32[]{:S(2)}) collective-permute-start(bf16[128,1280]{1,0:T(8,128)(2,1)S(1)} %dynamic-slice_convert_fusion), channel_id=1, source_target_pairs={{0,4},{4,0},{1,5},{5,1},{2,6},{6,2},{3,7},{7,3},{8,12},{12,8},{9,1... | collective-permute-start | bytes 983048 | tf_op jit(solution)/shard_map/ppermute | solution.py:32
  399.3 36.5 %collective-permute-start.41 = (bf16[320,1280]{1,0:T(8,128)(2,1)}, bf16[320,1280]{1,0:T(8,128)(2,1)}, u32[]{:S(2)}, u32[]{:S(2)}) collective-permute-start(bf16[320,1280]{1,0:T(8,128)(2,1)} %get-tuple-element.290), channel_id=1, source_target_pairs={{0,4},{4,0},{1,5},{5,1},{2,6},{6,2},{3,7},{7,3},{8,12},{12,8},{9,1... | collective-permute-start | bytes 2457608 | tf_op jit(solution)/shard_map/ppermute | solution.py:32
  440.7 32.5 %collective-permute-start.42 = (bf16[512,1152]{1,0:T(8,128)(2,1)S(1)}, bf16[512,1152]{1,0:T(8,128)(2,1)S(1)}, u32[]{:S(2)}, u32[]{:S(2)}) collective-permute-start(bf16[512,1152]{1,0:T(8,128)(2,1)S(1)} %slice.510), channel_id=1, source_target_pairs={{0,1},{1,0},{2,3},{3,2},{4,5},{5,4},{6,7},{7,6},{8,9},{9,8},{10,11... | collective-permute-start | bytes 3538952 | tf_op jit(solution)/shard_map/ppermute | solution.py:36
  443.0 17.8 %collective-permute-start.55 = (bf16[256,640]{1,0:T(8,128)(2,1)S(1)}, bf16[256,640]{1,0:T(8,128)(2,1)S(1)}, u32[]{:S(2)}, u32[]{:S(2)}) collective-permute-start(bf16[256,640]{1,0:T(8,128)(2,1)S(1)} %fusion.32), channel_id=1, source_target_pairs={{0,4},{4,0},{1,5},{5,1},{2,6},{6,2},{3,7},{7,3},{8,12},{12,8},{9,1... | collective-permute-start | bytes 983048 | tf_op jit(solution)/shard_map/ppermute | solution.py:32
  446.7 25.4 %collective-permute-start.53 = (bf16[384,480]{0,1:T(8,128)(2,1)S(1)}, bf16[384,480]{0,1:T(8,128)(2,1)S(1)}, u32[]{:S(2)}, u32[]{:S(2)}) collective-permute-start(bf16[384,480]{0,1:T(8,128)(2,1)S(1)} %get-tuple-element.305), channel_id=1, source_target_pairs={{0,4},{4,0},{1,5},{5,1},{2,6},{6,2},{3,7},{7,3},{8,12},{12,8},{9,1... | collective-permute-start | bytes 1105928 | tf_op jit(solution)/shard_map/ppermute | solution.py:32
  450.7 90.4 %collective-permute-start.48 = (bf16[640,1280]{1,0:T(8,128)(2,1)}, bf16[640,1280]{1,0:T(8,128)(2,1)}, u32[]{:S(2)}, u32[]{:S(2)}) collective-permute-start(bf16[640,1280]{1,0:T(8,128)(2,1)} %maximum_select_fusion.7), channel_id=1, source_target_pairs={{0,8},{24,16},{1,9},{25,17},{2,10},{26,18},{3,11},{27,19},{4,12},{... | collective-permute-start | bytes 4915208 | tf_op jit(solution)/shard_map/ppermute | solution.py:311
  480.0 24.9 %collective-permute-start.45 = (bf16[128,1152]{1,0:T(8,128)(2,1)S(1)}, bf16[128,1152]{1,0:T(8,128)(2,1)S(1)}, u32[]{:S(2)}, u32[]{:S(2)}) collective-permute-start(bf16[128,1152]{1,0:T(8,128)(2,1)S(1)} %pad_maximum_fusion.14), channel_id=1, source_target_pairs={{0,4},{4,0},{1,5},{5,1},{2,6},{6,2},{3,7},{7,3},{8,12},{12,8},{9,1... | collective-permute-start | bytes 884744 | tf_op jit(solution)/shard_map/ppermute | solution.py:32
  481.0 23.8 %collective-permute-start.46 = (bf16[128,1152]{1,0:T(8,128)(2,1)S(1)}, bf16[128,1152]{1,0:T(8,128)(2,1)S(1)}, u32[]{:S(2)}, u32[]{:S(2)}) collective-permute-start(bf16[128,1152]{1,0:T(8,128)(2,1)S(1)} %pad_maximum_fusion.15), channel_id=1, source_target_pairs={{0,2},{1,3},{2,0},{3,1},{4,6},{5,7},{6,4},{7,5},{8,10},{9,11},{10,... | collective-permute-start | bytes 884744 | tf_op jit(solution)/shard_map/ppermute | solution.py:40
  514.3 26.9 %collective-permute-start.47 = (bf16[128,1056]{1,0:T(8,128)(2,1)}, bf16[128,1056]{1,0:T(8,128)(2,1)}, u32[]{:S(2)}, u32[]{:S(2)}) collective-permute-start(bf16[128,1056]{1,0:T(8,128)(2,1)} %concatenate.313), channel_id=1, source_target_pairs={{0,4},{4,0},{1,5},{5,1},{2,6},{6,2},{3,7},{7,3},{8,12},{12,8},{9,1... | collective-permute-start | bytes 811016 | tf_op jit(solution)/shard_map/ppermute | solution.py:32
  544.8 55.2 %collective-permute-start.54 = (bf16[384,960]{0,1:T(8,128)(2,1)}, bf16[384,960]{0,1:T(8,128)(2,1)}, u32[]{:S(2)}, u32[]{:S(2)}) collective-permute-start(bf16[384,960]{0,1:T(8,128)(2,1)} %maximum_select_fusion.10), channel_id=1, source_target_pairs={{0,8},{24,16},{1,9},{25,17},{2,10},{26,18},{3,11},{27,19},{4,12},{... | collective-permute-start | bytes 2211848 | tf_op jit(solution)/shard_map/ppermute | solution.py:311
  552.9 47.1 %collective-permute-start.50 = (bf16[640,1280]{1,0:T(8,128)(2,1)}, bf16[640,1280]{1,0:T(8,128)(2,1)}, u32[]{:S(2)}, u32[]{:S(2)}) collective-permute-start(bf16[640,1280]{1,0:T(8,128)(2,1)} %add_convert_fusion.4), channel_id=1, source_target_pairs={{8,16},{16,8},{9,17},{17,9},{10,18},{18,10},{11,19},{19,11},{12,20... | collective-permute-start | bytes 4915208 | tf_op jit(solution)/shard_map/ppermute | solution.py:315
  557.1 29.4 %collective-permute-start.60 = (bf16[256,264]{1,0:T(8,128)(2,1)}, bf16[256,264]{1,0:T(8,128)(2,1)}, u32[]{:S(2)}, u32[]{:S(2)}) collective-permute-start(bf16[256,264]{1,0:T(8,128)(2,1)} %get-tuple-element.335), channel_id=1, source_target_pairs={{0,2},{1,3},{2,0},{3,1},{4,6},{5,7},{6,4},{7,5},{8,10},{9,11},{10,... | collective-permute-start | bytes 405512 | tf_op jit(solution)/shard_map/ppermute | solution.py:40
  558.1 24.5 %collective-permute-start.65 = (f32[38,128]{1,0:T(8,128)S(1)}, f32[38,128]{1,0:T(8,128)S(1)}, u32[]{:S(2)}, u32[]{:S(2)}) collective-permute-start(f32[38,128]{1,0:T(8,128)S(1)} %fusion.102), channel_id=1, source_target_pairs={{0,2},{1,3},{2,0},{3,1},{4,6},{5,7},{6,4},{7,5},{8,10},{9,11},{10,... | collective-permute-start | bytes 58376 | tf_op jit(solution)/shard_map/ppermute | solution.py:40
  586.5 10.7 %collective-permute-start.56 = (bf16[64,2560]{1,0:T(8,128)(2,1)}, bf16[64,2560]{1,0:T(8,128)(2,1)S(1)}, u32[]{:S(2)}, u32[]{:S(2)}) collective-permute-start(bf16[64,2560]{1,0:T(8,128)(2,1)} %get-tuple-element.271), channel_id=1, source_target_pairs={{0,4},{4,0},{1,5},{5,1},{2,6},{6,2},{3,7},{7,3},{8,12},{12,8},{9,1... | collective-permute-start | bytes 983048 | tf_op jit(solution)/shard_map/ppermute | solution.py:32
  588.0 12.1 %collective-permute-start.57 = (bf16[64,2560]{1,0:T(8,128)(2,1)}, bf16[64,2560]{1,0:T(8,128)(2,1)S(1)}, u32[]{:S(2)}, u32[]{:S(2)}) collective-permute-start(bf16[64,2560]{1,0:T(8,128)(2,1)} %get-tuple-element.270), channel_id=1, source_target_pairs={{0,2},{1,3},{2,0},{3,1},{4,6},{5,7},{6,4},{7,5},{8,10},{9,11},{10,... | collective-permute-start | bytes 983048 | tf_op jit(solution)/shard_map/ppermute | solution.py:40
  601.0 32.2 %collective-permute-start.67 = (bf16[128,2560]{1,0:T(8,128)(2,1)}, bf16[128,2560]{1,0:T(8,128)(2,1)}, u32[]{:S(2)}, u32[]{:S(2)}) collective-permute-start(bf16[128,2560]{1,0:T(8,128)(2,1)} %pad_maximum_fusion.11), channel_id=1, source_target_pairs={{0,4},{4,0},{1,5},{5,1},{2,6},{6,2},{3,7},{7,3},{8,12},{12,8},{9,1... | collective-permute-start | bytes 1966088 | tf_op jit(solution)/shard_map/ppermute | solution.py:32
  603.2 30.0 %collective-permute-start.68 = (bf16[128,2560]{1,0:T(8,128)(2,1)}, bf16[128,2560]{1,0:T(8,128)(2,1)}, u32[]{:S(2)}, u32[]{:S(2)}) collective-permute-start(bf16[128,2560]{1,0:T(8,128)(2,1)} %pad_maximum_fusion.12), channel_id=1, source_target_pairs={{0,2},{1,3},{2,0},{3,1},{4,6},{5,7},{6,4},{7,5},{8,10},{9,11},{10,... | collective-permute-start | bytes 1966088 | tf_op jit(solution)/shard_map/ppermute | solution.py:40
  606.0 28.9 %collective-permute-start.58 = (bf16[384,960]{0,1:T(8,128)(2,1)S(1)}, bf16[384,960]{0,1:T(8,128)(2,1)}, u32[]{:S(2)}, u32[]{:S(2)}) collective-permute-start(bf16[384,960]{0,1:T(8,128)(2,1)S(1)} %add_convert_fusion.7), channel_id=1, source_target_pairs={{8,16},{16,8},{9,17},{17,9},{10,18},{18,10},{11,19},{19,11},{12,20... | collective-permute-start | bytes 2211848 | tf_op jit(solution)/shard_map/ppermute | solution.py:315
  607.6 27.3 %collective-permute-start.59 = (bf16[256,1280]{1,0:T(8,128)(2,1)S(1)}, bf16[256,1280]{1,0:T(8,128)(2,1)}, u32[]{:S(2)}, u32[]{:S(2)}) collective-permute-start(bf16[256,1280]{1,0:T(8,128)(2,1)S(1)} %copy-done.37), channel_id=1, source_target_pairs={{0,8},{24,16},{1,9},{25,17},{2,10},{26,18},{3,11},{27,19},{4,12},{... | collective-permute-start | bytes 1966088 | tf_op jit(solution)/shard_map/ppermute | solution.py:311
  615.1 91.6 %collective-permute-start.77 = (bf16[640,1280]{1,0:T(8,128)(2,1)}, bf16[640,1280]{1,0:T(8,128)(2,1)}, u32[]{:S(2)}, u32[]{:S(2)}) collective-permute-start(bf16[640,1280]{1,0:T(8,128)(2,1)} %add_convert_fusion.3), channel_id=1, source_target_pairs={{8,0},{16,24},{9,1},{17,25},{10,2},{18,26},{11,3},{19,27},{12,4},{... | collective-permute-start | bytes 4915208 | tf_op jit(solution)/shard_map/ppermute | solution.py:319
  636.2 35.4 %collective-permute-start.70 = (bf16[256,1280]{1,0:T(8,128)(2,1)S(1)}, bf16[256,1280]{1,0:T(8,128)(2,1)S(1)}, u32[]{:S(2)}, u32[]{:S(2)}) collective-permute-start(bf16[256,1280]{1,0:T(8,128)(2,1)S(1)} %add_convert_fusion.11), channel_id=1, source_target_pairs={{8,16},{16,8},{9,17},{17,9},{10,18},{18,10},{11,19},{19,11},{12,20... | collective-permute-start | bytes 1966088 | tf_op jit(solution)/shard_map/ppermute | solution.py:315
  636.9 35.9 %collective-permute-start.71 = (bf16[268,1280]{1,0:T(8,128)(2,1)S(1)}, bf16[268,1280]{1,0:T(8,128)(2,1)S(1)}, u32[]{:S(2)}, u32[]{:S(2)}) collective-permute-start(bf16[268,1280]{1,0:T(8,128)(2,1)S(1)} %pad_maximum_fusion.5), channel_id=1, source_target_pairs={{0,8},{24,16},{1,9},{25,17},{2,10},{26,18},{3,11},{27,19},{4,12},{... | collective-permute-start | bytes 2058248 | tf_op jit(solution)/shard_map/ppermute | solution.py:311
  646.8 57.6 %collective-permute-start.75 = (bf16[384,960]{0,1:T(8,128)(2,1)S(1)}, bf16[384,960]{0,1:T(8,128)(2,1)}, u32[]{:S(2)}, u32[]{:S(2)}) collective-permute-start(bf16[384,960]{0,1:T(8,128)(2,1)S(1)} %add_convert_fusion.6), channel_id=1, source_target_pairs={{8,0},{16,24},{9,1},{17,25},{10,2},{18,26},{11,3},{19,27},{12,4},{... | collective-permute-start | bytes 2211848 | tf_op jit(solution)/shard_map/ppermute | solution.py:319
  648.2 22.2 %collective-permute-start.69 = (bf16[128,1280]{1,0:T(8,128)(2,1)S(1)}, bf16[128,1280]{1,0:T(8,128)(2,1)S(1)}, u32[]{:S(2)}, u32[]{:S(2)}) collective-permute-start(bf16[128,1280]{1,0:T(8,128)(2,1)S(1)} %get-tuple-element.309), channel_id=1, source_target_pairs={{0,4},{4,0},{1,5},{5,1},{2,6},{6,2},{3,7},{7,3},{8,12},{12,8},{9,1... | collective-permute-start | bytes 983048 | tf_op jit(solution)/shard_map/ppermute | solution.py:32
  673.0 39.5 %collective-permute-start.72 = (bf16[268,1280]{1,0:T(8,128)(2,1)S(1)}, bf16[268,1280]{1,0:T(8,128)(2,1)}, u32[]{:S(2)}, u32[]{:S(2)}) collective-permute-start(bf16[268,1280]{1,0:T(8,128)(2,1)S(1)} %add_convert_fusion.9), channel_id=1, source_target_pairs={{8,16},{16,8},{9,17},{17,9},{10,18},{18,10},{11,19},{19,11},{12,20... | collective-permute-start | bytes 2058248 | tf_op jit(solution)/shard_map/ppermute | solution.py:315
  676.6 35.9 %collective-permute-start.73 = (bf16[400,1280]{1,0:T(8,128)(2,1)}, bf16[400,1280]{1,0:T(8,128)(2,1)}, u32[]{:S(2)}, u32[]{:S(2)}) collective-permute-start(bf16[400,1280]{1,0:T(8,128)(2,1)} %dynamic_slice.220), channel_id=1, source_target_pairs={{0,4},{4,0},{1,5},{5,1},{2,6},{6,2},{3,7},{7,3},{8,12},{12,8},{9,1... | collective-permute-start | bytes 3072008 | tf_op jit(solution)/shard_map/ppermute | solution.py:32
  678.6 31.7 %collective-permute-start.76 = (bf16[256,1280]{1,0:T(8,128)(2,1)S(1)}, bf16[256,1280]{1,0:T(8,128)(2,1)}, u32[]{:S(2)}, u32[]{:S(2)}) collective-permute-start(bf16[256,1280]{1,0:T(8,128)(2,1)S(1)} %add_convert_fusion.10), channel_id=1, source_target_pairs={{8,0},{16,24},{9,1},{17,25},{10,2},{18,26},{11,3},{19,27},{12,4},{... | collective-permute-start | bytes 1966088 | tf_op jit(solution)/shard_map/ppermute | solution.py:319
  713.8 30.4 %collective-permute-start.74 = (bf16[268,1280]{1,0:T(8,128)(2,1)S(1)}, bf16[268,1280]{1,0:T(8,128)(2,1)S(1)}, u32[]{:S(2)}, u32[]{:S(2)}) collective-permute-start(bf16[268,1280]{1,0:T(8,128)(2,1)S(1)} %add_convert_fusion.8), channel_id=1, source_target_pairs={{8,0},{16,24},{9,1},{17,25},{10,2},{18,26},{11,3},{19,27},{12,4},{... | collective-permute-start | bytes 2058248 | tf_op jit(solution)/shard_map/ppermute | solution.py:319
  739.6 22.2 %collective-permute-start.79 = (bf16[400,1280]{1,0:T(8,128)(2,1)}, bf16[400,1280]{1,0:T(8,128)(2,1)}, u32[]{:S(2)}, u32[]{:S(2)}) collective-permute-start(bf16[400,1280]{1,0:T(8,128)(2,1)} %dynamic_slice.223), channel_id=1, source_target_pairs={{0,4},{4,0},{1,5},{5,1},{2,6},{6,2},{3,7},{7,3},{8,12},{12,8},{9,1... | collective-permute-start | bytes 3072008 | tf_op jit(solution)/shard_map/ppermute | solution.py:32
  739.8 23.3 %collective-permute-start.78 = (bf16[400,1280]{1,0:T(8,128)(2,1)}, bf16[400,1280]{1,0:T(8,128)(2,1)}, u32[]{:S(2)}, u32[]{:S(2)}) collective-permute-start(bf16[400,1280]{1,0:T(8,128)(2,1)} %collective-permute-done.73), channel_id=1, source_target_pairs={{0,8},{8,0},{16,24},{24,16},{1,9},{9,1},{17,25},{25,17},{2,10},{10... | collective-permute-start | bytes 3072008 | tf_op jit(solution)/shard_map/ppermute | solution.py:584
  764.8 21.1 %collective-permute-start.81 = (bf16[400,1280]{1,0:T(8,128)(2,1)S(1)}, bf16[400,1280]{1,0:T(8,128)(2,1)S(1)}, u32[]{:S(2)}, u32[]{:S(2)}) collective-permute-start(bf16[400,1280]{1,0:T(8,128)(2,1)S(1)} %dynamic_slice.226), channel_id=1, source_target_pairs={{0,4},{4,0},{1,5},{5,1},{2,6},{6,2},{3,7},{7,3},{8,12},{12,8},{9,1... | collective-permute-start | bytes 3072008 | tf_op jit(solution)/shard_map/ppermute | solution.py:32
  766.3 23.3 %collective-permute-start.80 = (bf16[400,1280]{1,0:T(8,128)(2,1)}, bf16[400,1280]{1,0:T(8,128)(2,1)S(1)}, u32[]{:S(2)}, u32[]{:S(2)}) collective-permute-start(bf16[400,1280]{1,0:T(8,128)(2,1)} %collective-permute-done.79), channel_id=1, source_target_pairs={{0,8},{8,0},{16,24},{24,16},{1,9},{9,1},{17,25},{25,17},{2,10},{10... | collective-permute-start | bytes 3072008 | tf_op jit(solution)/shard_map/ppermute | solution.py:584
  785.9 22.9 %collective-permute-start.82 = (bf16[400,1280]{1,0:T(8,128)(2,1)S(1)}, bf16[400,1280]{1,0:T(8,128)(2,1)S(1)}, u32[]{:S(2)}, u32[]{:S(2)}) collective-permute-start(bf16[400,1280]{1,0:T(8,128)(2,1)S(1)} %collective-permute-done.81), channel_id=1, source_target_pairs={{0,8},{8,0},{16,24},{24,16},{1,9},{9,1},{17,25},{25,17},{2,10},{10... | collective-permute-start | bytes 3072008 | tf_op jit(solution)/shard_map/ppermute | solution.py:584
  (124 other events, 1249.0 us)
Sparse Core Ops, SparseCore 0:
  48.0 114.4 all-gather.3
  165.3 159.1 all-gather.5
  328.0 179.5 all-gather.7

commit v4 on v3

--- a/solution.py
+++ b/solution.py
@@ -498,7 +498,7 @@
     latent_steps = scatter_far(scatter_core(latent_grad_part))
     if by_factors:
         *latent_steps, grads_all = together(*latent_steps, grads_all)
-        grad_act_all = dot(down, grads_all, (1, 1))
+        grad_act_all = dot(down, grads_all, (1, 1), BF16)
     latent_steps = list(latent_steps)
     latent_grad = scatter_near(*latent_steps)
     if by_factors:
@@ -528,7 +528,7 @@
     if by_factors:
         out_1 = inward(out_part)
         output_core = scatter_core(output_part)
-        gate_all = dot(gate_up[:units], rows_all, (1, 1))
+        gate_all = dot(gate_up[:units], rows_all, (1, 1), BF16)
         low_other, gate_all, out_1, output_core = barrier((low_other, gate_all, out_1, output_core))
     latent_low = pair(first_x, latent_low, low_other, 0)
     inner_half = pair(first_x, inner_in, inner_other, 0)
@@ -563,13 +563,13 @@
     if by_factors:
         input_gradient, up_part = barrier((input_gradient, up_part))
         out_2, up_1, output_far = across(*out_1), inward(up_part), scatter_far(output_core)
-        up_all = dot(gate_up[units:], rows_all, (1, 1))
+        up_all = dot(gate_up[units:], rows_all, (1, 1), BF16)
         gate_all, up_all, out_2, up_1, latent_up_part, output_far = barrier(
             (gate_all, up_all, out_2, up_1, latent_up_part, output_far)
         )
         out_3, up_2, latent_1 = outward(*out_2), across(*up_1), inward(latent_up_part)
         output_own = (middle + RESIDUAL_SCALE * scatter_near(*output_far)).astype(BF16)
-        act_all, grad_gate_all, grad_up_all = activate(gate_all, up_all, grad_act_all)
+        act_all, grad_gate_all, grad_up_all = activate(*(v.astype(F32) for v in (gate_all, up_all, grad_act_all)))
         act_all, grad_gate_all, grad_up_all, up_2, latent_1, latent_down_part, output_own = barrier(
             (act_all, grad_gate_all, grad_up_all, up_2, latent_1, latent_down_part, output_own)
         )

time: 831 us -> 822 us (0.989)
  other arithmetic: 102 us -> 90.4 us
    unnamed x242 -> x236, local copies, waits for them, and re-layouts: 39.6 us -> 38.5 us
  transfers between devices with their start and end apart: 86 -> 86, of which waited for: 44 -> 43; matrix products, arithmetic and copies ran while one was open for 47% -> 47% of each run, Pallas kernels for 5% -> 5%
where the time goes in v4:
time: 822 us; the launch traced here: 811 us
  waiting for transfers between devices  235 us (29%)
  matrix products  209 us (25%)
  local copies, waits for them, and re-layouts  117 us (14%)
  starting transfers between devices  101 us (12%)
  other arithmetic  90.4 us (11%)
  Pallas kernels  43.3 us (5%)
  between operations  16 us (2%)
    dot_general x20, matrix products, dot(): lax.dot_general(a, b, ((contract[:1], contract[1:]), ((), ())), preferred...  209 us
    ppermute x35, waiting for transfers between devices, px(): return lax.ppermute(values, 'row', OVER_X)  148 us
    ppermute x20, waiting for transfers between devices, py(): return lax.ppermute(values, 'col', OVER_Y)  47.6 us
    unnamed x236, local copies, waits for them, and re-layouts  38.5 us
    ppermute x35, starting transfers between devices, px(): return lax.ppermute(values, 'row', OVER_X)  38.4 us
    pallas_call x1, Pallas kernels, attend_back(): pl.pallas_call(lambda *refs: attend_back_kernel(heads, *refs), grid=(rows...  25.8 us
    ppermute x20, starting transfers between devices, py(): return lax.ppermute(values, 'col', OVER_Y)  24.4 us
    ppermute x4, starting transfers between devices, inward(): return (part, lax.ppermute(part, 'dp', ((0, 1), (3, 2))))  21.1 us
  transfers between devices with their start and end apart: 86, of which 43 were waited for; matrix products, arithmetic and copies ran while one was open for 47% of the time, Pallas kernels for 5%

profile of v4, /device:TPU:0, one launch (start us, length us, event | category | flops | bytes accessed | tf_op | source)
XLA Modules:
  0.0 811.1 jit_solution(8286662484102951079)
XLA Ops:
  11.0 2.9 collective-permute-start.2
  19.9 11.9 %collective-permute-done.1 = bf16[264,1280]{1,0:T(8,128)(2,1)} collective-permute-done((bf16[264,1280]{1,0:T(8,128)(2,1)}, bf16[264,1280]{1,0:T(8,128)(2,1)}, u32[]{:S(2)}, u32[]{:S(2)}) %collective-permute-start.1) | collective-permute-done | bytes 675872 | tf_op jit(solution)/shard_map/ppermute | solution.py:40
  34.0 13.8 %collective-permute-done.2 = bf16[600,1280]{1,0:T(8,128)(2,1)} collective-permute-done((bf16[600,1280]{1,0:T(8,128)(2,1)}, bf16[600,1280]{1,0:T(8,128)(2,1)}, u32[]{:S(2)}, u32[]{:S(2)}) %collective-permute-start.2) | collective-permute-done | bytes 1536032 | tf_op jit(solution)/shard_map/ppermute | solution.py:32
  58.1 3.1 fusion.42
  63.7 6.7 collective-permute-done.4
  82.1 4.4 collective-permute-done.5
  117.2 17.5 %attend.1 = (bf16[1024,640]{1,0:T(8,128)(2,1)}, bf16[1024,640]{1,0:T(8,128)(2,1)}, bf16[1024,320]{1,0:T(8,128)(2,1)S(1)}, bf16[1024,320]{1,0:T(8,128)(2,1)S(1)}, f32[1024,8]{1,0:T(8,128)S(1)}) custom-call(bf16[1024,1152]{1,0:T(8,128)(2,1)} %copy-done.71, bf16[1024,1152]{1,0:T(8,128)(2,1)} %copy-done.71, bf16[1024,1152]{1,0:T(8,128)(2,1)} %copy-done.71, ...), custom_call_target="tpu_custom_call" | custom-call | flops 3690987520 | bytes 8388608 | tf_op jit(solution)/shard_map/attend/pallas_call | solution.py:220
  137.9 6.6 collective-permute-done.13
  146.6 5.1 fusion.46
  151.9 4.9 collective-permute-done.15
  159.7 7.7 collective-permute-done.16
  173.2 16.4 %collective-permute-done.20 = bf16[1280]{0:T(1024)(128)(2,1)S(1)} collective-permute-done((bf16[1280]{0:T(1024)(128)(2,1)S(1)}, bf16[1280]{0:T(1024)(128)(2,1)S(1)}, u32[]{:S(2)}, u32[]{:S(2)}) %collective-permute-start.20) | collective-permute-done | bytes 2592 | tf_op jit(solution)/shard_map/ppermute | solution.py:32
  197.6 3.9 broadcast_in_dim.78
  210.3 14.7 %collective-permute-done.21 = bf16[128,2560]{1,0:T(8,128)(2,1)} collective-permute-done((bf16[128,2560]{1,0:T(8,128)(2,1)}, bf16[128,2560]{1,0:T(8,128)(2,1)}, u32[]{:S(2)}, u32[]{:S(2)}) %collective-permute-start.21) | collective-permute-done | bytes 655392 | tf_op jit(solution)/shard_map/ppermute | solution.py:32
  240.8 2.7 collective-permute-done.23
  243.6 6.7 collective-permute-done.24
  259.5 11.4 %fusion.68 = f32[1600,1024]{1,0:T(8,128)S(1)} fusion(bf16[1600,2560]{1,0:T(8,128)(2,1)} %get-tuple-element.263, bf16[1024,2560]{1,0:T(8,128)(2,1)S(1)} %constant_dynamic-update-slice_fusion.21), kind=kOutput, calls=%fused_computation.328 | convolution fusion | flops 8388608000 | bytes 19988480 | tf_op jit(solution)/shard_map/dot_general | solution.py:48
  271.0 3.7 collective-permute-done.28
  277.1 4.9 collective-permute-done.30
  282.1 7.8 multiply_convert_fusion.1
  290.2 12.8 %fusion.69 = bf16[1024,2560]{1,0:T(8,128)(2,1)S(1)} fusion(bf16[1600,1024]{1,0:T(8,128)(2,1)S(1)} %pad_maximum_fusion, bf16[1600,2560]{1,0:T(8,128)(2,1)} %get-tuple-element.263), kind=kOutput, calls=%fused_computation.329 | convolution fusion | flops 8388608000 | bytes 16711680 | tf_op jit(solution)/shard_map/dot_general | solution.py:48
  303.4 4.9 collective-permute-done.31
  309.6 9.2 %collective-permute-done.32 = bf16[64,2560]{1,0:T(8,128)(2,1)S(1)} collective-permute-done((bf16[64,2560]{1,0:T(8,128)(2,1)S(1)}, bf16[64,2560]{1,0:T(8,128)(2,1)S(1)}, u32[]{:S(2)}, u32[]{:S(2)}) %collective-permute-start.32) | collective-permute-done | bytes 327712 | tf_op jit(solution)/shard_map/ppermute | solution.py:40
  321.3 13.9 %collective-permute-done.33 = bf16[128,2560]{1,0:T(8,128)(2,1)S(1)} collective-permute-done((bf16[128,2560]{1,0:T(8,128)(2,1)S(1)}, bf16[128,2560]{1,0:T(8,128)(2,1)S(1)}, u32[]{:S(2)}, u32[]{:S(2)}) %collective-permute-start.33) | collective-permute-done | bytes 655392 | tf_op jit(solution)/shard_map/ppermute | solution.py:32
  340.9 15.2 %collective-permute-done.36 = bf16[128,2560]{1,0:T(8,128)(2,1)S(1)} collective-permute-done((bf16[128,2560]{1,0:T(8,128)(2,1)S(1)}, bf16[128,2560]{1,0:T(8,128)(2,1)S(1)}, u32[]{:S(2)}, u32[]{:S(2)}) %collective-permute-start.36) | collective-permute-done | bytes 655392 | tf_op jit(solution)/shard_map/ppermute | solution.py:32
  358.6 10.0 %fusion.70 = bf16[1024,2560]{1,0:T(8,128)(2,1)} fusion(bf16[800,1024]{1,0:T(8,128)(2,1)S(1)} %get-tuple-element.174, bf16[800,2560]{1,0:T(8,128)(2,1)} %get-tuple-element.262), kind=kOutput, calls=%fused_computation.330 | convolution fusion | flops 4194304000 | bytes 10977280 | tf_op jit(solution)/shard_map/dot_general | solution.py:48
  368.5 3.2 collective-permute-done.38
  385.4 3.6 constant_dynamic-update-slice_fusion.43
  389.0 4.5 fusion.71
  393.5 4.2 fusion.45
  407.1 25.8 %attend_back.1 = (bf16[1024,640]{1,0:T(8,128)(2,1)}, bf16[1024,640]{1,0:T(8,128)(2,1)}, bf16[1024,128]{1,0:T(8,128)(2,1)S(1)}) custom-call(bf16[1024,640]{1,0:T(8,128)(2,1)} %get-tuple-element.137.refs_0_, bf16[1024,640]{1,0:T(8,128)(2,1)} %get-tuple-element.138.refs_1_, bf16[1024,320]{1,0:T(8,128)(2,1)S(1)} %copy-done.7, f32[1024,8]{1,0:T(8,128)S(1)} %copy-done.9, ...), custom_call_target="tpu_custom_call" | custom-call | flops 6710886400 | bytes 8388608 | tf_op jit(solution)/shard_map/attend_back/pallas_call | solution.py:253
  447.2 3.0 maximum_select_fusion.7
  450.2 3.8 collective-permute-start.48
  454.0 6.2 collective-permute-done.55
  461.3 10.6 %collective-permute-done.53 = bf16[384,480]{0,1:T(8,128)(2,1)S(1)} collective-permute-done((bf16[384,480]{0,1:T(8,128)(2,1)S(1)}, bf16[384,480]{0,1:T(8,128)(2,1)S(1)}, u32[]{:S(2)}, u32[]{:S(2)}) %collective-permute-start.53) | collective-permute-done | bytes 368672 | tf_op jit(solution)/shard_map/ppermute | solution.py:32
  475.9 2.7 collective-permute-done.43
  481.6 22.6 %fusion.74 = bf16[800,4096]{1,0:T(8,128)(2,1)} fusion(bf16[800,2560]{1,0:T(8,128)(2,1)} %get-tuple-element.262, bf16[4096,2560]{1,0:T(8,128)(2,1)} %all-gather.6.cloned.1.call-done), kind=kOutput, calls=%fused_computation.334 | convolution fusion | flops 16777216000 | bytes 31621120 | tf_op jit(solution)/shard_map/dot_general | solution.py:48
  504.4 3.7 slice.453
  514.0 3.2 add_convert_fusion
  517.3 22.7 %fusion.11 = bf16[800,4096]{1,0:T(8,128)(2,1)} fusion(bf16[4096,2560]{1,0:T(8,128)(2,1)} %all-gather.8.cloned.1.call-done, bf16[1600,2560]{1,0:T(8,128)(2,1)} %get-tuple-element.263), kind=kOutput, calls=%fused_computation.22 | convolution fusion | flops 16777216000 | bytes 31621120 | tf_op jit(solution)/shard_map/dot_general | solution.py:48
  543.6 4.3 collective-permute-start.54
  547.9 3.5 add_convert_fusion.4
  557.7 22.9 %fusion.9 = bf16[800,4096]{1,0:T(8,128)(2,1)} fusion(bf16[4096,2560]{1,0:T(8,128)(2,1)} %all-gather.8.cloned.1.call-done, bf16[1600,2560]{1,0:T(8,128)(2,1)} %get-tuple-element.263), kind=kOutput, calls=%fused_computation.20 | convolution fusion | flops 16777216000 | bytes 31621120 | tf_op jit(solution)/shard_map/dot_general | solution.py:48
  586.8 4.8 collective-permute-done.62
  591.5 2.9 fusion.15
  594.6 4.2 collective-permute-done.57
  606.7 4.6 collective-permute-start.59
  615.1 10.7 %fusion.4 = (bf16[800,4096]{1,0:T(8,128)(2,1)}, bf16[800,4096]{1,0:T(8,128)(2,1)}, bf16[800,4096]{1,0:T(8,128)(2,1)S(1)}) fusion(bf16[800,4096]{1,0:T(8,128)(2,1)S(1)} %bitcast.79, bf16[800,4096]{1,0:T(8,128)(2,1)S(1)} %bitcast.81, bf16[800,4096]{1,0:T(8,128)(2,1)S(1)} %copy-done.15), kind=kLoop, calls=%fused_computation.10 | loop fusion | flops 58982400 | bytes 39321600 | tf_op jit(solution)/shard_map/convert_element_type | solution.py:282
  629.5 8.4 %collective-permute-start.71 = (bf16[268,1280]{1,0:T(8,128)(2,1)S(1)}, bf16[268,1280]{1,0:T(8,128)(2,1)S(1)}, u32[]{:S(2)}, u32[]{:S(2)}) collective-permute-start(bf16[268,1280]{1,0:T(8,128)(2,1)S(1)} %pad_maximum_fusion.5), channel_id=1, source_target_pairs={{0,8},{24,16},{1,9},{25,17},{2,10},{26,18},{3,11},{27,19},{4,12},{... | collective-permute-start | bytes 2058248 | tf_op jit(solution)/shard_map/ppermute | solution.py:311
  639.9 24.8 %fusion.75 = bf16[800,2560]{1,0:T(8,128)(2,1)} fusion(bf16[800,4096]{1,0:T(8,128)(2,1)} %get-tuple-element.218, bf16[4096,2560]{1,0:T(8,128)(2,1)} %all-gather.8.cloned.1.call-done), kind=kOutput, calls=%fused_computation.335 | convolution fusion | flops 16777216000 | bytes 31621120 | tf_op jit(solution)/shard_map/dot_general | solution.py:48
  671.5 24.5 %fusion.76 = bf16[800,2560]{1,0:T(8,128)(2,1)} fusion(bf16[800,4096]{1,0:T(8,128)(2,1)} %get-tuple-element.223, bf16[4096,2560]{1,0:T(8,128)(2,1)} %all-gather.8.cloned.1.call-done), kind=kOutput, calls=%fused_computation.336 | convolution fusion | flops 16777216000 | bytes 31621120 | tf_op jit(solution)/shard_map/dot_general | solution.py:48
  699.0 3.4 select_convert_fusion
  705.0 22.9 %fusion.77 = bf16[800,2560]{1,0:T(8,128)(2,1)} fusion(bf16[800,4096]{1,0:T(8,128)(2,1)S(1)} %get-tuple-element.237, bf16[4096,2560]{1,0:T(8,128)(2,1)} %all-gather.6.cloned.1.call-done), kind=kOutput, calls=%fused_computation.337 | convolution fusion | flops 16777216000 | bytes 31621120 | tf_op jit(solution)/shard_map/dot_general | solution.py:48
  727.8 2.7 dynamic_slice.223
  731.0 3.1 collective-permute-start.78
  734.1 3.0 constant_dynamic-slice_fusion
  741.4 11.6 %collective-permute-done.79 = bf16[400,1280]{1,0:T(8,128)(2,1)} collective-permute-done((bf16[400,1280]{1,0:T(8,128)(2,1)}, bf16[400,1280]{1,0:T(8,128)(2,1)}, u32[]{:S(2)}, u32[]{:S(2)}) %collective-permute-start.79) | collective-permute-done | bytes 1024032 | tf_op jit(solution)/shard_map/ppermute | solution.py:32
  759.1 2.9 maximum_select_fusion.4
  762.1 3.9 convert_bitcast_fusion
  766.0 10.7 %collective-permute-done.81 = bf16[400,1280]{1,0:T(8,128)(2,1)S(1)} collective-permute-done((bf16[400,1280]{1,0:T(8,128)(2,1)S(1)}, bf16[400,1280]{1,0:T(8,128)(2,1)S(1)}, u32[]{:S(2)}, u32[]{:S(2)}) %collective-permute-start.81) | collective-permute-done | bytes 1024032 | tf_op jit(solution)/shard_map/ppermute | solution.py:32
  778.1 2.7 collective-permute-done.80
  783.0 3.7 convert_bitcast_fusion.1
  786.8 12.9 %collective-permute-done.82 = bf16[400,1280]{1,0:T(8,128)(2,1)S(1)} collective-permute-done((bf16[400,1280]{1,0:T(8,128)(2,1)S(1)}, bf16[400,1280]{1,0:T(8,128)(2,1)S(1)}, u32[]{:S(2)}, u32[]{:S(2)}) %collective-permute-start.82) | collective-permute-done | bytes 1024032 | tf_op jit(solution)/shard_map/ppermute | solution.py:584
  800.6 3.7 fusion.13
  (586 shorter events, 249.5 us)
Async XLA Ops:
  7.2 217.8 %all-gather.4.cloned.1.call-start = ((), (), s32[]{:S(2)}) async-start(), calls=%async_computation | async-start | bytes 7680000 | tf_op jit(solution)/shard_map/all_gather | solution.py:378
  11.0 36.9 %collective-permute-start.2 = (bf16[600,1280]{1,0:T(8,128)(2,1)}, bf16[600,1280]{1,0:T(8,128)(2,1)}, u32[]{:S(2)}, u32[]{:S(2)}) collective-permute-start(bf16[600,1280]{1,0:T(8,128)(2,1)} %pad_maximum_fusion.2), channel_id=1, source_target_pairs={{0,4},{4,0},{1,5},{5,1},{2,6},{6,2},{3,7},{7,3},{8,12},{12,8},{9,1... | collective-permute-start | bytes 4608008 | tf_op jit(solution)/shard_map/ppermute | solution.py:32
  14.8 16.9 %collective-permute-start.1 = (bf16[264,1280]{1,0:T(8,128)(2,1)}, bf16[264,1280]{1,0:T(8,128)(2,1)}, u32[]{:S(2)}, u32[]{:S(2)}) collective-permute-start(bf16[264,1280]{1,0:T(8,128)(2,1)} %pad_maximum_fusion.6), channel_id=1, source_target_pairs={{0,2},{1,3},{2,0},{3,1},{4,6},{5,7},{6,4},{7,5},{8,10},{9,11},{10,... | collective-permute-start | bytes 2027528 | tf_op jit(solution)/shard_map/ppermute | solution.py:40
  16.6 32.6 %collective-permute-start = (f32[1,256]{1,0:T(1,128)S(1)}, f32[1,256]{1,0:T(1,128)S(1)}, u32[]{:S(2)}, u32[]{:S(2)}) collective-permute-start(f32[1,256]{1,0:T(1,128)S(1)} %bitcast.91), channel_id=1, source_target_pairs={{0,4},{4,0},{1,5},{5,1},{2,6},{6,2},{3,7},{7,3},{8,12},{12,8},{9,1... | collective-permute-start | bytes 3080 | tf_op jit(solution)/shard_map/ppermute | solution.py:32
  47.9 431.7 %all-gather.6.cloned.1.call-start = ((), (), s32[]{:S(2)}) async-start(), calls=%async_computation.1 | async-start | bytes 21626880 | tf_op jit(solution)/shard_map/all_gather | solution.py:429
  54.9 15.4 %collective-permute-start.4 = (f32[128,1056]{0,1:T(8,128)}, f32[128,1056]{0,1:T(8,128)}, u32[]{:S(2)}, u32[]{:S(2)}) collective-permute-start(f32[128,1056]{0,1:T(8,128)} %get-tuple-element.129), channel_id=1, source_target_pairs={{0,4},{4,0},{1,5},{5,1},{2,6},{6,2},{3,7},{7,3},{8,12},{12,8},{9,1... | collective-permute-start | bytes 1622024 | tf_op jit(solution)/shard_map/ppermute | solution.py:32
  63.3 18.8 %collective-permute-start.7 = (bf16[384,480]{0,1:T(8,128)(2,1)}, bf16[384,480]{0,1:T(8,128)(2,1)}, u32[]{:S(2)}, u32[]{:S(2)}) collective-permute-start(bf16[384,480]{0,1:T(8,128)(2,1)} %get-tuple-element.130), channel_id=1, source_target_pairs={{0,4},{4,0},{1,5},{5,1},{2,6},{6,2},{3,7},{7,3},{8,12},{12,8},{9,1... | collective-permute-start | bytes 1105928 | tf_op jit(solution)/shard_map/ppermute | solution.py:32
  109.6 34.9 %collective-permute-start.11 = (bf16[320,1280]{1,0:T(8,128)(2,1)}, bf16[320,1280]{1,0:T(8,128)(2,1)}, u32[]{:S(2)}, u32[]{:S(2)}) collective-permute-start(bf16[320,1280]{1,0:T(8,128)(2,1)} %get-tuple-element.142), channel_id=1, source_target_pairs={{0,4},{4,0},{1,5},{5,1},{2,6},{6,2},{3,7},{7,3},{8,12},{12,8},{9,1... | collective-permute-start | bytes 2457608 | tf_op jit(solution)/shard_map/ppermute | solution.py:32
  111.5 25.8 %collective-permute-start.14 = (bf16[256,1280]{1,0:T(8,128)(2,1)}, bf16[256,1280]{1,0:T(8,128)(2,1)}, u32[]{:S(2)}, u32[]{:S(2)}) collective-permute-start(bf16[256,1280]{1,0:T(8,128)(2,1)} %copy-done.35), channel_id=1, source_target_pairs={{0,2},{1,3},{2,0},{3,1},{4,6},{5,7},{6,4},{7,5},{8,10},{9,11},{10,... | collective-permute-start | bytes 1966088 | tf_op jit(solution)/shard_map/ppermute | solution.py:40
  114.0 23.9 %collective-permute-start.12 = (bf16[128,1280]{1,0:T(8,128)(2,1)}, bf16[128,1280]{1,0:T(8,128)(2,1)S(1)}, u32[]{:S(2)}, u32[]{:S(2)}) collective-permute-start(bf16[128,1280]{1,0:T(8,128)(2,1)} %get-tuple-element.143), channel_id=1, source_target_pairs={{0,4},{4,0},{1,5},{5,1},{2,6},{6,2},{3,7},{7,3},{8,12},{12,8},{9,1... | collective-permute-start | bytes 983048 | tf_op jit(solution)/shard_map/ppermute | solution.py:32
  114.5 30.1 %collective-permute-start.13 = (bf16[128,1280]{1,0:T(8,128)(2,1)}, bf16[128,1280]{1,0:T(8,128)(2,1)S(1)}, u32[]{:S(2)}, u32[]{:S(2)}) collective-permute-start(bf16[128,1280]{1,0:T(8,128)(2,1)} %get-tuple-element.144), channel_id=1, source_target_pairs={{0,4},{4,0},{1,5},{5,1},{2,6},{6,2},{3,7},{7,3},{8,12},{12,8},{9,1... | collective-permute-start | bytes 983048 | tf_op jit(solution)/shard_map/ppermute | solution.py:32
  146.3 370.9 %all-gather.8.cloned.1.call-start = ((), (), s32[]{:S(2)}) async-start(), calls=%async_computation.2 | async-start | bytes 21626880 | tf_op jit(solution)/shard_map/all_gather | solution.py:448
  157.6 9.8 %collective-permute-start.16 = (bf16[64,2560]{1,0:T(8,128)(2,1)S(1)}, bf16[64,2560]{1,0:T(8,128)(2,1)S(1)}, u32[]{:S(2)}, u32[]{:S(2)}) collective-permute-start(bf16[64,2560]{1,0:T(8,128)(2,1)S(1)} %get-tuple-element.284), channel_id=1, source_target_pairs={{0,2},{1,3},{2,0},{3,1},{4,6},{5,7},{6,4},{7,5},{8,10},{9,11},{10,... | collective-permute-start | bytes 983048 | tf_op jit(solution)/shard_map/ppermute | solution.py:40
  168.6 20.9 %collective-permute-start.17 = (bf16[128,2560]{1,0:T(8,128)(2,1)}, bf16[128,2560]{1,0:T(8,128)(2,1)}, u32[]{:S(2)}, u32[]{:S(2)}) collective-permute-start(bf16[128,2560]{1,0:T(8,128)(2,1)} %pad_maximum_fusion.7), channel_id=1, source_target_pairs={{0,4},{4,0},{1,5},{5,1},{2,6},{6,2},{3,7},{7,3},{8,12},{12,8},{9,1... | collective-permute-start | bytes 1966088 | tf_op jit(solution)/shard_map/ppermute | solution.py:32
  171.1 20.3 %collective-permute-start.19 = (bf16[128,2560]{1,0:T(8,128)(2,1)}, bf16[128,2560]{1,0:T(8,128)(2,1)S(1)}, u32[]{:S(2)}, u32[]{:S(2)}) collective-permute-start(bf16[128,2560]{1,0:T(8,128)(2,1)} %pad_maximum_fusion.8), channel_id=1, source_target_pairs={{0,2},{1,3},{2,0},{3,1},{4,6},{5,7},{6,4},{7,5},{8,10},{9,11},{10,... | collective-permute-start | bytes 1966088 | tf_op jit(solution)/shard_map/ppermute | solution.py:40
  172.6 16.9 %collective-permute-start.20 = (bf16[1280]{0:T(1024)(128)(2,1)S(1)}, bf16[1280]{0:T(1024)(128)(2,1)S(1)}, u32[]{:S(2)}, u32[]{:S(2)}) collective-permute-start(bf16[1280]{0:T(1024)(128)(2,1)S(1)} %copy-done.83), channel_id=1, source_target_pairs={{0,4},{4,0},{1,5},{5,1},{2,6},{6,2},{3,7},{7,3},{8,12},{12,8},{9,1... | collective-permute-start | bytes 7688 | tf_op jit(solution)/shard_map/ppermute | solution.py:32
  195.6 29.3 %collective-permute-start.21 = (bf16[128,2560]{1,0:T(8,128)(2,1)}, bf16[128,2560]{1,0:T(8,128)(2,1)}, u32[]{:S(2)}, u32[]{:S(2)}) collective-permute-start(bf16[128,2560]{1,0:T(8,128)(2,1)} %multiply_convert_fusion.4), channel_id=1, source_target_pairs={{0,4},{4,0},{1,5},{5,1},{2,6},{6,2},{3,7},{7,3},{8,12},{12,8},{9,1... | collective-permute-start | bytes 1966088 | tf_op jit(solution)/shard_map/ppermute | solution.py:32
  196.2 28.8 %collective-permute-start.22 = (bf16[128,2560]{1,0:T(8,128)(2,1)}, bf16[128,2560]{1,0:T(8,128)(2,1)}, u32[]{:S(2)}, u32[]{:S(2)}) collective-permute-start(bf16[128,2560]{1,0:T(8,128)(2,1)} %multiply_convert_fusion.4), channel_id=1, source_target_pairs={{0,2},{1,3},{2,0},{3,1},{4,6},{5,7},{6,4},{7,5},{8,10},{9,11},{10,... | collective-permute-start | bytes 1966088 | tf_op jit(solution)/shard_map/ppermute | solution.py:40
  225.0 31.9 %collective-permute-start.26 = (bf16[128,2560]{1,0:T(8,128)(2,1)S(1)}, bf16[128,2560]{1,0:T(8,128)(2,1)S(1)}, u32[]{:S(2)}, u32[]{:S(2)}) collective-permute-start(bf16[128,2560]{1,0:T(8,128)(2,1)S(1)} %copy-done.19), channel_id=1, source_target_pairs={{0,4},{4,0},{1,5},{5,1},{2,6},{6,2},{3,7},{7,3},{8,12},{12,8},{9,1... | collective-permute-start | bytes 1966088 | tf_op jit(solution)/shard_map/ppermute | solution.py:32
  225.6 31.3 %collective-permute-start.27 = (bf16[128,2560]{1,0:T(8,128)(2,1)S(1)}, bf16[128,2560]{1,0:T(8,128)(2,1)S(1)}, u32[]{:S(2)}, u32[]{:S(2)}) collective-permute-start(bf16[128,2560]{1,0:T(8,128)(2,1)S(1)} %copy-done.19), channel_id=1, source_target_pairs={{0,2},{1,3},{2,0},{3,1},{4,6},{5,7},{6,4},{7,5},{8,10},{9,11},{10,... | collective-permute-start | bytes 1966088 | tf_op jit(solution)/shard_map/ppermute | solution.py:40
  229.4 14.1 %collective-permute-start.23 = (bf16[64,2560]{1,0:T(8,128)(2,1)S(1)}, bf16[64,2560]{1,0:T(8,128)(2,1)S(1)}, u32[]{:S(2)}, u32[]{:S(2)}) collective-permute-start(bf16[64,2560]{1,0:T(8,128)(2,1)S(1)} %slice.409), channel_id=1, source_target_pairs={{0,2},{1,3},{2,0},{3,1},{4,6},{5,7},{6,4},{7,5},{8,10},{9,11},{10,... | collective-permute-start | bytes 983048 | tf_op jit(solution)/shard_map/ppermute | solution.py:40
  231.1 19.2 %collective-permute-start.24 = (bf16[64,2560]{1,0:T(8,128)(2,1)S(1)}, bf16[64,2560]{1,0:T(8,128)(2,1)S(1)}, u32[]{:S(2)}, u32[]{:S(2)}) collective-permute-start(bf16[64,2560]{1,0:T(8,128)(2,1)S(1)} %slice.410), channel_id=1, source_target_pairs={{0,4},{4,0},{1,5},{5,1},{2,6},{6,2},{3,7},{7,3},{8,12},{12,8},{9,1... | collective-permute-start | bytes 983048 | tf_op jit(solution)/shard_map/ppermute | solution.py:32
  257.0 17.7 %collective-permute-start.28 = (bf16[64,2560]{1,0:T(8,128)(2,1)S(1)}, bf16[64,2560]{1,0:T(8,128)(2,1)S(1)}, u32[]{:S(2)}, u32[]{:S(2)}) collective-permute-start(bf16[64,2560]{1,0:T(8,128)(2,1)S(1)} %slice.411), channel_id=1, source_target_pairs={{0,2},{1,3},{2,0},{3,1},{4,6},{5,7},{6,4},{7,5},{8,10},{9,11},{10,... | collective-permute-start | bytes 983048 | tf_op jit(solution)/shard_map/ppermute | solution.py:40
  259.2 17.4 %collective-permute-start.29 = (bf16[64,2560]{1,0:T(8,128)(2,1)S(1)}, bf16[64,2560]{1,0:T(8,128)(2,1)S(1)}, u32[]{:S(2)}, u32[]{:S(2)}) collective-permute-start(bf16[64,2560]{1,0:T(8,128)(2,1)S(1)} %slice.412), channel_id=1, source_target_pairs={{0,4},{4,0},{1,5},{5,1},{2,6},{6,2},{3,7},{7,3},{8,12},{12,8},{9,1... | collective-permute-start | bytes 983048 | tf_op jit(solution)/shard_map/ppermute | solution.py:32
  319.2 16.0 %collective-permute-start.33 = (bf16[128,2560]{1,0:T(8,128)(2,1)S(1)}, bf16[128,2560]{1,0:T(8,128)(2,1)S(1)}, u32[]{:S(2)}, u32[]{:S(2)}) collective-permute-start(bf16[128,2560]{1,0:T(8,128)(2,1)S(1)} %pad_maximum_fusion.9), channel_id=1, source_target_pairs={{0,4},{4,0},{1,5},{5,1},{2,6},{6,2},{3,7},{7,3},{8,12},{12,8},{9,1... | collective-permute-start | bytes 1966088 | tf_op jit(solution)/shard_map/ppermute | solution.py:32
  319.6 15.8 %collective-permute-start.35 = (bf16[128,2560]{1,0:T(8,128)(2,1)S(1)}, bf16[128,2560]{1,0:T(8,128)(2,1)S(1)}, u32[]{:S(2)}, u32[]{:S(2)}) collective-permute-start(bf16[128,2560]{1,0:T(8,128)(2,1)S(1)} %pad_maximum_fusion.10), channel_id=1, source_target_pairs={{0,2},{1,3},{2,0},{3,1},{4,6},{5,7},{6,4},{7,5},{8,10},{9,11},{10,... | collective-permute-start | bytes 1966088 | tf_op jit(solution)/shard_map/ppermute | solution.py:40
  337.8 18.3 %collective-permute-start.36 = (bf16[128,2560]{1,0:T(8,128)(2,1)S(1)}, bf16[128,2560]{1,0:T(8,128)(2,1)S(1)}, u32[]{:S(2)}, u32[]{:S(2)}) collective-permute-start(bf16[128,2560]{1,0:T(8,128)(2,1)S(1)} %get-tuple-element.175), channel_id=1, source_target_pairs={{0,4},{4,0},{1,5},{5,1},{2,6},{6,2},{3,7},{7,3},{8,12},{12,8},{9,1... | collective-permute-start | bytes 1966088 | tf_op jit(solution)/shard_map/ppermute | solution.py:32
  339.5 16.9 %collective-permute-start.37 = (bf16[128,2560]{1,0:T(8,128)(2,1)S(1)}, bf16[128,2560]{1,0:T(8,128)(2,1)S(1)}, u32[]{:S(2)}, u32[]{:S(2)}) collective-permute-start(bf16[128,2560]{1,0:T(8,128)(2,1)S(1)} %get-tuple-element.175), channel_id=1, source_target_pairs={{0,2},{1,3},{2,0},{3,1},{4,6},{5,7},{6,4},{7,5},{8,10},{9,11},{10,... | collective-permute-start | bytes 1966088 | tf_op jit(solution)/shard_map/ppermute | solution.py:40
  356.4 15.4 %collective-permute-start.38 = (bf16[64,2560]{1,0:T(8,128)(2,1)S(1)}, bf16[64,2560]{1,0:T(8,128)(2,1)S(1)}, u32[]{:S(2)}, u32[]{:S(2)}) collective-permute-start(bf16[64,2560]{1,0:T(8,128)(2,1)S(1)} %slice.428), channel_id=1, source_target_pairs={{0,2},{1,3},{2,0},{3,1},{4,6},{5,7},{6,4},{7,5},{8,10},{9,11},{10,... | collective-permute-start | bytes 983048 | tf_op jit(solution)/shard_map/ppermute | solution.py:40
  357.7 15.6 %collective-permute-start.39 = (bf16[64,2560]{1,0:T(8,128)(2,1)S(1)}, bf16[64,2560]{1,0:T(8,128)(2,1)S(1)}, u32[]{:S(2)}, u32[]{:S(2)}) collective-permute-start(bf16[64,2560]{1,0:T(8,128)(2,1)S(1)} %slice.429), channel_id=1, source_target_pairs={{0,4},{4,0},{1,5},{5,1},{2,6},{6,2},{3,7},{7,3},{8,12},{12,8},{9,1... | collective-permute-start | bytes 983048 | tf_op jit(solution)/shard_map/ppermute | solution.py:32
  380.1 203.2 %collective-permute-start.63 = (bf16[512,1280]{1,0:T(8,128)(2,1)}, bf16[512,1280]{1,0:T(8,128)(2,1)}, u32[]{:S(2)}, u32[]{:S(2)}) collective-permute-start(bf16[512,1280]{1,0:T(8,128)(2,1)} %pad_maximum_fusion.4), channel_id=1, source_target_pairs={{0,1},{1,0},{2,3},{3,2},{4,5},{5,4},{6,7},{7,6},{8,9},{9,8},{10,11... | collective-permute-start | bytes 3932168 | tf_op jit(solution)/shard_map/ppermute | solution.py:36
  381.8 19.3 %collective-permute-start.51 = (bf16[128,1280]{1,0:T(8,128)(2,1)S(1)}, bf16[128,1280]{1,0:T(8,128)(2,1)S(1)}, u32[]{:S(2)}, u32[]{:S(2)}) collective-permute-start(bf16[128,1280]{1,0:T(8,128)(2,1)S(1)} %dynamic-slice_convert_fusion), channel_id=1, source_target_pairs={{0,4},{4,0},{1,5},{5,1},{2,6},{6,2},{3,7},{7,3},{8,12},{12,8},{9,1... | collective-permute-start | bytes 983048 | tf_op jit(solution)/shard_map/ppermute | solution.py:32
  399.0 36.2 %collective-permute-start.41 = (bf16[320,1280]{1,0:T(8,128)(2,1)}, bf16[320,1280]{1,0:T(8,128)(2,1)}, u32[]{:S(2)}, u32[]{:S(2)}) collective-permute-start(bf16[320,1280]{1,0:T(8,128)(2,1)} %get-tuple-element.290), channel_id=1, source_target_pairs={{0,4},{4,0},{1,5},{5,1},{2,6},{6,2},{3,7},{7,3},{8,12},{12,8},{9,1... | collective-permute-start | bytes 2457608 | tf_op jit(solution)/shard_map/ppermute | solution.py:32
  440.2 32.8 %collective-permute-start.42 = (bf16[512,1152]{1,0:T(8,128)(2,1)S(1)}, bf16[512,1152]{1,0:T(8,128)(2,1)S(1)}, u32[]{:S(2)}, u32[]{:S(2)}) collective-permute-start(bf16[512,1152]{1,0:T(8,128)(2,1)S(1)} %slice.510), channel_id=1, source_target_pairs={{0,1},{1,0},{2,3},{3,2},{4,5},{5,4},{6,7},{7,6},{8,9},{9,8},{10,11... | collective-permute-start | bytes 3538952 | tf_op jit(solution)/shard_map/ppermute | solution.py:36
  442.5 17.7 %collective-permute-start.55 = (bf16[256,640]{1,0:T(8,128)(2,1)S(1)}, bf16[256,640]{1,0:T(8,128)(2,1)S(1)}, u32[]{:S(2)}, u32[]{:S(2)}) collective-permute-start(bf16[256,640]{1,0:T(8,128)(2,1)S(1)} %fusion.40), channel_id=1, source_target_pairs={{0,4},{4,0},{1,5},{5,1},{2,6},{6,2},{3,7},{7,3},{8,12},{12,8},{9,1... | collective-permute-start | bytes 983048 | tf_op jit(solution)/shard_map/ppermute | solution.py:32
  446.2 25.7 %collective-permute-start.53 = (bf16[384,480]{0,1:T(8,128)(2,1)S(1)}, bf16[384,480]{0,1:T(8,128)(2,1)S(1)}, u32[]{:S(2)}, u32[]{:S(2)}) collective-permute-start(bf16[384,480]{0,1:T(8,128)(2,1)S(1)} %get-tuple-element.305), channel_id=1, source_target_pairs={{0,4},{4,0},{1,5},{5,1},{2,6},{6,2},{3,7},{7,3},{8,12},{12,8},{9,1... | collective-permute-start | bytes 1105928 | tf_op jit(solution)/shard_map/ppermute | solution.py:32
  450.2 89.8 %collective-permute-start.48 = (bf16[640,1280]{1,0:T(8,128)(2,1)}, bf16[640,1280]{1,0:T(8,128)(2,1)}, u32[]{:S(2)}, u32[]{:S(2)}) collective-permute-start(bf16[640,1280]{1,0:T(8,128)(2,1)} %maximum_select_fusion.7), channel_id=1, source_target_pairs={{0,8},{24,16},{1,9},{25,17},{2,10},{26,18},{3,11},{27,19},{4,12},{... | collective-permute-start | bytes 4915208 | tf_op jit(solution)/shard_map/ppermute | solution.py:311
  479.7 24.4 %collective-permute-start.45 = (bf16[128,1152]{1,0:T(8,128)(2,1)S(1)}, bf16[128,1152]{1,0:T(8,128)(2,1)S(1)}, u32[]{:S(2)}, u32[]{:S(2)}) collective-permute-start(bf16[128,1152]{1,0:T(8,128)(2,1)S(1)} %pad_maximum_fusion.14), channel_id=1, source_target_pairs={{0,4},{4,0},{1,5},{5,1},{2,6},{6,2},{3,7},{7,3},{8,12},{12,8},{9,1... | collective-permute-start | bytes 884744 | tf_op jit(solution)/shard_map/ppermute | solution.py:32
  480.8 23.4 %collective-permute-start.46 = (bf16[128,1152]{1,0:T(8,128)(2,1)S(1)}, bf16[128,1152]{1,0:T(8,128)(2,1)S(1)}, u32[]{:S(2)}, u32[]{:S(2)}) collective-permute-start(bf16[128,1152]{1,0:T(8,128)(2,1)S(1)} %pad_maximum_fusion.15), channel_id=1, source_target_pairs={{0,2},{1,3},{2,0},{3,1},{4,6},{5,7},{6,4},{7,5},{8,10},{9,11},{10,... | collective-permute-start | bytes 884744 | tf_op jit(solution)/shard_map/ppermute | solution.py:40
  513.7 26.4 %collective-permute-start.47 = (bf16[128,1056]{1,0:T(8,128)(2,1)}, bf16[128,1056]{1,0:T(8,128)(2,1)}, u32[]{:S(2)}, u32[]{:S(2)}) collective-permute-start(bf16[128,1056]{1,0:T(8,128)(2,1)} %concatenate.313), channel_id=1, source_target_pairs={{0,4},{4,0},{1,5},{5,1},{2,6},{6,2},{3,7},{7,3},{8,12},{12,8},{9,1... | collective-permute-start | bytes 811016 | tf_op jit(solution)/shard_map/ppermute | solution.py:32
  543.6 55.2 %collective-permute-start.54 = (bf16[384,960]{0,1:T(8,128)(2,1)}, bf16[384,960]{0,1:T(8,128)(2,1)}, u32[]{:S(2)}, u32[]{:S(2)}) collective-permute-start(bf16[384,960]{0,1:T(8,128)(2,1)} %maximum_select_fusion.10), channel_id=1, source_target_pairs={{0,8},{24,16},{1,9},{25,17},{2,10},{26,18},{3,11},{27,19},{4,12},{... | collective-permute-start | bytes 2211848 | tf_op jit(solution)/shard_map/ppermute | solution.py:311
  551.4 47.4 %collective-permute-start.50 = (bf16[640,1280]{1,0:T(8,128)(2,1)}, bf16[640,1280]{1,0:T(8,128)(2,1)}, u32[]{:S(2)}, u32[]{:S(2)}) collective-permute-start(bf16[640,1280]{1,0:T(8,128)(2,1)} %add_convert_fusion.4), channel_id=1, source_target_pairs={{8,16},{16,8},{9,17},{17,9},{10,18},{18,10},{11,19},{19,11},{12,20... | collective-permute-start | bytes 4915208 | tf_op jit(solution)/shard_map/ppermute | solution.py:315
  555.6 28.9 %collective-permute-start.60 = (bf16[256,264]{1,0:T(8,128)(2,1)}, bf16[256,264]{1,0:T(8,128)(2,1)}, u32[]{:S(2)}, u32[]{:S(2)}) collective-permute-start(bf16[256,264]{1,0:T(8,128)(2,1)} %get-tuple-element.335), channel_id=1, source_target_pairs={{0,2},{1,3},{2,0},{3,1},{4,6},{5,7},{6,4},{7,5},{8,10},{9,11},{10,... | collective-permute-start | bytes 405512 | tf_op jit(solution)/shard_map/ppermute | solution.py:40
  557.3 23.2 %collective-permute-start.65 = (f32[38,128]{1,0:T(8,128)S(1)}, f32[38,128]{1,0:T(8,128)S(1)}, u32[]{:S(2)}, u32[]{:S(2)}) collective-permute-start(f32[38,128]{1,0:T(8,128)S(1)} %fusion.110), channel_id=1, source_target_pairs={{0,2},{1,3},{2,0},{3,1},{4,6},{5,7},{6,4},{7,5},{8,10},{9,11},{10,... | collective-permute-start | bytes 58376 | tf_op jit(solution)/shard_map/ppermute | solution.py:40
  584.5 10.1 %collective-permute-start.56 = (bf16[64,2560]{1,0:T(8,128)(2,1)}, bf16[64,2560]{1,0:T(8,128)(2,1)S(1)}, u32[]{:S(2)}, u32[]{:S(2)}) collective-permute-start(bf16[64,2560]{1,0:T(8,128)(2,1)} %get-tuple-element.271), channel_id=1, source_target_pairs={{0,4},{4,0},{1,5},{5,1},{2,6},{6,2},{3,7},{7,3},{8,12},{12,8},{9,1... | collective-permute-start | bytes 983048 | tf_op jit(solution)/shard_map/ppermute | solution.py:32
  586.3 12.5 %collective-permute-start.57 = (bf16[64,2560]{1,0:T(8,128)(2,1)}, bf16[64,2560]{1,0:T(8,128)(2,1)S(1)}, u32[]{:S(2)}, u32[]{:S(2)}) collective-permute-start(bf16[64,2560]{1,0:T(8,128)(2,1)} %get-tuple-element.270), channel_id=1, source_target_pairs={{0,2},{1,3},{2,0},{3,1},{4,6},{5,7},{6,4},{7,5},{8,10},{9,11},{10,... | collective-permute-start | bytes 983048 | tf_op jit(solution)/shard_map/ppermute | solution.py:40
  601.9 23.9 %collective-permute-start.67 = (bf16[128,2560]{1,0:T(8,128)(2,1)}, bf16[128,2560]{1,0:T(8,128)(2,1)}, u32[]{:S(2)}, u32[]{:S(2)}) collective-permute-start(bf16[128,2560]{1,0:T(8,128)(2,1)} %pad_maximum_fusion.11), channel_id=1, source_target_pairs={{0,4},{4,0},{1,5},{5,1},{2,6},{6,2},{3,7},{7,3},{8,12},{12,8},{9,1... | collective-permute-start | bytes 1966088 | tf_op jit(solution)/shard_map/ppermute | solution.py:32
  602.1 23.7 %collective-permute-start.68 = (bf16[128,2560]{1,0:T(8,128)(2,1)S(1)}, bf16[128,2560]{1,0:T(8,128)(2,1)}, u32[]{:S(2)}, u32[]{:S(2)}) collective-permute-start(bf16[128,2560]{1,0:T(8,128)(2,1)S(1)} %pad_maximum_fusion.12), channel_id=1, source_target_pairs={{0,2},{1,3},{2,0},{3,1},{4,6},{5,7},{6,4},{7,5},{8,10},{9,11},{10,... | collective-permute-start | bytes 1966088 | tf_op jit(solution)/shard_map/ppermute | solution.py:40
  605.9 21.6 %collective-permute-start.58 = (bf16[384,960]{0,1:T(8,128)(2,1)S(1)}, bf16[384,960]{0,1:T(8,128)(2,1)S(1)}, u32[]{:S(2)}, u32[]{:S(2)}) collective-permute-start(bf16[384,960]{0,1:T(8,128)(2,1)S(1)} %add_convert_fusion.7), channel_id=1, source_target_pairs={{8,16},{16,8},{9,17},{17,9},{10,18},{18,10},{11,19},{19,11},{12,20... | collective-permute-start | bytes 2211848 | tf_op jit(solution)/shard_map/ppermute | solution.py:315
  606.7 20.8 %collective-permute-start.59 = (bf16[256,1280]{1,0:T(8,128)(2,1)S(1)}, bf16[256,1280]{1,0:T(8,128)(2,1)}, u32[]{:S(2)}, u32[]{:S(2)}) collective-permute-start(bf16[256,1280]{1,0:T(8,128)(2,1)S(1)} %copy-done.37), channel_id=1, source_target_pairs={{0,8},{24,16},{1,9},{25,17},{2,10},{26,18},{3,11},{27,19},{4,12},{... | collective-permute-start | bytes 1966088 | tf_op jit(solution)/shard_map/ppermute | solution.py:311
  613.6 85.4 %collective-permute-start.77 = (bf16[640,1280]{1,0:T(8,128)(2,1)S(1)}, bf16[640,1280]{1,0:T(8,128)(2,1)}, u32[]{:S(2)}, u32[]{:S(2)}) collective-permute-start(bf16[640,1280]{1,0:T(8,128)(2,1)S(1)} %add_convert_fusion.3), channel_id=1, source_target_pairs={{8,0},{16,24},{9,1},{17,25},{10,2},{18,26},{11,3},{19,27},{12,4},{... | collective-permute-start | bytes 4915208 | tf_op jit(solution)/shard_map/ppermute | solution.py:319
  628.8 36.8 %collective-permute-start.70 = (bf16[256,1280]{1,0:T(8,128)(2,1)S(1)}, bf16[256,1280]{1,0:T(8,128)(2,1)S(1)}, u32[]{:S(2)}, u32[]{:S(2)}) collective-permute-start(bf16[256,1280]{1,0:T(8,128)(2,1)S(1)} %add_convert_fusion.11), channel_id=1, source_target_pairs={{8,16},{16,8},{9,17},{17,9},{10,18},{18,10},{11,19},{19,11},{12,20... | collective-permute-start | bytes 1966088 | tf_op jit(solution)/shard_map/ppermute | solution.py:315
  629.5 36.1 %collective-permute-start.71 = (bf16[268,1280]{1,0:T(8,128)(2,1)S(1)}, bf16[268,1280]{1,0:T(8,128)(2,1)S(1)}, u32[]{:S(2)}, u32[]{:S(2)}) collective-permute-start(bf16[268,1280]{1,0:T(8,128)(2,1)S(1)} %pad_maximum_fusion.5), channel_id=1, source_target_pairs={{0,8},{24,16},{1,9},{25,17},{2,10},{26,18},{3,11},{27,19},{4,12},{... | collective-permute-start | bytes 2058248 | tf_op jit(solution)/shard_map/ppermute | solution.py:311
  638.0 59.7 %collective-permute-start.75 = (bf16[384,960]{0,1:T(8,128)(2,1)S(1)}, bf16[384,960]{0,1:T(8,128)(2,1)S(1)}, u32[]{:S(2)}, u32[]{:S(2)}) collective-permute-start(bf16[384,960]{0,1:T(8,128)(2,1)S(1)} %add_convert_fusion.6), channel_id=1, source_target_pairs={{8,0},{16,24},{9,1},{17,25},{10,2},{18,26},{11,3},{19,27},{12,4},{... | collective-permute-start | bytes 2211848 | tf_op jit(solution)/shard_map/ppermute | solution.py:319
  639.4 25.2 %collective-permute-start.69 = (bf16[128,1280]{1,0:T(8,128)(2,1)S(1)}, bf16[128,1280]{1,0:T(8,128)(2,1)S(1)}, u32[]{:S(2)}, u32[]{:S(2)}) collective-permute-start(bf16[128,1280]{1,0:T(8,128)(2,1)S(1)} %get-tuple-element.309), channel_id=1, source_target_pairs={{0,4},{4,0},{1,5},{5,1},{2,6},{6,2},{3,7},{7,3},{8,12},{12,8},{9,1... | collective-permute-start | bytes 983048 | tf_op jit(solution)/shard_map/ppermute | solution.py:32
  665.8 37.7 %collective-permute-start.72 = (bf16[268,1280]{1,0:T(8,128)(2,1)S(1)}, bf16[268,1280]{1,0:T(8,128)(2,1)S(1)}, u32[]{:S(2)}, u32[]{:S(2)}) collective-permute-start(bf16[268,1280]{1,0:T(8,128)(2,1)S(1)} %add_convert_fusion.9), channel_id=1, source_target_pairs={{8,16},{16,8},{9,17},{17,9},{10,18},{18,10},{11,19},{19,11},{12,20... | collective-permute-start | bytes 2058248 | tf_op jit(solution)/shard_map/ppermute | solution.py:315
  668.3 35.2 %collective-permute-start.73 = (bf16[400,1280]{1,0:T(8,128)(2,1)S(1)}, bf16[400,1280]{1,0:T(8,128)(2,1)}, u32[]{:S(2)}, u32[]{:S(2)}) collective-permute-start(bf16[400,1280]{1,0:T(8,128)(2,1)S(1)} %dynamic_slice.220), channel_id=1, source_target_pairs={{0,4},{4,0},{1,5},{5,1},{2,6},{6,2},{3,7},{7,3},{8,12},{12,8},{9,1... | collective-permute-start | bytes 3072008 | tf_op jit(solution)/shard_map/ppermute | solution.py:32
  670.2 32.1 %collective-permute-start.76 = (bf16[256,1280]{1,0:T(8,128)(2,1)S(1)}, bf16[256,1280]{1,0:T(8,128)(2,1)S(1)}, u32[]{:S(2)}, u32[]{:S(2)}) collective-permute-start(bf16[256,1280]{1,0:T(8,128)(2,1)S(1)} %add_convert_fusion.10), channel_id=1, source_target_pairs={{8,0},{16,24},{9,1},{17,25},{10,2},{18,26},{11,3},{19,27},{12,4},{... | collective-permute-start | bytes 1966088 | tf_op jit(solution)/shard_map/ppermute | solution.py:319
  703.7 33.4 %collective-permute-start.74 = (bf16[268,1280]{1,0:T(8,128)(2,1)S(1)}, bf16[268,1280]{1,0:T(8,128)(2,1)S(1)}, u32[]{:S(2)}, u32[]{:S(2)}) collective-permute-start(bf16[268,1280]{1,0:T(8,128)(2,1)S(1)} %add_convert_fusion.8), channel_id=1, source_target_pairs={{8,0},{16,24},{9,1},{17,25},{10,2},{18,26},{11,3},{19,27},{12,4},{... | collective-permute-start | bytes 2058248 | tf_op jit(solution)/shard_map/ppermute | solution.py:319
  730.6 22.4 %collective-permute-start.79 = (bf16[400,1280]{1,0:T(8,128)(2,1)}, bf16[400,1280]{1,0:T(8,128)(2,1)}, u32[]{:S(2)}, u32[]{:S(2)}) collective-permute-start(bf16[400,1280]{1,0:T(8,128)(2,1)} %dynamic_slice.223), channel_id=1, source_target_pairs={{0,4},{4,0},{1,5},{5,1},{2,6},{6,2},{3,7},{7,3},{8,12},{12,8},{9,1... | collective-permute-start | bytes 3072008 | tf_op jit(solution)/shard_map/ppermute | solution.py:32
  731.0 23.1 %collective-permute-start.78 = (bf16[400,1280]{1,0:T(8,128)(2,1)}, bf16[400,1280]{1,0:T(8,128)(2,1)}, u32[]{:S(2)}, u32[]{:S(2)}) collective-permute-start(bf16[400,1280]{1,0:T(8,128)(2,1)} %collective-permute-done.73), channel_id=1, source_target_pairs={{0,8},{8,0},{16,24},{24,16},{1,9},{9,1},{17,25},{25,17},{2,10},{10... | collective-permute-start | bytes 3072008 | tf_op jit(solution)/shard_map/ppermute | solution.py:584
  755.8 20.9 %collective-permute-start.81 = (bf16[400,1280]{1,0:T(8,128)(2,1)S(1)}, bf16[400,1280]{1,0:T(8,128)(2,1)S(1)}, u32[]{:S(2)}, u32[]{:S(2)}) collective-permute-start(bf16[400,1280]{1,0:T(8,128)(2,1)S(1)} %dynamic_slice.226), channel_id=1, source_target_pairs={{0,4},{4,0},{1,5},{5,1},{2,6},{6,2},{3,7},{7,3},{8,12},{12,8},{9,1... | collective-permute-start | bytes 3072008 | tf_op jit(solution)/shard_map/ppermute | solution.py:32
  757.3 23.6 %collective-permute-start.80 = (bf16[400,1280]{1,0:T(8,128)(2,1)}, bf16[400,1280]{1,0:T(8,128)(2,1)S(1)}, u32[]{:S(2)}, u32[]{:S(2)}) collective-permute-start(bf16[400,1280]{1,0:T(8,128)(2,1)} %collective-permute-done.79), channel_id=1, source_target_pairs={{0,8},{8,0},{16,24},{24,16},{1,9},{9,1},{17,25},{25,17},{2,10},{10... | collective-permute-start | bytes 3072008 | tf_op jit(solution)/shard_map/ppermute | solution.py:584
  776.7 23.0 %collective-permute-start.82 = (bf16[400,1280]{1,0:T(8,128)(2,1)S(1)}, bf16[400,1280]{1,0:T(8,128)(2,1)S(1)}, u32[]{:S(2)}, u32[]{:S(2)}) collective-permute-start(bf16[400,1280]{1,0:T(8,128)(2,1)S(1)} %collective-permute-done.81), channel_id=1, source_target_pairs={{0,8},{8,0},{16,24},{24,16},{1,9},{9,1},{17,25},{25,17},{2,10},{10... | collective-permute-start | bytes 3072008 | tf_op jit(solution)/shard_map/ppermute | solution.py:584
  (121 other events, 1235.5 us)
Sparse Core Ops, SparseCore 0:
  48.0 114.4 all-gather.3
  165.3 159.0 all-gather.5
  327.9 179.7 all-gather.7
